TPU v7x, 32 devices: a whole 2x2x4 slice. The times are simulated.
32 devices in a mesh: row: 4 (over y, x), col: 8 (over z, core).
Axes of the slice: x: 2, y: 2, z: 4, core: 2. Of those that a mesh axis runs over, the one named last changes fastest.
Arguments:
- block_input: float32 [2, 8192, 640], P(None, ('row', 'col')), may hold values from -6 to 6
- output_grad: float32 [2, 8192, 640], P(None, ('row', 'col')), may hold values from -6 to 6
- sequence_ids: int32 [2, 8192], P(None, ('row', 'col')), may hold values from 0 to 7, as said below
- attn_weights: float32 [640, 2560], P(None, ('row', 'col')), may hold values from -0.29646353 to 0.29646353
- attn_momentum: float32 [640, 2560], P(None, ('row', 'col')), may hold values from -422.4 to 422.4
- attn_average: float32 [640, 2560], P(None, ('row', 'col')), may hold values from -0.29646353 to 0.29646353
- norm_params: float32 [2560], P(('row', 'col')), may hold values from -0.6 to 1.3
- norm_momentum: float32 [2560], P(('row', 'col')), may hold values from -806.4 to 806.4
- norm_average: float32 [2560], P(('row', 'col')), may hold values from -0.6 to 1.3
- ffn_weights: float32 [2, 640, 5120], P(None, 'row', 'col'), may hold values from -0.118585412 to 0.118585412
- ffn_momentum: float32 [2, 640, 5120], P(None, 'row', 'col'), may hold values from -249.6 to 249.6
- ffn_average: float32 [2, 640, 5120], P(None, 'row', 'col'), may hold values from -0.118585412 to 0.118585412
Outputs:
- block_output: float32 [2, 8192, 640], P(None, ('row', 'col'))
- input_grad: float32 [2, 8192, 640], P(None, ('row', 'col'))
- attn_grad: float32 [640, 2560], P(None, ('row', 'col'))
- attn_momentum_new: float32 [640, 2560], P(None, ('row', 'col'))
- attn_weights_new: float32 [640, 2560], P(None, ('row', 'col'))
- attn_average_new: float32 [640, 2560], P(None, ('row', 'col'))
- attn_copy: bfloat16 [640, 2560], P(None, ('row', 'col'))
- norm_grad: float32 [2560], P(('row', 'col'))
- norm_momentum_new: float32 [2560], P(('row', 'col'))
- norm_params_new: float32 [2560], P(('row', 'col'))
- norm_average_new: float32 [2560], P(('row', 'col'))
- norm_copy: bfloat16 [2560], P(('row', 'col'))
- ffn_grad: float32 [2, 640, 5120], P(None, 'row', 'col')
- ffn_momentum_new: float32 [2, 640, 5120], P(None, 'row', 'col')
- ffn_weights_new: float32 [2, 640, 5120], P(None, 'row', 'col')
- ffn_average_new: float32 [2, 640, 5120], P(None, 'row', 'col')
- ffn_copy: bfloat16 [2, 640, 5120], P(None, 'row', 'col')
Inputs may be any that keep to these rules, and one draw needn't show every extreme that they name: `sequence_ids`: within each aligned block of 256 tokens the numbers start at 0, never fall and step by one; a sequence (a run of equal numbers) holds 20 to 256 tokens; in each micro-batch one block holds a single sequence and another holds 8 sequences.
All inputs are finite; a program needn't handle non-finite values.
Results may differ from a plain program's by a relative error of at most 0.014.
The roundings to bfloat16 on the way count: a program that leaves them out, or rounds other values in their place, can miss the bound.
Values may be sent and summed in bfloat16 or wider, within the bound.
A program may use at most 128 MiB of HBM per device.

v0:
```python
import math

import jax
import jax.numpy as jnp
from jax import lax
from jax.sharding import PartitionSpec as P

D = 640
H = 20
HD = 32
MB = 2


EPSILON = 1e-05
MOMENT_DECAY = 0.9
AVERAGE_DECAY = 0.85
RATE_SCALE = 0.06
MASKED = -1e30


def layer_norm(values, gain, shift):
    center = values - jnp.mean(values, axis=-1, keepdims=True)
    spread = jnp.mean(center * center, axis=-1, keepdims=True)
    return center * lax.rsqrt(spread + EPSILON) * gain + shift


def gelu_exact(values):
    return jax.nn.gelu(values, approximate=False)


def matmul(left_side, right_side):
    return jnp.dot(left_side, right_side, preferred_element_type=jnp.float32)


def contract_rows(left_side, right_side):
    return lax.dot_general(
        left_side, right_side, (((0,), (0,)), ((), ())), preferred_element_type=jnp.float32
    )


def contract_cols(left_side, right_side):
    return lax.dot_general(
        left_side, right_side, (((1,), (1,)), ((), ())), preferred_element_type=jnp.float32
    )


def head_slices(qkv_low, first_col, head_group):
    length = qkv_low.shape[0]
    group_width = head_group * HD
    queries = lax.dynamic_slice_in_dim(qkv_low, first_col, group_width, 1).reshape(
        length, head_group, HD
    )
    keys_part = lax.dynamic_slice_in_dim(qkv_low, D + first_col, group_width, 1).reshape(
        length, head_group, HD
    )
    values = lax.dynamic_slice_in_dim(qkv_low, 2 * D + first_col, group_width, 1).reshape(
        length, head_group, HD
    )
    return (queries, keys_part, values)


def masked_scores(queries, keys_part, same_seq):
    scores = jnp.einsum(
        "qhe,khe->hqk", queries, keys_part, preferred_element_type=jnp.float32
    ) * HD ** (-0.5)
    return jnp.where(same_seq[None], scores, MASKED)


def attend_forward(qkv_low, same_seq):
    length = qkv_low.shape[0]
    head_group = math.gcd(H, 4)
    group_width = head_group * HD

    def one_group(group_index, state_all):
        mixed_all, maxima, totals = state_all
        first_col = group_index * group_width
        queries, keys_part, values = head_slices(qkv_low, first_col, head_group)
        scores = masked_scores(queries, keys_part, same_seq)
        row_max = jnp.max(scores, axis=-1, keepdims=True)
        exponent = jnp.exp(scores - row_max)
        row_total = jnp.sum(exponent, axis=-1, keepdims=True)
        attn_probs = (exponent / row_total).astype(jnp.bfloat16)
        mixed_rows = jnp.einsum(
            "hqk,khe->qhe", attn_probs, values, preferred_element_type=jnp.float32
        )
        mixed_all = lax.dynamic_update_slice_in_dim(
            mixed_all, mixed_rows.reshape(length, group_width), first_col, 1
        )
        maxima = lax.dynamic_update_slice_in_dim(
            maxima, row_max[:, :, 0], group_index * head_group, 0
        )
        totals = lax.dynamic_update_slice_in_dim(
            totals, row_total[:, :, 0], group_index * head_group, 0
        )
        return (mixed_all, maxima, totals)

    initial = (
        jnp.zeros((length, D), jnp.float32),
        jnp.zeros((H, length), jnp.float32),
        jnp.zeros((H, length), jnp.float32),
    )
    return lax.fori_loop(0, H // head_group, one_group, initial)


def attend_backward(qkv_low, same_seq, maxima, totals, grad_mixed):
    length = qkv_low.shape[0]
    head_group = math.gcd(H, 4)
    group_width = head_group * HD

    def one_group(group_index, grad_qkv):
        first_col = group_index * group_width
        queries, keys_part, values = head_slices(qkv_low, first_col, head_group)
        grad_part = lax.dynamic_slice_in_dim(grad_mixed, first_col, group_width, 1).reshape(
            length, head_group, HD
        )
        scores = masked_scores(queries, keys_part, same_seq)
        row_max = lax.dynamic_slice_in_dim(maxima, group_index * head_group, head_group, 0)[
            :, :, None
        ]
        row_total = lax.dynamic_slice_in_dim(totals, group_index * head_group, head_group, 0)[
            :, :, None
        ]
        attn_probs = jnp.exp(scores - row_max) / row_total
        grad_probs = jnp.einsum(
            "qhe,khe->hqk", grad_part, values, preferred_element_type=jnp.float32
        )
        grad_values = jnp.einsum(
            "hqk,qhe->khe",
            attn_probs.astype(jnp.bfloat16),
            grad_part,
            preferred_element_type=jnp.float32,
        )
        grad_scores = attn_probs * (
            grad_probs - jnp.sum(grad_probs * attn_probs, axis=-1, keepdims=True)
        )
        grad_scores = grad_scores.astype(jnp.bfloat16)
        grad_queries = jnp.einsum(
            "hqk,khe->qhe", grad_scores, keys_part, preferred_element_type=jnp.float32
        ) * HD ** (-0.5)
        grad_keys = jnp.einsum(
            "hqk,qhe->khe", grad_scores, queries, preferred_element_type=jnp.float32
        ) * HD ** (-0.5)
        for offset, grad_piece in ((0, grad_queries), (D, grad_keys), (2 * D, grad_values)):
            grad_qkv = lax.dynamic_update_slice_in_dim(
                grad_qkv, grad_piece.reshape(length, group_width), offset + first_col, 1
            )
        return grad_qkv

    return lax.fori_loop(0, H // head_group, one_group, jnp.zeros((length, 3 * D), jnp.float32))


def sgd_update(weights_old, moment, average, grad_sum, step_rate):
    moment_new = MOMENT_DECAY * moment + grad_sum
    weights_new = weights_old - step_rate * (grad_sum + MOMENT_DECAY * moment_new)
    average_new = AVERAGE_DECAY * average + (1.0 - AVERAGE_DECAY) * weights_new
    return (moment_new, weights_new, average_new, weights_new.astype(jnp.bfloat16))


def local(
    block_input,
    output_grad,
    sequence_ids,
    attn_weights,
    attn_momentum,
    attn_average,
    norm_params,
    norm_momentum,
    norm_average,
    ffn_weights,
    ffn_momentum,
    ffn_average,
):
    attn_full, norm_full = (
        lax.all_gather(attn_weights.astype(jnp.bfloat16), ("row", "col"), axis=1, tiled=True),
        lax.all_gather(norm_params.astype(jnp.bfloat16), ("row", "col"), axis=0, tiled=True),
    )
    norm_values = norm_full.astype(jnp.float32)
    gain_one = norm_values[:D]
    shift_one = norm_values[D : 2 * D]
    gain_two = norm_values[2 * D : 3 * D]
    shift_two = norm_values[3 * D :]
    qkv_weights = attn_full[:, : 3 * D]
    out_weights = attn_full[:, 3 * D :]
    ffn_rows = lax.all_gather(ffn_weights.astype(jnp.bfloat16), "row", axis=1, tiled=True)
    col_width = ffn_weights.shape[2]
    length = block_input.shape[1]
    attn_acc = jnp.zeros((D, 4 * D), jnp.float32)
    norm_acc = jnp.zeros((4 * D,), jnp.float32)
    ffn_acc = jnp.zeros((2, D, col_width), jnp.float32)
    outputs_all = []
    grads_all = []
    for micro_step in range(MB):
        inputs = block_input[micro_step]
        ids_row = sequence_ids[micro_step]
        same_seq = ids_row[:, None] == ids_row[None, :]
        normed, pull_one = jax.vjp(layer_norm, inputs, gain_one, shift_one)
        normed_low = normed.astype(jnp.bfloat16)
        qkv_low = matmul(normed_low, qkv_weights).astype(jnp.bfloat16)
        mixed_all, maxima, totals = attend_forward(qkv_low, same_seq)
        mixed_low = mixed_all.astype(jnp.bfloat16)
        hidden_in = inputs + matmul(mixed_low, out_weights)
        normed_two, pull_two = jax.vjp(layer_norm, hidden_in, gain_two, shift_two)
        normed_two_low = normed_two.astype(jnp.bfloat16)
        grad_out = output_grad[micro_step]
        grad_out_low = grad_out.astype(jnp.bfloat16)
        normed_all = lax.all_gather(normed_two_low, "col", axis=0, tiled=True)
        up_proj = matmul(normed_all, ffn_rows[0])
        activation, pull_gelu = jax.vjp(gelu_exact, up_proj)
        activ_low = activation.astype(jnp.bfloat16)
        ffn_out = lax.psum_scatter(
            contract_cols(activ_low, ffn_rows[1]).astype(jnp.bfloat16),
            "col",
            scatter_dimension=0,
            tiled=True,
        ).astype(jnp.float32)
        grad_all = lax.all_gather(grad_out_low, "col", axis=0, tiled=True)
        grad_act = matmul(grad_all, ffn_rows[1])
        grad_up = pull_gelu(grad_act)[0].astype(jnp.bfloat16)
        grad_normed_two = lax.psum_scatter(
            contract_cols(grad_up, ffn_rows[0]).astype(jnp.bfloat16),
            "col",
            scatter_dimension=0,
            tiled=True,
        ).astype(jnp.float32)
        ffn_acc = ffn_acc + jnp.stack(
            [contract_rows(normed_all, grad_up), contract_rows(grad_all, activ_low)]
        )
        outputs_all.append(hidden_in + ffn_out)
        grad_ln_two, gain_two_grad, shift_two_grad = pull_two(grad_normed_two)
        grad_hidden = grad_out + grad_ln_two
        grad_branch_low = grad_hidden.astype(jnp.bfloat16)
        out_proj_grad = contract_rows(mixed_low, grad_branch_low)
        grad_mixed_low = contract_cols(grad_branch_low, out_weights).astype(jnp.bfloat16)
        grad_qkv_low = attend_backward(qkv_low, same_seq, maxima, totals, grad_mixed_low).astype(
            jnp.bfloat16
        )
        qkv_grad = contract_rows(normed_low, grad_qkv_low)
        grad_normed = contract_cols(grad_qkv_low, qkv_weights)
        grad_ln_one, gain_one_grad, shift_one_grad = pull_one(grad_normed)
        grads_all.append(grad_hidden + grad_ln_one)
        attn_acc = attn_acc + jnp.concatenate([qkv_grad, out_proj_grad], axis=1)
        norm_acc = norm_acc + jnp.concatenate(
            [gain_one_grad, shift_one_grad, gain_two_grad, shift_two_grad]
        )
    ffn_grad = lax.psum_scatter(
        ffn_acc.astype(jnp.bfloat16), "row", scatter_dimension=1, tiled=True
    ).astype(jnp.float32)
    attn_grad, norm_grad = (
        lax.psum_scatter(attn_acc, ("row", "col"), scatter_dimension=1, tiled=True),
        lax.psum_scatter(norm_acc, ("row", "col"), scatter_dimension=0, tiled=True),
    )
    total_tokens = MB * length * lax.axis_size("row") * lax.axis_size("col")
    step_rate = RATE_SCALE * total_tokens ** (-0.5)
    attn_moment_new, attn_new, attn_avg_new, attn_copy = sgd_update(
        attn_weights, attn_momentum, attn_average, attn_grad, step_rate
    )
    norm_moment_new, norm_new, norm_avg_new, norm_copy = sgd_update(
        norm_params, norm_momentum, norm_average, norm_grad, step_rate
    )
    ffn_moment_new, ffn_new, ffn_avg_new, ffn_copy = sgd_update(
        ffn_weights, ffn_momentum, ffn_average, ffn_grad, step_rate
    )
    return (
        jnp.stack(outputs_all),
        jnp.stack(grads_all),
        attn_grad,
        attn_moment_new,
        attn_new,
        attn_avg_new,
        attn_copy,
        norm_grad,
        norm_moment_new,
        norm_new,
        norm_avg_new,
        norm_copy,
        ffn_grad,
        ffn_moment_new,
        ffn_new,
        ffn_avg_new,
        ffn_copy,
    )


def solution(mesh):
    return jax.shard_map(
        local,
        mesh=mesh,
        in_specs=(
            P(None, ("row", "col"), None),
            P(None, ("row", "col"), None),
            P(None, ("row", "col")),
            P(None, ("row", "col")),
            P(None, ("row", "col")),
            P(None, ("row", "col")),
            P(("row", "col")),
            P(("row", "col")),
            P(("row", "col")),
            P(None, "row", "col"),
            P(None, "row", "col"),
            P(None, "row", "col"),
        ),
        out_specs=(
            P(None, ("row", "col"), None),
            P(None, ("row", "col"), None),
            P(None, ("row", "col")),
            P(None, ("row", "col")),
            P(None, ("row", "col")),
            P(None, ("row", "col")),
            P(None, ("row", "col")),
            P(("row", "col")),
            P(("row", "col")),
            P(("row", "col")),
            P(("row", "col")),
            P(("row", "col")),
            P(None, "row", "col"),
            P(None, "row", "col"),
            P(None, "row", "col"),
            P(None, "row", "col"),
            P(None, "row", "col"),
        ),
        check_vma=False,
    )
```

profile of v0, /device:TPU:0, one launch (start us, length us, event | category | flops | bytes accessed | tf_op | source)
XLA Modules:
  0.0 634.5 jit_solution(1245583940344998893)
XLA Ops:
  16.0 42.1 %all-reduce = bf16[2560]{0:T(1024)(128)(2,1)S(1)} all-reduce(bf16[2560]{0:T(1024)(128)(2,1)S(1)} %dynamic-update-slice), channel_id=1, replica_groups=mesh['row'=4,'col'=8] {'row','col'}, use_global_device_ids=true, to_apply=%add | all-reduce | flops 2560 | bytes 10240
  58.1 15.5 %all-gather.7.cloned.1.call-done = bf16[640,2560]{0,1:T(8,128)(2,1)} async-done(((bf16[640,80]{0,1:T(8,128)(2,1)}), bf16[640,2560]{0,1:T(8,128)(2,1)}) %all-gather.7.cloned.1.call-update) | async-done | bytes 3276816 | tf_op jit(solution)/shard_map/all_gather | solution.py:174
  77.3 5.3 while.73
  85.1 4.0 convolution_convert_fusion.5
  91.6 8.2 %while.72 = (s32[]{:T(128)}, bf16[256,640]{0,1:T(8,128)(2,1)}, f32[20,256]{1,0:T(8,128)S(1)}, f32[20,256]{1,0:T(8,128)S(1)}, bf16[256,1920]{0,1:T(8,128)(2,1)S(1...) while((s32[]{:T(128)}, bf16[256,640]{0,1:T(8,128)(2,1)}, ...), condition=%wide.region_5.6_spmd.clone, body=%wide.region_2.5_spmd.clone.sunk | while | flops 35715084 | bytes 4101494 | solution.py:102
  109.4 33.3 %all-gather.9.cloned.1.call-done = bf16[2048,640]{1,0:T(8,128)(2,1)} async-done(((bf16[256,640]{1,0:T(8,128)(2,1)}), bf16[2048,640]{1,0:T(8,128)(2,1)}) %all-gather.9.cloned.1.call-update) | async-done | bytes 2621456 | tf_op jit(solution)/shard_map/all_gather | solution.py:206
  142.7 16.6 %multiply_convert_fusion.3 = (bf16[2048,640]{1,0:T(8,128)(2,1)}, f32[2048,640]{1,0:T(8,128)}, f32[2048,640]{1,0:T(8,128)}) fusion(bf16[2048,640]{1,0:T(8,128)(2,1)} %all-gather.9.cloned.1.call-done, bf16[2,640,640]{2,1,0:T(8,128)(2,1)} %all-gather.11.cloned.1.call-done), kind=kOutput, calls=%fused_computation.92 | convolution fusion | flops 1762918400 | bytes 16547840 | tf_op jit(solution)/shard_map/dot_general | solution.py:32
  159.3 17.8 %all-gather.15.cloned.1.call-done = bf16[2048,640]{1,0:T(8,128)(2,1)} async-done(((bf16[256,640]{1,0:T(8,128)(2,1)}), bf16[2048,640]{1,0:T(8,128)(2,1)}) %all-gather.15.cloned.1.call-update) | async-done | bytes 2621456 | tf_op jit(solution)/shard_map/all_gather | solution.py:216
  177.1 8.6 %add_convert_fusion.1 = bf16[2048,640]{1,0:T(8,128)(2,1)S(1)} fusion(f32[2048,640]{1,0:T(8,128)} %get-tuple-element.929, f32[2048,640]{1,0:T(8,128)} %get-tuple-element.981, bf16[2048,640]{1,0:T(8,128)(2,1)} %all-gather.15.cloned.1.call-done, bf16[2,640,640]{2,1,0:T(8,128)(2,1)} %all-gather.11.cloned.1.call-done), kind=kOutput, calls=%fused_computation.78 | convolution fusion | flops 1696071680 | bytes 16547840 | tf_op jit(solution)/shard_map/dot_general | solution.py:32
  191.2 20.9 %all-gather.13.cloned.1.call-done = bf16[2048,640]{1,0:T(8,128)(2,1)} async-done(((bf16[256,640]{1,0:T(8,128)(2,1)}), bf16[2048,640]{1,0:T(8,128)(2,1)}) %all-gather.13.cloned.1.call-update) | async-done | bytes 2621456 | tf_op jit(solution)/shard_map/all_gather | solution.py:206
  212.0 16.5 %multiply_convert_fusion.2 = (bf16[2048,640]{1,0:T(8,128)(2,1)}, f32[2048,640]{1,0:T(8,128)}, f32[2048,640]{1,0:T(8,128)}) fusion(bf16[2048,640]{1,0:T(8,128)(2,1)} %all-gather.13.cloned.1.call-done, bf16[2,640,640]{2,1,0:T(8,128)(2,1)} %all-gather.11.cloned.1.call-done), kind=kOutput, calls=%fused_computation.79 | convolution fusion | flops 1762918400 | bytes 16547840 | tf_op jit(solution)/shard_map/dot_general | solution.py:32
  228.6 17.9 %all-gather.17.cloned.1.call-done = bf16[2048,640]{1,0:T(8,128)(2,1)} async-done(((bf16[256,640]{1,0:T(8,128)(2,1)}), bf16[2048,640]{1,0:T(8,128)(2,1)}) %all-gather.17.cloned.1.call-update) | async-done | bytes 2621456 | tf_op jit(solution)/shard_map/all_gather | solution.py:216
  246.4 8.6 %add_convert_fusion = bf16[2048,640]{1,0:T(8,128)(2,1)S(1)} fusion(f32[2048,640]{1,0:T(8,128)} %get-tuple-element.931, f32[2048,640]{1,0:T(8,128)} %get-tuple-element.982, bf16[2048,640]{1,0:T(8,128)(2,1)} %all-gather.17.cloned.1.call-done, bf16[2,640,640]{2,1,0:T(8,128)(2,1)} %all-gather.11.cloned.1.call-done), kind=kOutput, calls=%fused_computation.77 | convolution fusion | flops 1696071680 | bytes 16547840 | tf_op jit(solution)/shard_map/dot_general | solution.py:32
  260.4 6.0 convolution_convert_fusion.2
  266.7 5.9 convolution_convert_fusion.3
  272.7 5.0 convolution_bitcast_fusion
  288.4 35.9 %reduce-scatter.15.cloned.1.call-done = bf16[256,640]{1,0:T(8,128)(2,1)} async-done(((bf16[2048,640]{1,0:T(8,128)(2,1)}), bf16[256,640]{1,0:T(8,128)(2,1)}) %reduce-scatter.15.cloned.1.call-update) | async-done | bytes 327696 | tf_op jit(solution)/shard_map/reduce_scatter | solution.py:219
  327.2 35.8 %reduce-scatter.11.cloned.1.call-done = bf16[256,640]{1,0:T(8,128)(2,1)} async-done(((bf16[2048,640]{1,0:T(8,128)(2,1)}), bf16[256,640]{1,0:T(8,128)(2,1)}) %reduce-scatter.11.cloned.1.call-update) | async-done | bytes 327696 | tf_op jit(solution)/shard_map/reduce_scatter | solution.py:210
  363.1 38.7 %reduce-scatter.9.cloned.1.call-done = bf16[256,640]{1,0:T(8,128)(2,1)} async-done(((bf16[2048,640]{1,0:T(8,128)(2,1)}), bf16[256,640]{1,0:T(8,128)(2,1)}) %reduce-scatter.9.cloned.1.call-update) | async-done | bytes 327696 | tf_op jit(solution)/shard_map/reduce_scatter | solution.py:210
  407.1 15.2 %while.74 = (s32[]{:T(128)}, bf16[256,1920]{0,1:T(8,128)(2,1)S(1)}, bf16[256,1920]{0,1:T(8,128)(2,1)}, f32[20,256]{1,0:T(8,128)S(1)}, f32[20,256]{1,0:T(8,128)S(...) while((s32[]{:T(128)}, bf16[256,1920]{0,1:T(8,128)(2,1)S(1)}, ...), condition=%wide.region_23.24_spmd.clone, body=%wide.region_21.0_spmd.clone.sunk | while | flops 86703120 | bytes 9733514 | solution.py:149
  426.0 31.9 %while.75 = (s32[]{:T(128)}, bf16[256,1920]{0,1:T(8,128)(2,1)}, bf16[256,1920]{0,1:T(8,128)(2,1)}, f32[20,256]{1,0:T(8,128)}, f32[20,256]{1,0:T(8,128)}, /*index...) while((s32[]{:T(128)}, bf16[256,1920]{0,1:T(8,128)(2,1)}, ...), condition=%wide.region_31.32_spmd.clone, body=%wide.region_29.0_spmd.clone.sunk | while | flops 86703120 | bytes 9733514 | solution.py:149
  466.5 8.2 %copy.93 = f32[640,2560]{0,1:T(8,128)} copy(f32[640,2560]{1,0:T(8,128)} %maximum_add_fusion) | data formatting | bytes 13107200
  488.4 38.9 %all-reduce.1 = f32[2560]{0:T(1024)S(1)} all-reduce(f32[2560]{0:T(1024)S(1)} %maximum_add_fusion.2), channel_id=7, replica_groups=mesh['row'=4,'col'=8] {'row','col'}, use_global_device_ids=true, to_apply=%region_43.44.clone | all-reduce | flops 2560 | bytes 20480
  534.1 87.8 %reduce-scatter.19.cloned.1.call-done = f32[80,640]{1,0:T(8,128)} async-done(((f32[2560,640]{1,0:T(8,128)}), f32[80,640]{1,0:T(8,128)}) %reduce-scatter.19.cloned.1.call-update) | async-done | bytes 204816
  (427 shorter events, 153.8 us)
Async XLA Ops:
  7.2 66.4 %all-gather.7.cloned.1.call-start = ((), (), s32[]{:S(2)}) async-start(), calls=%async_computation.6 | async-start | bytes 3379200 | tf_op jit(solution)/shard_map/all_gather | solution.py:174
  8.8 100.5 %all-gather.11.cloned.1.call-start = ((), (), s32[]{:S(2)}) async-start(), calls=%async_computation.8 | async-start | bytes 2048000 | tf_op jit(solution)/shard_map/all_gather | solution.py:184
  10.9 131.8 %all-gather.9.cloned.1.call-start = ((), (), s32[]{:S(2)}) async-start(), calls=%async_computation.7 | async-start | bytes 2949120 | tf_op jit(solution)/shard_map/all_gather | solution.py:206
  13.8 63.5 %copy-start.35 = (f32[256]{0:T(256)}, f32[256]{0:T(256)S(1)}, u32[]{:S(2)}) copy-start(f32[256]{0:T(256)S(1)} %get-tuple-element.984) | copy-start | bytes 3076
  13.8 68.8 %copy-start.37 = (f32[256]{0:T(256)}, f32[256]{0:T(256)S(1)}, u32[]{:S(2)}) copy-start(f32[256]{0:T(256)S(1)} %get-tuple-element.985) | copy-start | bytes 3076
  15.4 67.2 %copy-start.39 = (f32[256]{0:T(256)}, f32[256]{0:T(256)S(1)}, u32[]{:S(2)}) copy-start(f32[256]{0:T(256)S(1)} %fusion.77) | copy-start | bytes 3076
  15.4 61.8 %copy-start.41 = (f32[256]{0:T(256)}, f32[256]{0:T(256)S(1)}, u32[]{:S(2)}) copy-start(f32[256]{0:T(256)S(1)} %fusion.79) | copy-start | bytes 3076
  105.4 71.7 %all-gather.15.cloned.1.call-start = ((), (), s32[]{:S(2)}) async-start(), calls=%async_computation.12 | async-start | bytes 2949120 | tf_op jit(solution)/shard_map/all_gather | solution.py:216
  107.6 104.4 %all-gather.13.cloned.1.call-start = ((), (), s32[]{:S(2)}) async-start(), calls=%async_computation.10 | async-start | bytes 2949120 | tf_op jit(solution)/shard_map/all_gather | solution.py:206
  108.2 138.2 %all-gather.17.cloned.1.call-start = ((), (), s32[]{:S(2)}) async-start(), calls=%async_computation.14 | async-start | bytes 2949120 | tf_op jit(solution)/shard_map/all_gather | solution.py:216
  108.8 178.4 %reduce-scatter.13.cloned.1.call-start = ((), (), s32[]{:S(2)}) async-start(), calls=%async_computation.13 | async-start | bytes 2949120 | tf_op jit(solution)/shard_map/reduce_scatter | solution.py:219
  190.9 133.3 %reduce-scatter.15.cloned.1.call-start = ((), (), s32[]{:S(2)}) async-start(), calls=%async_computation.15 | async-start | bytes 2949120 | tf_op jit(solution)/shard_map/reduce_scatter | solution.py:219
  260.3 102.7 %reduce-scatter.11.cloned.1.call-start = ((), (), s32[]{:S(2)}) async-start(), calls=%async_computation.11 | async-start | bytes 2949120 | tf_op jit(solution)/shard_map/reduce_scatter | solution.py:210
  266.4 135.4 %reduce-scatter.9.cloned.1.call-start = ((), (), s32[]{:S(2)}) async-start(), calls=%async_computation.9 | async-start | bytes 2949120 | tf_op jit(solution)/shard_map/reduce_scatter | solution.py:210
  272.6 205.7 %reduce-scatter.17.cloned.1.call-start = ((), (), s32[]{:S(2)}) async-start(), calls=%async_computation.16 | async-start | bytes 2048000 | tf_op jit(solution)/shard_map/reduce_scatter | solution.py:245
  285.2 116.6 %copy-start.13 = (f32[2,256,640]{2,1,0:T(8,128)S(1)}, f32[2,256,640]{2,1,0:T(8,128)}, u32[]{:S(2)}) copy-start(f32[2,256,640]{2,1,0:T(8,128)} %param.21) | copy-start | bytes 3932164
  286.7 335.2 %reduce-scatter.19.cloned.1.call-start = ((), (), s32[]{:S(2)}) async-start(), calls=%async_computation.17 | async-start | bytes 6758400
  426.0 32.4 %copy-start.3 = (f32[256,640]{1,0:T(8,128)S(1)}, f32[256,640]{1,0:T(8,128)}, u32[]{:S(2)}) copy-start(f32[256,640]{1,0:T(8,128)} %copy-done.2) | copy-start | bytes 1966084
  484.0 43.4 %copy-start.20 = (f32[1,256,640]{2,1,0:T(8,128)S(1)}, f32[1,256,640]{2,1,0:T(8,128)}, u32[]{:S(2)}) copy-start(f32[1,256,640]{2,1,0:T(8,128)} %get-tuple-element.966) | copy-start | bytes 1966084
  486.3 43.3 %copy-start.46 = (f32[256]{0:T(256)S(1)}, f32[256]{0:T(256)}, u32[]{:S(2)}) copy-start(f32[256]{0:T(256)} %copy-done.45) | copy-start | bytes 3076
  486.3 43.3 %copy-start.44 = (f32[256]{0:T(256)S(1)}, f32[256]{0:T(256)}, u32[]{:S(2)}) copy-start(f32[256]{0:T(256)} %copy-done.43) | copy-start | bytes 3076
  531.5 91.5 %copy-start.21 = (f32[640,80]{1,0:T(8,128)S(1)}, f32[640,80]{1,0:T(8,128)}, u32[]{:S(2)}) copy-start(f32[640,80]{1,0:T(8,128)} %copy.72) | copy-start | bytes 614404
  531.5 91.5 %copy-start.22 = (f32[640,80]{1,0:T(8,128)S(1)}, f32[640,80]{1,0:T(8,128)}, u32[]{:S(2)}) copy-start(f32[640,80]{1,0:T(8,128)} %copy.71) | copy-start | bytes 614404
  533.5 93.9 %copy-start.49 = (f32[80]{0:T(128)}, f32[80]{0:T(128)S(1)}, u32[]{:S(2)}) copy-start(f32[80]{0:T(128)S(1)} %get-tuple-element.919) | copy-start | bytes 964
  (43 other events, 220.4 us)
Sparse Core Ops, SparseCore 0:
  11.4 62.0 all-gather.6
  76.0 30.5 all-gather.10
  108.8 33.8 all-gather.8
  144.2 32.8 all-gather.14
  179.1 32.8 all-gather.12
  213.5 32.8 all-gather.16
  248.7 36.4 reduce-scatter.12
  287.6 36.6 reduce-scatter.14
  326.5 36.4 reduce-scatter.10
  365.2 36.4 reduce-scatter.8
  404.8 30.5 reduce-scatter.16
  474.8 147.0 reduce-scatter.18
where the time goes:
time: 642 us; the launch traced here: 634 us
  waiting for transfers between devices  305 us (48%)
  matrix products  128 us (20%)
  blocking collectives  81 us (13%)
  local copies, waits for them, and re-layouts  62.4 us (10%)
  other arithmetic  39.2 us (6%)
  between operations  15.2 us (2%)
    unnamed x13, waiting for transfers between devices  89.1 us
    unnamed x2, blocking collectives  81 us
    reduce_scatter x2, waiting for transfers between devices, local(): lax.psum_scatter(contract_cols(activ_low, ffn_rows[1]).astype(jnp.bfloat1...  74.5 us
    dot_general x8, matrix products, matmul(): return jnp.dot(left_side, right_side, preferred_element_type=jnp.float32)  61.2 us
    all_gather x2, waiting for transfers between devices, local(): normed_all = lax.all_gather(normed_two_low, 'col', axis=0, tiled=True)  54.2 us
    reduce_scatter x2, waiting for transfers between devices, local(): lax.psum_scatter(contract_cols(grad_up, ffn_rows[0]).astype(jnp.bfloat16)...  35.9 us
    all_gather x2, waiting for transfers between devices, local(): grad_all = lax.all_gather(grad_out_low, 'col', axis=0, tiled=True)  35.7 us
    dot_general x8, matrix products, contract_cols(): lax.dot_general(left_side, right_side, (((1,), (1,)), ((), ())), preferre...  28 us
  transfers between devices with their start and end apart: 12, of which 9 were waited for; matrix products, arithmetic and copies ran while one was open for 34% of the time, Pallas kernels for 0%

commit v1 on v0

--- a/solution.py
+++ b/solution.py
@@ -1,8 +1,11 @@
+import functools
 import math
 
 import jax
 import jax.numpy as jnp
 from jax import lax
+from jax.experimental import pallas as pl
+from jax.experimental.pallas import tpu as pltpu
 from jax.sharding import PartitionSpec as P
 
 D = 640
@@ -156,7 +159,7 @@
     return (moment_new, weights_new, average_new, weights_new.astype(jnp.bfloat16))
 
 
-def local(
+def local_general(
     block_input,
     output_grad,
     sequence_ids,
@@ -281,6 +284,682 @@
     )
 
 
+MESH_ID = pl.DeviceIdType.MESH
+BF = jnp.bfloat16
+F32 = jnp.float32
+LANES = 128
+HEADS_TILE = LANES // HD
+PAD_ROWS = 96
+HALF_ROWS = PAD_ROWS // 2
+Z_SIZE = 4
+ROWS = 4
+
+
+def dot_nn(a, b):
+    return lax.dot_general(a, b, (((1,), (0,)), ((), ())), preferred_element_type=F32)
+
+
+def dot_nt(a, b):
+    return lax.dot_general(a, b, (((1,), (1,)), ((), ())), preferred_element_type=F32)
+
+
+def dot_tn(a, b):
+    return lax.dot_general(a, b, (((0,), (0,)), ((), ())), preferred_element_type=F32)
+
+
+def ln_stats(values):
+    center = values - jnp.mean(values, axis=-1, keepdims=True)
+    spread = jnp.mean(center * center, axis=-1, keepdims=True)
+    inv = lax.rsqrt(spread + EPSILON)
+    return center * inv, inv
+
+
+def ln_backward(normal, inv, gain, grad):
+    scaled = grad * gain
+    mean_one = jnp.mean(scaled, axis=-1, keepdims=True)
+    mean_two = jnp.mean(scaled * normal, axis=-1, keepdims=True)
+    return inv * (scaled - mean_one - normal * mean_two)
+
+
+def erf_f32(v):
+    v = jnp.clip(v, -3.832506856900711, 3.832506856900711)
+    s = v * v
+    num = jnp.full_like(s, 0.00022905065861350646)
+    for coef in (
+        0.0034082910107109506,
+        0.050955695062380861,
+        0.18520832239976145,
+        1.128379143519084,
+    ):
+        num = num * s + coef
+    den = jnp.full_like(s, -1.1791602954361697e-7)
+    for coef in (
+        0.000023547966471313185,
+        0.0010179625278914885,
+        0.014070470171167667,
+        0.11098505178285362,
+        0.49746925110067538,
+        1.0,
+    ):
+        den = den * s + coef
+    return v * num / den
+
+
+def gelu_pair(u):
+    phi_cap = 0.5 + 0.5 * erf_f32(u * (2.0 ** -0.5))
+    density = jnp.exp(-0.5 * u * u) * (1.0 / math.sqrt(2.0 * math.pi))
+    return u * phi_cap, phi_cap + u * density
+
+
+def step_kernel(
+    x_hbm, dy_hbm, idr, idc, wsh, fsh,
+    yout, ig, fgrad, agrad,
+    wslot, wall, fw, n1, qkv, abuf, obuf, tn2, tdy, n2t, dyt, gb, dub, yacc, dnacc, ry, rdn, dyv, dw,
+    fr1, fr2, fr3, rc, ar1, ar2, ar3, bias, dob,
+    ld_sem, ag_s, ag_r, fg_s, fg_r, sib_s, sib_r, tok_s, tok_r, part_s, part_r,
+    frs_s, frs_r, ars_s, ars_r, rc_s, rc_r,
+):
+    r = lax.axis_index("row")
+    c = lax.axis_index("col")
+    y, x, z, k = r // 2, r % 2, c // 2, c % 2
+    rx, ry_, rd = y * 2 + (1 - x), (1 - y) * 2 + x, (1 - y) * 2 + (1 - x)
+    dev_x = (rx, c)
+    dev_y = (ry_, c)
+    dev_sib = (r, z * 2 + (1 - k))
+
+    def zat(j):
+        return ((z // 2 + j // 2) % 2) * 2 + (z % 2 + j % 2) % 2
+
+    def dev_z(j):
+        return (r, zat(j) * 2 + k)
+
+    def remote(src, dst, ss, rs, dev):
+        return pltpu.make_async_remote_copy(
+            src_ref=src, dst_ref=dst, send_sem=ss, recv_sem=rs, device_id=dev, device_id_type=MESH_ID
+        )
+
+    ld_x = pltpu.make_async_copy(x_hbm, ig, ld_sem.at[0])
+    ld_y = pltpu.make_async_copy(dy_hbm, dyv, ld_sem.at[1])
+    ld_x.start()
+    ld_y.start()
+
+    barrier = pltpu.get_barrier_semaphore()
+    for dev in (dev_sib, dev_x, dev_y, dev_z(1), dev_z(2), dev_z(3)):
+        pl.semaphore_signal(barrier, inc=1, device_id=dev, device_id_type=MESH_ID)
+
+    wslot[r, z, k] = wsh[...]
+    fw[z, :, r] = fsh[...]
+    pl.semaphore_wait(barrier, 6)
+
+    def a_piece(rr, zz):
+        return wslot.at[rr, zz, k]
+
+    def a_part(rr, zz, p):
+        return wslot.at[rr, zz, k, pl.ds(HALF_ROWS * p, HALF_ROWS)]
+
+    def f_piece(rr, zz):
+        return fw.at[zz, :, rr]
+
+    def f_part(rr, zz, p):
+        return fw.at[zz, p, rr]
+
+    def gather_ops(piece, part, ss, rs):
+        def cz(j):
+            return remote(piece(r, z), piece(r, z), ss.at[0, j], rs.at[0, j], dev_z(j))
+
+        def cx(j):
+            return remote(piece(r, zat(j)), piece(r, zat(j)), ss.at[1, j], rs.at[1, j], dev_x)
+
+        def cy(j):
+            return remote(piece(r, zat(j)), piece(r, zat(j)), ss.at[2, j], rs.at[2, j], dev_y)
+
+        def cd0(j):
+            return remote(part(rx, zat(j), 0), part(rx, zat(j), 0), ss.at[3, j], rs.at[3, j], dev_y)
+
+        def cd1(j):
+            return remote(part(ry_, zat(j), 1), part(ry_, zat(j), 1), ss.at[4, j], rs.at[4, j], dev_x)
+
+        return cz, cx, cy, cd0, cd1
+
+    az, ax, ay, ad0, ad1 = gather_ops(a_piece, a_part, ag_s, ag_r)
+    fz, fx, fy, fd0, fd1 = gather_ops(f_piece, f_part, fg_s, fg_r)
+
+    def sib(j):
+        return remote(
+            wslot.at[:, zat(j), k], wslot.at[:, zat(j), k], sib_s.at[j], sib_r.at[j], dev_sib
+        )
+
+    for j in (1, 2, 3):
+        az(j).start()
+    ax(0).start()
+    ay(0).start()
+
+    ld_y.wait()
+
+    def make_bias(m, _):
+        bias[m] = jnp.where(idr[m] == idc[m], 0.0, MASKED).astype(F32)
+        tdy[2 * k + m] = dyv[m].astype(BF)
+        return 0
+
+    lax.fori_loop(0, MB, make_bias, 0)
+
+    def tok_dy():
+        return remote(tdy.at[pl.ds(2 * k, 2)], tdy.at[pl.ds(2 * k, 2)], tok_s.at[0], tok_r.at[0], dev_sib)
+
+    def tok_n2():
+        return remote(tn2.at[pl.ds(2 * k, 2)], tn2.at[pl.ds(2 * k, 2)], tok_s.at[1], tok_r.at[1], dev_sib)
+
+    tok_dy().start()
+
+    ax(0).wait_recv()
+    ad0(0).start()
+    ay(0).wait_recv()
+    ad1(0).start()
+    for j in (1, 2, 3):
+        az(j).wait_recv()
+        ax(j).start()
+        ay(j).start()
+    for j in (1, 2, 3):
+        fz(j).start()
+    for j in (1, 2, 3):
+        ax(j).wait_recv()
+        ad0(j).start()
+        ay(j).wait_recv()
+        ad1(j).start()
+    fx(0).start()
+    fy(0).start()
+    for j in range(Z_SIZE):
+        ad0(j).wait_recv()
+        ad1(j).wait_recv()
+        sib(j).start()
+    for j in range(Z_SIZE):
+        sib(j).wait_recv()
+
+    def compact(d, _):
+        wall[d] = wslot[d // (2 * Z_SIZE), (d // 2) % Z_SIZE, d % 2, 0:80]
+        return 0
+
+    lax.fori_loop(0, 8 * ROWS, compact, 0)
+
+    def norm_vector(row):
+        total = jnp.zeros((1, D), F32)
+        for zz in range(Z_SIZE):
+            for kk in range(2):
+                total = total + wslot[row, zz, kk, 80:96].astype(F32)[0:1]
+        return total
+
+    gain_one, shift_one, gain_two, shift_two = [norm_vector(row) for row in range(4)]
+
+    ld_x.wait()
+
+    def first_norm(m, _):
+        normal, _inv = ln_stats(ig[m])
+        n1[m] = (normal * gain_one + shift_one).astype(BF)
+        return 0
+
+    lax.fori_loop(0, MB, first_norm, 0)
+
+    def project(i, _):
+        m, p = i // 3, i % 3
+        weights = wall[pl.ds(8 * p, 8)].reshape(D, D)
+        qkv[m, p] = dot_nt(n1[m], weights).astype(BF)
+        return 0
+
+    lax.fori_loop(0, 3 * MB, project, 0)
+
+    lane_head = lax.broadcasted_iota(jnp.int32, (1, LANES), 1) // HD
+    head_mask = [jnp.where(lane_head == h, 1.0, 0.0).astype(BF) for h in range(HEADS_TILE)]
+    groups = D // LANES
+    scale = HD ** (-0.5)
+
+    def at_step(it, i, fn):
+        @pl.when(it == i)
+        def _():
+            fn()
+
+    def gather_xy(j):
+        fz(j).wait_recv()
+        fx(j).start()
+        fy(j).start()
+
+    def gather_diag(j):
+        fx(j).wait_recv()
+        fd0(j).start()
+        fy(j).wait_recv()
+        fd1(j).start()
+
+    def forward_group(it, _):
+        m, g = it // groups, it % groups
+        at_step(it, 1, lambda: gather_diag(0))
+        at_step(it, 3, lambda: gather_xy(1))
+        at_step(it, 5, lambda: gather_xy(2))
+        at_step(it, 6, lambda: gather_diag(1))
+        at_step(it, 8, lambda: gather_xy(3))
+        lanes = pl.ds(pl.multiple_of(g * LANES, LANES), LANES)
+        q = qkv[m, 0, :, lanes]
+        kk = qkv[m, 1, :, lanes]
+        v = qkv[m, 2, :, lanes]
+        mask_bias = bias[m]
+        mixed = None
+        for h in range(HEADS_TILE):
+            scores = dot_nt(q * head_mask[h], kk) * scale + mask_bias
+            row_max = jnp.max(scores, axis=-1, keepdims=True)
+            expo = jnp.exp(scores - row_max)
+            total = jnp.sum(expo, axis=-1, keepdims=True)
+            probs = (expo * (1.0 / total)).astype(BF)
+            abuf[it * HEADS_TILE + h] = probs
+            part = dot_nn(probs, v * head_mask[h])
+            mixed = part if mixed is None else mixed + part
+        obuf[m, :, lanes] = mixed.astype(BF)
+        return 0
+
+    lax.fori_loop(0, MB * groups, forward_group, 0)
+
+    def second_norm(m, _):
+        hidden = ig[m] + dot_nt(obuf[m], wall[24:32].reshape(D, D))
+        yout[m] = hidden
+        normal, _inv = ln_stats(hidden)
+        tn2[2 * k + m] = (normal * gain_two + shift_two).astype(BF)
+        return 0
+
+    lax.fori_loop(0, MB, second_norm, 0)
+    tok_n2().start()
+    gather_diag(2)
+    tok_dy().wait_recv()
+    tok_n2().wait_recv()
+
+    def turn(t, _):
+        cols = pl.ds(pl.multiple_of(t * 256, 256), 256)
+        n2t[:, :, cols] = tn2[t].T.reshape(ROWS, 160, 256)
+        dyt[:, :, cols] = tdy[t].T.reshape(ROWS, 160, 256)
+        return 0
+
+    lax.fori_loop(0, 2 * MB, turn, 0)
+
+    def scatter_ops(block, r1, r2, r3, ss, rs):
+        def one(j, p, b):
+            dev = dev_y if p == 0 else dev_x
+            rr = rd if b == 1 else (ry_ if p == 0 else rx)
+            return remote(block(rr, zat(j), p), r1(j, p, b), ss.at[2 * p + b, j], rs.at[2 * p + b, j], dev)
+
+        def two(j, p):
+            dev = dev_x if p == 0 else dev_y
+            rr = rx if p == 0 else ry_
+            return remote(block(rr, zat(j), p), r2(j, p), ss.at[4 + p, j], rs.at[4 + p, j], dev)
+
+        def three(j, p):
+            return remote(block(r, zat(j), p), r3(j, p), ss.at[6 + p, j], rs.at[6 + p, j], dev_z(j))
+
+        def start_one(j):
+            for p in range(2):
+                for b in (1, 0):
+                    one(j, p, b).start()
+
+        def start_two(j):
+            for p in range(2):
+                one(j, p, 0).wait_recv()
+                one(j, p, 1).wait_recv()
+                rr = rx if p == 0 else ry_
+                mine = block(rr, zat(j), p)
+                mine[...] = (mine[...].astype(F32) + r1(j, p, 1)[...].astype(F32)).astype(BF)
+                two(j, p).start()
+
+        def own_sum(j, p):
+            return (
+                block(r, zat(j), p)[...].astype(F32)
+                + r1(j, p, 0)[...].astype(F32)
+                + r2(j, p)[...].astype(F32)
+            )
+
+        def start_three(j):
+            for p in range(2):
+                two(j, p).wait_recv()
+                mine = block(r, zat(j), p)
+                mine[...] = own_sum(j, p).astype(BF)
+                three(j, p).start()
+
+        def finish(out):
+            for p in range(2):
+                two(0, p).wait_recv()
+                total = own_sum(0, p)
+                for j in (1, 2, 3):
+                    three(j, p).wait_recv()
+                    total = total + r3(j, p)[...].astype(F32)
+                out(p)[...] = total
+
+        def drain(j):
+            for p in range(2):
+                one(j, p, 0).wait_send()
+                one(j, p, 1).wait_send()
+                two(j, p).wait_send()
+
+        def drain_three(j):
+            for p in range(2):
+                three(j, p).wait_send()
+
+        return start_one, start_two, start_three, finish, drain, drain_three
+
+    f_one, f_two, f_three, f_finish, f_drain, f_drain3 = scatter_ops(
+        lambda rr, zz, p: dw.at[zz, p, rr],
+        lambda j, p, b: fr1.at[j, p, b],
+        lambda j, p: fr2.at[j, p],
+        lambda j, p: fr3.at[j - 1, p],
+        frs_s, frs_r,
+    )
+    a_one, a_two, a_three, a_finish, a_drain, a_drain3 = scatter_ops(
+        lambda rr, zz, p: wslot.at[rr, zz, k, pl.ds(HALF_ROWS * p, HALF_ROWS)],
+        lambda j, p, b: ar1.at[j, p, b],
+        lambda j, p: ar2.at[j, p],
+        lambda j, p: ar3.at[j - 1, p],
+        ars_s, ars_r,
+    )
+
+    def hidden_block(j, _):
+        @pl.when(j == 0)
+        def _():
+            gather_diag(3)
+
+        fd0(j).wait_recv()
+        fd1(j).wait_recv()
+        zz = zat(j)
+
+        def token_tile(t, _):
+            up = fw[zz, 0].reshape(D, D)
+            down = fw[zz, 1].reshape(D, D)
+            u = dot_nn(tn2[t], up)
+            grad_act = dot_nn(tdy[t], down)
+            act, slope = gelu_pair(u)
+            act = act.astype(BF)
+            grad_up = (grad_act * slope).astype(BF)
+            gb[t] = act
+            dub[t] = grad_up
+            y_part = dot_nt(act, down)
+            dn_part = dot_nt(grad_up, up)
+
+            @pl.when(j == 0)
+            def _():
+                yacc[t] = y_part
+                dnacc[t] = dn_part
+
+            @pl.when(j > 0)
+            def _():
+                yacc[t] += y_part
+                dnacc[t] += dn_part
+
+            return 0
+
+        lax.fori_loop(0, 2 * MB, token_tile, 0)
+
+        @pl.when(j == Z_SIZE - 1)
+        def _():
+            part_dn().start()
+            part_y().start()
+
+        def weight_rows(rr, _):
+            dw[zz, 0, rr] = dot_nn(n2t[rr], dub[...].reshape(4 * 256, D)).astype(BF)
+            dw[zz, 1, rr] = dot_nn(dyt[rr], gb[...].reshape(4 * 256, D)).astype(BF)
+            return 0
+
+        lax.fori_loop(0, ROWS, weight_rows, 0)
+        f_one(j)
+
+        @pl.when(j >= 2)
+        def _():
+            f_two(j - 2)
+
+        return 0
+
+    def part_dn():
+        return remote(dnacc.at[pl.ds(2 * (1 - k), 2)], rdn, part_s.at[0], part_r.at[0], dev_sib)
+
+    def part_y():
+        return remote(yacc.at[pl.ds(2 * (1 - k), 2)], ry, part_s.at[1], part_r.at[1], dev_sib)
+
+    lax.fori_loop(0, Z_SIZE, hidden_block, 0)
+
+    for j in (1, 2, 3):
+        az(j).wait_send()
+        fz(j).wait_send()
+    for j in range(Z_SIZE):
+        for op in (ax, ay, ad0, ad1, fx, fy, fd0, fd1, sib):
+            op(j).wait_send()
+
+    part_dn().wait_recv()
+    part_y().wait_recv()
+
+    zero = jnp.zeros((1, D), F32)
+
+    def second_backward(m, sums):
+        gain_sum, shift_sum = sums
+        hidden = yout[m]
+        normal, inv = ln_stats(hidden)
+        grad = dnacc[2 * k + m] + rdn[m]
+        yout[m] = hidden + (yacc[2 * k + m] + ry[m])
+        grad_hidden = dyv[m] + ln_backward(normal, inv, gain_two, grad)
+        dyv[m] = grad_hidden
+        low = grad_hidden.astype(BF)
+        n1_rows = wall[24:32].reshape(D, D)
+        dob[m] = dot_nn(low, n1_rows).astype(BF)
+        dhb = low
+        tn2[2 * k + m] = dhb
+        return (
+            gain_sum + jnp.sum(grad * normal, axis=0, keepdims=True),
+            shift_sum + jnp.sum(grad, axis=0, keepdims=True),
+        )
+
+    tok_n2().wait_send()
+    gain_two_grad, shift_two_grad = lax.fori_loop(0, MB, second_backward, (zero, zero))
+
+    out_grad = dot_tn(tn2[2 * k], obuf[0]) + dot_tn(tn2[2 * k + 1], obuf[1])
+    wslot[3, :, :, 0:80] = out_grad.astype(BF).reshape(Z_SIZE, 2, 80, D)
+
+    def backward_group(it, _):
+        m, g = it // groups, it % groups
+        at_step(it, 0, lambda: f_two(2))
+        at_step(it, 2, lambda: f_two(3))
+        at_step(it, 3, lambda: f_three(1))
+        at_step(it, 6, lambda: f_three(2))
+        at_step(it, 9, lambda: f_three(3))
+        lanes = pl.ds(pl.multiple_of(g * LANES, LANES), LANES)
+        q = qkv[m, 0, :, lanes]
+        kk = qkv[m, 1, :, lanes]
+        v = qkv[m, 2, :, lanes]
+        do = dob[m, :, lanes]
+        q_turned = q.T
+        do_turned = do.T
+        grad_q = None
+        grad_k = []
+        grad_v = []
+        for h in range(HEADS_TILE):
+            probs = abuf[it * HEADS_TILE + h]
+            wide = probs.astype(F32)
+            grad_probs = dot_nt(do * head_mask[h], v)
+            product = grad_probs * wide
+            row = jnp.sum(product, axis=-1, keepdims=True)
+            grad_scores = (product - wide * row).astype(BF)
+            part = dot_nn(grad_scores, kk * head_mask[h])
+            grad_q = part if grad_q is None else grad_q + part
+            grad_v.append(dot_nn(do_turned[h * HD : (h + 1) * HD], probs))
+            grad_k.append(dot_nn(q_turned[h * HD : (h + 1) * HD], grad_scores))
+        qkv[m, 0, :, lanes] = (grad_q * scale).astype(BF)
+        qkv[m, 1, :, lanes] = (jnp.concatenate(grad_k, axis=0).T * scale).astype(BF)
+        qkv[m, 2, :, lanes] = jnp.concatenate(grad_v, axis=0).T.astype(BF)
+        return 0
+
+    lax.fori_loop(0, MB * groups, backward_group, 0)
+
+    def qkv_grad(p, _):
+        total = dot_tn(qkv[0, p], n1[0]) + dot_tn(qkv[1, p], n1[1])
+        wslot[p, :, :, 0:80] = total.astype(BF).reshape(Z_SIZE, 2, 80, D)
+        return 0
+
+    lax.fori_loop(0, 3, qkv_grad, 0)
+
+    def first_backward(m, sums):
+        gain_sum, shift_sum = sums
+        grad = dot_nn(qkv[m, 0], wall[0:8].reshape(D, D))
+        grad = grad + dot_nn(qkv[m, 1], wall[8:16].reshape(D, D))
+        grad = grad + dot_nn(qkv[m, 2], wall[16:24].reshape(D, D))
+        normal, inv = ln_stats(ig[m])
+        ig[m] = dyv[m] + ln_backward(normal, inv, gain_one, grad)
+        return (
+            gain_sum + jnp.sum(grad * normal, axis=0, keepdims=True),
+            shift_sum + jnp.sum(grad, axis=0, keepdims=True),
+        )
+
+    gain_one_grad, shift_one_grad = lax.fori_loop(0, MB, first_backward, (zero, zero))
+
+    first_row = lax.broadcasted_iota(jnp.int32, (16, D), 0) == 0
+    for row, vec in enumerate((gain_one_grad, shift_one_grad, gain_two_grad, shift_two_grad)):
+        tile = jnp.where(first_row, jnp.broadcast_to(vec, (16, D)), 0.0).astype(BF)
+        for zz in range(Z_SIZE):
+            for kk in range(2):
+                wslot[row, zz, kk, 80:96] = tile
+
+    def cross(j):
+        return remote(wslot.at[:, zat(j), 1 - k], rc.at[j], rc_s.at[j], rc_r.at[j], dev_sib)
+
+    order = (3, 2, 1, 0)
+    for j in order:
+        cross(j).start()
+    for j in order:
+        cross(j).wait_recv()
+
+        def add_pair(rr, _):
+            mine = wslot[rr, zat(j), k].astype(F32) + rc[j, rr].astype(F32)
+            wslot[rr, zat(j), k] = mine.astype(BF)
+            return 0
+
+        lax.fori_loop(0, ROWS, add_pair, 0)
+        a_one(j)
+    for j in order:
+        a_two(j)
+    for j in (3, 2, 1):
+        a_three(j)
+    f_finish(lambda p: fgrad.at[p])
+    a_finish(lambda p: agrad.at[pl.ds(HALF_ROWS * p, HALF_ROWS)])
+
+    tok_dy().wait_send()
+    part_dn().wait_send()
+    part_y().wait_send()
+    for j in range(Z_SIZE):
+        f_drain(j)
+        a_drain(j)
+        cross(j).wait_send()
+    for j in (1, 2, 3):
+        f_drain3(j)
+        a_drain3(j)
+
+
+def run_step(x, dy, ids, wsh, fsh):
+    length = x.shape[1]
+    vm = pltpu.VMEM
+    dma = pltpu.SemaphoreType.DMA
+    idr = ids[:, :, None]
+    idc = ids[:, None, :]
+    any_spec = pl.BlockSpec(memory_space=pl.ANY)
+    vspec = pl.BlockSpec(memory_space=pltpu.VMEM)
+    fr, fc = fsh.shape[1], fsh.shape[2]
+    return pl.pallas_call(
+        step_kernel,
+        out_shape=(
+            jax.ShapeDtypeStruct((MB, length, D), F32),
+            jax.ShapeDtypeStruct((MB, length, D), F32),
+            jax.ShapeDtypeStruct((2, fr, fc), F32),
+            jax.ShapeDtypeStruct((PAD_ROWS, D), F32),
+        ),
+        in_specs=[any_spec, any_spec, vspec, vspec, vspec, vspec],
+        out_specs=(vspec, vspec, vspec, vspec),
+        scratch_shapes=[
+            vm((ROWS, Z_SIZE, 2, PAD_ROWS, D), BF),
+            vm((32, 80, D), BF),
+            vm((Z_SIZE, 2, ROWS, fr, fc), BF),
+            vm((MB, length, D), BF),
+            vm((MB, 3, length, D), BF),
+            vm((MB * H, length, length), BF),
+            vm((MB, length, D), BF),
+            vm((2 * MB, length, D), BF),
+            vm((2 * MB, length, D), BF),
+            vm((ROWS, fr, 2 * MB * length), BF),
+            vm((ROWS, fr, 2 * MB * length), BF),
+            vm((2 * MB, length, fc), BF),
+            vm((2 * MB, length, fc), BF),
+            vm((2 * MB, length, D), F32),
+            vm((2 * MB, length, D), F32),
+            vm((MB, length, D), F32),
+            vm((MB, length, D), F32),
+            vm((MB, length, D), F32),
+            vm((Z_SIZE, 2, ROWS, fr, fc), BF),
+            vm((Z_SIZE, 2, 2, fr, fc), BF),
+            vm((Z_SIZE, 2, fr, fc), BF),
+            vm((Z_SIZE - 1, 2, fr, fc), BF),
+            vm((Z_SIZE, ROWS, PAD_ROWS, D), BF),
+            vm((Z_SIZE, 2, 2, HALF_ROWS, D), BF),
+            vm((Z_SIZE, 2, HALF_ROWS, D), BF),
+            vm((Z_SIZE - 1, 2, HALF_ROWS, D), BF),
+            vm((MB, length, length), F32),
+            vm((MB, length, D), BF),
+            dma((2,)),
+            dma((5, Z_SIZE)), dma((5, Z_SIZE)),
+            dma((5, Z_SIZE)), dma((5, Z_SIZE)),
+            dma((Z_SIZE,)), dma((Z_SIZE,)),
+            dma((2,)), dma((2,)),
+            dma((2,)), dma((2,)),
+            dma((8, Z_SIZE)), dma((8, Z_SIZE)),
+            dma((8, Z_SIZE)), dma((8, Z_SIZE)),
+            dma((Z_SIZE,)), dma((Z_SIZE,)),
+        ],
+        compiler_params=pltpu.CompilerParams(
+            collective_id=0, has_side_effects=True, vmem_limit_bytes=64 * 1024 * 1024 - 4096
+        ),
+        name="encoder_step",
+    )(x, dy, idr, idc, wsh, fsh)
+
+
+def local_slice(
+    block_input, output_grad, sequence_ids,
+    attn_weights, attn_momentum, attn_average,
+    norm_params, norm_momentum, norm_average,
+    ffn_weights, ffn_momentum, ffn_average,
+):
+    width = attn_weights.shape[1]
+    shift = lax.axis_index("col") * width
+    norm_row = lax.dynamic_update_slice(
+        jnp.zeros((D,), BF), norm_params.astype(BF), (shift,)
+    )
+    wsh = jnp.concatenate(
+        [
+            attn_weights.astype(BF).T,
+            norm_row[None],
+            jnp.zeros((PAD_ROWS - width - 1, D), BF),
+        ],
+        axis=0,
+    )
+    outputs, grads, ffn_grad, shard = run_step(
+        block_input, output_grad, sequence_ids, wsh, ffn_weights.astype(BF)
+    )
+    attn_grad = shard[:width].T
+    norm_grad = lax.dynamic_slice(shard[width], (shift,), (width,))
+    total_tokens = MB * block_input.shape[1] * lax.axis_size("row") * lax.axis_size("col")
+    step_rate = RATE_SCALE * total_tokens ** (-0.5)
+    attn = sgd_update(attn_weights, attn_momentum, attn_average, attn_grad, step_rate)
+    norm = sgd_update(norm_params, norm_momentum, norm_average, norm_grad, step_rate)
+    ffn = sgd_update(ffn_weights, ffn_momentum, ffn_average, ffn_grad, step_rate)
+    return (outputs, grads, attn_grad, *attn, norm_grad, *norm, ffn_grad, *ffn)
+
+
+def local(*args):
+    ffn_block = args[9].shape
+    on_slice = (
+        lax.axis_size("row") == ROWS
+        and lax.axis_size("col") == 2 * Z_SIZE
+        and ffn_block == (2, D // ROWS, D)
+        and args[3].shape == (D, 80)
+        and args[0].shape[1] == 256
+    )
+    return (local_slice if on_slice else local_general)(*args)
+
+
 def solution(mesh):
     return jax.shard_map(
         local,

time: 642 us -> 208 us (0.32); the launches traced: 634 us -> 208 us
  waiting for transfers between devices: 305 us -> 0 us
  Pallas kernels: 0 us -> 187 us
  matrix products: 128 us -> 0 us
  blocking collectives: 81 us -> 0 us
  local copies, waits for them, and re-layouts: 62.4 us -> 8.44 us
  other arithmetic: 39.2 us -> 11.5 us
  between operations: 15.2 us -> 0.76 us
    pallas_call x0 -> x1, Pallas kernels: none -> 187 us  [run_step(): pl.pallas_call(step_kernel, out_shape=(jax.ShapeDtypeStruct((MB, length,...]
    dot_general x94 -> x0, matrix products: 128 us -> none  [the longest x8 61.2 us: matmul(): return jnp.dot(left_side, right_side, preferred_element_type=jnp.float32)]
    reduce_scatter x5 -> x0, waiting for transfers between devices: 110 us -> none  [the longest x2 74.5 us: local(): lax.psum_scatter(contract_cols(activ_low, ffn_rows[1]).astype(jnp.bfloat1...]
    all_gather x6 -> x0, waiting for transfers between devices: 105 us -> none  [the longest x2 54.2 us: local(): normed_all = lax.all_gather(normed_two_low, 'col', axis=0, tiled=True)]
    unnamed x13 -> x0, waiting for transfers between devices: 89.1 us -> none
    unnamed x2 -> x0, blocking collectives: 81 us -> none
    unnamed x123 -> x27, local copies, waits for them, and re-layouts: 25.9 us -> 4.66 us
    dynamic_slice x50 -> x0, local copies, waits for them, and re-layouts: 18.6 us -> none  [the longest x10 9.29 us: head_slices(): lax.dynamic_slice_in_dim(qkv_low, 2 * D + first_col, group_width, 1)]
  transfers between devices with their start and end apart: 12 -> 0, of which waited for: 9 -> 0; matrix products, arithmetic and copies ran while one was open for 34% -> 0% of each run, Pallas kernels for 0% -> 0%
where the time goes in v1:
time: 208 us
  Pallas kernels  187 us (90%)
  other arithmetic  11.5 us (6%)
  local copies, waits for them, and re-layouts  8.44 us (4%)
    pallas_call x1, Pallas kernels, run_step(): pl.pallas_call(step_kernel, out_shape=(jax.ShapeDtypeStruct((MB, length,...  187 us
    convert_element_type x3, other arithmetic, sgd_update(): weights_new.astype(jnp.bfloat16)  5.13 us
    unnamed x27, local copies, waits for them, and re-layouts  4.66 us

profile of v1, /device:TPU:0, one launch (start us, length us, event | category | flops | bytes accessed | tf_op | source)
XLA Modules:
  0.0 208.1 jit_solution(17830465987523199234)
XLA Ops:
  0.7 0.0 copy-start
  0.7 1.6 copy.29.idr
  2.3 1.3 broadcast_in_dim.16.idc
  3.5 0.7 convert_bitcast_fusion.1
  4.2 0.1 dynamic_update_slice.4
  4.3 0.9 convert_bitcast_fusion
  5.3 0.1 pad.2.clone
  5.3 0.7 maximum_maximum_fusion.wsh
  6.1 0.8 convert_element_type.20.fsh
  6.9 187.3 %encoder_step.1 = (f32[2,256,640]{2,1,0:T(8,128)}, f32[2,256,640]{2,1,0:T(8,128)}, f32[2,160,640]{2,1,0:T(8,128)}, f32[96,640]{1,0:T(8,128)}) custom-call(f32[2,256,640]{2,1,0:T(8,128)} %x_hbm.1, f32[2,256,640]{2,1,0:T(8,128)} %dy_hbm.1, s32[2,256,1]{2,1,0:T(8,128)} %copy.29.idr, s32[2,1,256]{2,1,0:T(1,128)} %broadcast_in_dim.16.idc, ...), custom_call_target="tpu_custom_call" | custom-call | tf_op jit(solution)/shard_map/encoder_step/pallas_call | solution.py:863
  194.2 0.0 copy-start.8
  194.2 0.0 copy-start.9
  194.3 2.1 fusion.2
  196.4 1.7 multiply_add_fusion.2
  198.1 0.7 slice.7
  198.8 0.6 fusion.1
  199.4 0.5 multiply_add_fusion.4
  199.9 2.5 %fusion = (bf16[2,160,640]{2,1,0:T(8,128)(2,1)}, f32[2,160,640]{2,1,0:T(8,128)S(1)}, f32[2,160,640]{2,1,0:T(8,128)}) fusion(f32[2,160,640]{2,1,0:T(8,128)S(1)} %copy-done.1, f32[2,160,640]{2,1,0:T(8,128)S(1)} %copy-done.2, f32[2,160,640]{2,1,0:T(8,128)} %param.22), kind=kLoop, calls=%fused_computation.14 | loop fusion | flops 1433600 | bytes 4505600 | tf_op jit(solution)/shard_map/convert_element_type | solution.py:159
  202.4 1.0 multiply_add_fusion
  203.4 0.9 copy-done.5
  204.3 1.1 copy.34
  205.4 0.7 copy-done.4
  206.1 1.1 copy.35
  207.2 0.9 copy.36
  (21 shorter events, 0.0 us)
Async XLA Ops:
  0.7 5.4 %copy-start = (f32[2,160,640]{2,1,0:T(8,128)S(1)}, f32[2,160,640]{2,1,0:T(8,128)}, u32[]{:S(2)}) copy-start(f32[2,160,640]{2,1,0:T(8,128)} %param.21) | copy-start | bytes 2457604
  194.2 4.6 %copy-start.8 = (f32[80]{0:T(128)S(1)}, f32[80]{0:T(128)}, u32[]{:S(2)}) copy-start(f32[80]{0:T(128)} %param.18) | copy-start | bytes 964
  194.2 4.6 %copy-start.9 = (f32[80]{0:T(128)S(1)}, f32[80]{0:T(128)}, u32[]{:S(2)}) copy-start(f32[80]{0:T(128)} %param.19) | copy-start | bytes 964
  194.3 5.2 %copy-start.11 = (f32[80]{0:T(128)S(1)}, f32[80]{0:T(128)}, u32[]{:S(2)}) copy-start(f32[80]{0:T(128)} %param.20) | copy-start | bytes 964
  194.3 5.7 %copy-start.1 = (f32[2,160,640]{2,1,0:T(8,128)S(1)}, f32[2,160,640]{2,1,0:T(8,128)}, u32[]{:S(2)}) copy-start(f32[2,160,640]{2,1,0:T(8,128)} %param.21) | copy-start | bytes 2457604
  194.3 5.6 %copy-start.2 = (f32[2,160,640]{2,1,0:T(8,128)S(1)}, f32[2,160,640]{2,1,0:T(8,128)}, u32[]{:S(2)}) copy-start(f32[2,160,640]{2,1,0:T(8,128)} %get-tuple-element.65) | copy-start | bytes 2457604
  196.4 6.0 %copy-start.7 = (f32[640,80]{0,1:T(8,128)}, f32[640,80]{0,1:T(8,128)S(1)}, u32[]{:S(2)}) copy-start(f32[640,80]{0,1:T(8,128)S(1)} %get-tuple-element.57) | copy-start | bytes 614404
  199.4 3.0 %copy-start.10 = (f32[80]{0:T(128)}, f32[80]{0:T(128)S(1)}, u32[]{:S(2)}) copy-start(f32[80]{0:T(128)S(1)} %get-tuple-element.62) | copy-start | bytes 964
  199.9 2.5 %copy-start.6 = (f32[2,160,640]{2,1,0:T(8,128)S(1)}, f32[2,160,640]{2,1,0:T(8,128)}, u32[]{:S(2)}) copy-start(f32[2,160,640]{2,1,0:T(8,128)} %param.23) | copy-start | bytes 2457604
  202.4 3.0 %copy-start.3 = (f32[2,160,640]{2,1,0:T(8,128)}, f32[2,160,640]{2,1,0:T(8,128)S(1)}, u32[]{:S(2)}) copy-start(f32[2,160,640]{2,1,0:T(8,128)S(1)} %get-tuple-element.67) | copy-start | bytes 2457604
  202.4 1.9 copy-start.5
  204.3 1.8 copy-start.4

commit v2 on v0

--- a/solution.py
+++ b/solution.py
@@ -1,8 +1,11 @@
+import functools
 import math
 
 import jax
 import jax.numpy as jnp
 from jax import lax
+from jax.experimental import pallas as pl
+from jax.experimental.pallas import tpu as pltpu
 from jax.sharding import PartitionSpec as P
 
 D = 640
@@ -156,7 +159,7 @@
     return (moment_new, weights_new, average_new, weights_new.astype(jnp.bfloat16))
 
 
-def local(
+def local_general(
     block_input,
     output_grad,
     sequence_ids,
@@ -281,6 +284,811 @@
     )
 
 
+MESH_ID = pl.DeviceIdType.MESH
+BF = jnp.bfloat16
+F32 = jnp.float32
+LANES = 128
+HEADS_TILE = LANES // HD
+GROUPS = D // LANES
+Z_SIZE = 4
+COLS = 2 * Z_SIZE
+ROWS = 4
+WIDTH = D // COLS
+LENGTH = 256
+FEATURES = D // ROWS
+PART_ROWS = (48, 32)
+UNITS = ((0, 512), (512, 128), (640, 640))
+CHUNKS = ((0, 512), (512, 768))
+
+
+def dot_nn(a, b):
+    return lax.dot_general(a, b, (((1,), (0,)), ((), ())), preferred_element_type=F32)
+
+
+def dot_nt(a, b):
+    return lax.dot_general(a, b, (((1,), (1,)), ((), ())), preferred_element_type=F32)
+
+
+def dot_tn(a, b):
+    return lax.dot_general(a, b, (((0,), (0,)), ((), ())), preferred_element_type=F32)
+
+
+def ln_stats(values):
+    center = values - jnp.mean(values, axis=-1, keepdims=True)
+    spread = jnp.mean(center * center, axis=-1, keepdims=True)
+    inv = lax.rsqrt(spread + EPSILON)
+    return center * inv, inv
+
+
+def ln_backward(normal, inv, gain, grad):
+    scaled = grad * gain
+    mean_one = jnp.mean(scaled, axis=-1, keepdims=True)
+    mean_two = jnp.mean(scaled * normal, axis=-1, keepdims=True)
+    return inv * (scaled - mean_one - normal * mean_two)
+
+
+def gelu_pair(u):
+    size = jnp.abs(u) * (2.0 ** -0.5)
+    t = 1.0 / (1.0 + 0.3275911 * size)
+    poly = 0.5 * 1.061405429
+    for coef in (-1.453152027, 1.421413741, -0.284496736, 0.254829592):
+        poly = poly * t + 0.5 * coef
+    bell = jnp.exp2(u * u * (-0.5 * math.log2(math.e)))
+    tail = poly * t * bell
+    cap = jnp.where(u < 0.0, tail, 1.0 - tail)
+    return u * cap, cap + u * (bell * (1.0 / math.sqrt(2.0 * math.pi)))
+
+
+def step_kernel(
+    x_hbm, dy_hbm, ffn_hbm, ids, attn_w, norm_w,
+    yout, ig, fgrad, agrad, nout, probs_hbm,
+    wall, wgrad, fw, n1, qkv, abuf, obuf, tn2, tdy, gb, dub, acc, near, stage, far, dyv,
+    fr1, fr2, fr3, rc, ar1, ar2, ar3, bias, dob, nbuf, ngrad, nsum, nr1, nr2,
+    ld_sem, pb_sem, ag_s, ag_r, fg_s, fg_r, sib_s, sib_r, tok_s, tok_r, part_s, part_r,
+    frs_s, frs_r, ars_s, ars_r, rc_s, rc_r, na_s, na_r, nb_s, nb_r,
+):
+    r = lax.axis_index("row")
+    c = lax.axis_index("col")
+    y, x, z, k = r // 2, r % 2, c // 2, c % 2
+    rx, ry, rd = y * 2 + (1 - x), (1 - y) * 2 + x, (1 - y) * 2 + (1 - x)
+    dev_x = (rx, c)
+    dev_y = (ry, c)
+    dev_d = (rd, c)
+    dev_sib = (r, z * 2 + (1 - k))
+
+    def exclusive(a, b):
+        return ((a // 2 + b // 2) % 2) * 2 + (a % 2 + b % 2) % 2
+
+    def zat(j):
+        return exclusive(z, j)
+
+    def dev_z(j):
+        return (r, zat(j) * 2 + k)
+
+    def dev_row(j):
+        return (r, zat(j // 2) * 2 + (k + j % 2) % 2)
+
+    def owner(z_rel, k_rel):
+        return ((z + z_rel) % 2) * 2 + (k + k_rel) % 2
+
+    def rows16(start, size):
+        return pl.ds(pl.multiple_of(start, 16), size)
+
+    def remote(src, dst, ss, rs, dev):
+        return pltpu.make_async_remote_copy(
+            src_ref=src, dst_ref=dst, send_sem=ss, recv_sem=rs, device_id=dev, device_id_type=MESH_ID
+        )
+
+    barrier = pltpu.get_barrier_semaphore()
+    for dev in (dev_x, dev_y, dev_d, *[dev_row(j) for j in range(1, COLS)]):
+        pl.semaphore_signal(barrier, inc=1, device_id=dev, device_id_type=MESH_ID)
+
+    ld_f = [pltpu.make_async_copy(ffn_hbm.at[s], acc.at[0, s, pl.ds(0, FEATURES)], ld_sem.at[2 + s]) for s in range(2)]
+    ld_x = pltpu.make_async_copy(x_hbm, ig, ld_sem.at[0])
+    ld_y = pltpu.make_async_copy(dy_hbm, dyv, ld_sem.at[1])
+    for s in range(2):
+        ld_f[s].start()
+    ld_y.start()
+    ld_x.start()
+
+    wall[r, rows16(c * WIDTH, WIDTH)] = attn_w[...].T.astype(BF)
+    nbuf[r, c] = jnp.zeros((1, LANES), F32)
+    nbuf[r, c, :, 0:WIDTH] = norm_w[...].astype(BF).astype(F32)
+    pl.semaphore_wait(barrier, COLS + 2)
+
+    def norm_one(j):
+        return remote(nbuf.at[r, c], nbuf.at[r, c], na_s.at[j], na_r.at[j], dev_row(j))
+
+    def norm_two(i):
+        return remote(nbuf.at[r], nbuf.at[r], na_s.at[COLS + i], na_r.at[COLS + i], (dev_x, dev_y, dev_d)[i])
+
+    def a_rows(j, p):
+        start = (zat(j) * 2 + k) * WIDTH
+        if p is None:
+            return rows16(start, WIDTH)
+        return rows16(start + PART_ROWS[0] * p, PART_ROWS[p])
+
+    def gather_ops(piece, part, far_piece, far_dev, ss, rs):
+        def cz(j):
+            return remote(piece(r, 0), far_piece(j), ss.at[0, j], rs.at[0, j], far_dev(j))
+
+        def cx(j):
+            return remote(piece(r, j), piece(r, j), ss.at[1, j], rs.at[1, j], dev_x)
+
+        def cy(j):
+            return remote(piece(r, j), piece(r, j), ss.at[2, j], rs.at[2, j], dev_y)
+
+        def cd0(j):
+            return remote(part(rx, j, 0), part(rx, j, 0), ss.at[3, j], rs.at[3, j], dev_y)
+
+        def cd1(j):
+            return remote(part(ry, j, 1), part(ry, j, 1), ss.at[4, j], rs.at[4, j], dev_x)
+
+        return cz, cx, cy, cd0, cd1
+
+    az, ax, ay, ad0, ad1 = gather_ops(
+        lambda rr, j: wall.at[rr, a_rows(j, None)],
+        lambda rr, j, p: wall.at[rr, a_rows(j, p)],
+        lambda j: wall.at[r, a_rows(0, None)],
+        dev_z, ag_s, ag_r,
+    )
+    fz, fx, fy, fd0, fd1 = gather_ops(
+        lambda rr, i: fw.at[:, rr, :, pl.ds(i * D, D)],
+        lambda rr, i, p: fw.at[p, rr, :, pl.ds(i * D, D)],
+        lambda i: fw.at[:, r, :, pl.ds(D, D)],
+        lambda i: dev_z(2), fg_s, fg_r,
+    )
+
+    def sib(j):
+        ref = wall.at[:, a_rows(j, None)]
+        return remote(ref, ref, sib_s.at[j], sib_r.at[j], dev_sib)
+
+    for j in (1, 2, 3):
+        az(j).start()
+    ax(0).start()
+    ay(0).start()
+    for j in range(1, COLS):
+        norm_one(j).start()
+
+    for s in range(2):
+        ld_f[s].wait()
+        fw[s, r, :, 0:D] = acc[0, s, 0:FEATURES].astype(BF)
+    ld_y.wait()
+
+    def make_bias(m, _):
+        across = jnp.broadcast_to(ids[pl.ds(m, 1)].astype(F32), (LENGTH, LENGTH))
+        bias[m] = jnp.where(across == across.T, 0.0, MASKED)
+        tdy[owner(0, 0), pl.ds(m * LENGTH, LENGTH)] = dyv[m].astype(BF)
+        return 0
+
+    lax.fori_loop(0, MB, make_bias, 0)
+
+    def tok_copy(q, n, m, dev, whose):
+        ref = (tdy, tn2)[q].at[whose, pl.ds(m * LENGTH, LENGTH)]
+        return remote(ref, ref, tok_s.at[q, n, m], tok_r.at[q, n, m], dev)
+
+    def tok_sib(q, m):
+        return tok_copy(q, 0, m, dev_sib, owner(0, 0))
+
+    def tok_far(q, m):
+        return tok_copy(q, 1, m, dev_z(1), owner(0, 0))
+
+    def tok_fwd(q, m):
+        return tok_copy(q, 2, m, dev_sib, owner(1, 0))
+
+    for m in range(MB):
+        tok_sib(0, m).start()
+
+    for j in range(1, COLS):
+        norm_one(j).wait_recv()
+    for i in range(3):
+        norm_two(i).start()
+    ax(0).wait_recv()
+    ad0(0).start()
+    ay(0).wait_recv()
+    ad1(0).start()
+    for j in (1, 2, 3):
+        az(j).wait_recv()
+        ax(j).start()
+        ay(j).start()
+    fz(1).start()
+    for m in range(MB):
+        tok_far(0, m).start()
+    for j in (1, 2, 3):
+        ax(j).wait_recv()
+        ad0(j).start()
+        ay(j).wait_recv()
+        ad1(j).start()
+    fx(0).start()
+    fy(0).start()
+    for i in range(3):
+        norm_two(i).wait_recv()
+
+    vectors = None
+    for cc in range(COLS):
+        shard = jnp.concatenate([nbuf[:, cc, 0, :], jnp.zeros((ROWS, D - LANES), F32)], axis=1)
+        shard = pltpu.roll(shard, cc * WIDTH, 1) if cc else shard
+        vectors = shard if vectors is None else vectors + shard
+    gain_one, shift_one, gain_two, shift_two = [vectors[i : i + 1] for i in range(4)]
+
+    ld_x.wait()
+
+    def first_norm(m, _):
+        normal, _inv = ln_stats(ig[m])
+        n1[m] = (normal * gain_one + shift_one).astype(BF)
+        return 0
+
+    lax.fori_loop(0, MB, first_norm, 0)
+
+    for j in range(Z_SIZE):
+        ad0(j).wait_recv()
+        ad1(j).wait_recv()
+        sib(j).start()
+    for j in range(Z_SIZE):
+        sib(j).wait_recv()
+
+    def project(i, _):
+        m, p = i // 3, i % 3
+        qkv[m, p] = dot_nt(n1[m], wall[p]).astype(BF)
+        return 0
+
+    lax.fori_loop(0, 3 * MB, project, 0)
+
+    lane_head = lax.broadcasted_iota(jnp.int32, (1, LANES), 1) // HD
+    head_mask = [jnp.where(lane_head == h, 1.0, 0.0).astype(BF) for h in range(HEADS_TILE)]
+    scale = HD ** (-0.5)
+    log2_scale = scale * math.log2(math.e)
+
+    def at_step(it, i, fn):
+        @pl.when(it == i)
+        def _():
+            fn()
+
+    def gather_xy(j):
+        fz(j).wait_recv()
+        fx(j).start()
+        fy(j).start()
+
+    def gather_diag(j):
+        fx(j).wait_recv()
+        fd0(j).start()
+        fy(j).wait_recv()
+        fd1(j).start()
+
+    def save_probs(it):
+        return pltpu.make_async_copy(abuf.at[it % 2], probs_hbm.at[it], pb_sem.at[it % 2])
+
+    def load_probs(it, where):
+        return pltpu.make_async_copy(probs_hbm.at[where], abuf.at[it % 2], pb_sem.at[2 + it % 2])
+
+    def second_norm(m):
+        hidden = ig[m] + dot_nt(obuf[m], wall[3])
+        yout[m] = hidden
+        normal, _inv = ln_stats(hidden)
+        tn2[owner(0, 0), pl.ds(m * LENGTH, LENGTH)] = (normal * gain_two + shift_two).astype(BF)
+        tok_far(1, m).start()
+        tok_sib(1, m).start()
+
+    def forward_group(it, _):
+        m, g = it // GROUPS, it % GROUPS
+        at_step(it, 5, lambda: gather_diag(0))
+        at_step(it, 9, lambda: gather_xy(1))
+        slot = it % 2
+
+        @pl.when(it >= 2)
+        def _():
+            save_probs(it - 2).wait()
+
+        lanes = pl.ds(pl.multiple_of(g * LANES, LANES), LANES)
+        q = qkv[m, 0, :, lanes]
+        kk = qkv[m, 1, :, lanes]
+        v = qkv[m, 2, :, lanes]
+        mask_bias = bias[m]
+        mixed = None
+        for h in range(HEADS_TILE):
+            scores = dot_nt(q * head_mask[h], kk) * log2_scale + mask_bias
+            row_max = jnp.max(scores, axis=-1, keepdims=True)
+            expo = jnp.exp2(scores - row_max)
+            total = jnp.sum(expo, axis=-1, keepdims=True)
+            probs = (expo * (1.0 / total)).astype(BF)
+            abuf[slot, h] = probs
+            part = dot_nn(probs, v * head_mask[h])
+            mixed = part if mixed is None else mixed + part
+        obuf[m, :, lanes] = mixed.astype(BF)
+        save_probs(it).start()
+
+        @pl.when(g == GROUPS - 1)
+        def _():
+            second_norm(m)
+
+        return 0
+
+    lax.fori_loop(0, MB * GROUPS, forward_group, 0)
+    save_probs(MB * GROUPS - 2).wait()
+    save_probs(MB * GROUPS - 1).wait()
+    for m in range(MB):
+        tok_far(0, m).wait_recv()
+        tok_fwd(0, m).start()
+
+    def scatter_ops(block, r1, r2, ss, rs):
+        def one(u, p, b):
+            dev = dev_y if p == 0 else dev_x
+            rr = rd if b == 1 else (ry if p == 0 else rx)
+            return remote(block(rr, u, p), r1(u, p, b), ss.at[2 * p + b, u], rs.at[2 * p + b, u], dev)
+
+        def two(u, p):
+            dev = dev_x if p == 0 else dev_y
+            rr = rx if p == 0 else ry
+            return remote(block(rr, u, p), r2(u, p), ss.at[4 + p, u], rs.at[4 + p, u], dev)
+
+        def start_one(u):
+            for p in range(2):
+                for b in (1, 0):
+                    one(u, p, b).start()
+
+        def start_two(u):
+            for p in range(2):
+                one(u, p, 0).wait_recv()
+                one(u, p, 1).wait_recv()
+                mine = block(rx if p == 0 else ry, u, p)
+                mine[...] = (mine[...].astype(F32) + r1(u, p, 1)[...].astype(F32)).astype(BF)
+                two(u, p).start()
+
+        def own_sum(u, p):
+            two(u, p).wait_recv()
+            return (
+                block(r, u, p)[...].astype(F32)
+                + r1(u, p, 0)[...].astype(F32)
+                + r2(u, p)[...].astype(F32)
+            )
+
+        def drain(u):
+            for p in range(2):
+                one(u, p, 0).wait_send()
+                one(u, p, 1).wait_send()
+                two(u, p).wait_send()
+
+        return start_one, start_two, own_sum, drain
+
+    def unit_lanes(u):
+        return pl.ds(UNITS[u][0], UNITS[u][1])
+
+    f_one, f_two, f_sum, f_drain = scatter_ops(
+        lambda rr, u, p: fw.at[p, rr, :, unit_lanes(u)],
+        lambda u, p, b: fr1.at[p, b, :, unit_lanes(u)],
+        lambda u, p: fr2.at[p, :, unit_lanes(u)],
+        frs_s, frs_r,
+    )
+
+    def f_far(p):
+        return remote(fw.at[p, r, :, unit_lanes(2)], fr3.at[p], frs_s.at[6 + p, 2], frs_r.at[6 + p, 2], dev_z(2))
+
+    def f_three():
+        for p in range(2):
+            fw[p, r, :, unit_lanes(2)] = f_sum(2, p).astype(BF)
+            f_far(p).start()
+
+    def g_rows(zz, p, parity):
+        start = (zz * 2 + parity) * WIDTH
+        if p is None:
+            return rows16(start, WIDTH)
+        return rows16(start + PART_ROWS[0] * p, PART_ROWS[p])
+
+    def part_rows(p):
+        return pl.ds(PART_ROWS[0] * p, PART_ROWS[p])
+
+    a_one, a_two, a_sum, a_drain = scatter_ops(
+        lambda rr, zz, p: wgrad.at[rr, g_rows(zz, p, k)],
+        lambda zz, p, b: ar1.at[zz, b, part_rows(p)],
+        lambda zz, p: ar2.at[zz, part_rows(p)],
+        ars_s, ars_r,
+    )
+
+    def a_far(zz, j):
+        return remote(wgrad.at[r, g_rows(zz, None, k)], ar3.at[j - 1], ars_s.at[6, j], ars_r.at[6, j], (r, zz * 2 + k))
+
+    def a_three(zz):
+        total = [a_sum(zz, p) for p in range(2)]
+
+        @pl.when(z == zz)
+        def _():
+            for p in range(2):
+                agrad[part_rows(p)] = total[p]
+
+        @pl.when(z != zz)
+        def _():
+            for p in range(2):
+                wgrad[r, g_rows(zz, p, k)] = total[p].astype(BF)
+            a_far(zz, exclusive(z, zz)).start()
+
+    def cross(zz):
+        return remote(wgrad.at[:, g_rows(zz, None, 1 - k)], rc.at[zz], rc_s.at[zz], rc_r.at[zz], dev_sib)
+
+    def a_start(zz):
+        cross(zz).wait_recv()
+        for rr in range(ROWS):
+            mine = wgrad.at[rr, g_rows(zz, None, k)]
+            mine[...] = (mine[...].astype(F32) + rc[zz, rr].astype(F32)).astype(BF)
+        a_one(zz)
+
+    def ffn_tile(i, t):
+        first, width = CHUNKS[i]
+        up = fw[0, :, :, first : first + width].reshape(D, width)
+        down = fw[1, :, :, first : first + width].reshape(D, width)
+        act, slope = gelu_pair(dot_nn(tn2[t], up))
+        grad_act = dot_nn(tdy[t], down)
+        act = act.astype(BF)
+        grad_up = (grad_act * slope).astype(BF)
+        gb[t, :, 0:width] = act
+        dub[t, :, 0:width] = grad_up
+        dn_part = dot_nt(grad_up, up)
+        y_part = dot_nt(act, down)
+        if i == 0:
+            acc[0, t] = dn_part
+            acc[1, t] = y_part
+        else:
+            acc[0, t] += dn_part
+            acc[1, t] += y_part
+
+    def weight_grads(i):
+        first, width = CHUNKS[i]
+        for p, (left, right) in enumerate(((tn2, dub), (tdy, gb))):
+            grad = dot_tn(left[...].reshape(4 * MB * LENGTH, D), right[:, :, 0:width].reshape(4 * MB * LENGTH, width))
+            fw[p, :, :, first : first + width] = grad.astype(BF).reshape(ROWS, FEATURES, width)
+
+    fd0(0).wait_recv()
+    fd1(0).wait_recv()
+
+    def first_block(s, _):
+        def sib_tiles():
+            for q in range(2):
+                for m in range(MB):
+                    tok_sib(q, m).wait_recv()
+
+        def far_tiles():
+            for m in range(MB):
+                tok_far(1, m).wait_recv()
+                tok_fwd(1, m).start()
+
+        def fwd_tiles():
+            for q in range(2):
+                for m in range(MB):
+                    tok_fwd(q, m).wait_recv()
+
+        at_step(s, 1, sib_tiles)
+        at_step(s, 2, far_tiles)
+        at_step(s, 3, fwd_tiles)
+        at_step(s, 3, lambda: gather_diag(1))
+        ffn_tile(0, owner(s // 2, s % 2))
+        return 0
+
+    lax.fori_loop(0, 4, first_block, 0)
+    fz(1).wait_send()
+    for op in (fx, fy, fd0, fd1):
+        op(0).wait_send()
+    weight_grads(0)
+    f_one(0)
+    fd0(1).wait_recv()
+    fd1(1).wait_recv()
+
+    def part_sib(q, n):
+        return remote(acc.at[q, owner(n, 1)], near.at[q, n], part_s.at[q, n], part_r.at[q, n], dev_sib)
+
+    def part_far(q, m):
+        return remote(stage.at[q, m], far.at[q, m], part_s.at[q, 2 + m], part_r.at[q, 2 + m], dev_z(1))
+
+    def to_far(q):
+        part_sib(q, 1).wait_recv()
+        for m in range(MB):
+            rows = pl.ds(m * LENGTH, LENGTH)
+            stage[q, m] = (acc[q, owner(1, 0), rows] + near[q, 1, rows]).astype(BF)
+            part_far(q, m).start()
+
+    def second_block(s, _):
+        ffn_tile(1, owner(1 - s // 2, 1 - s % 2))
+        for n in range(2):
+
+            def to_sib(n=n):
+                part_sib(0, n).start()
+                part_sib(1, n).start()
+
+            at_step(s, 2 * (1 - n), to_sib)
+        at_step(s, 1, lambda: to_far(0))
+        at_step(s, 2, lambda: f_two(0))
+        at_step(s, 3, lambda: to_far(1))
+        return 0
+
+    lax.fori_loop(0, 4, second_block, 0)
+    for op in (fx, fy, fd0, fd1):
+        op(1).wait_send()
+    weight_grads(1)
+    f_one(2)
+    f_one(1)
+
+    zero = jnp.zeros((1, D), F32)
+    for m in range(MB):
+        tok_far(1, m).wait_send()
+        tok_sib(1, m).wait_send()
+    part_sib(0, 0).wait_recv()
+
+    def whole(q, m):
+        rows = pl.ds(m * LENGTH, LENGTH)
+        return acc[q, owner(0, 0), rows] + near[q, 0, rows] + far[q, m].astype(F32)
+
+    def second_backward(m):
+        part_far(0, m).wait_recv()
+        normal, inv = ln_stats(yout[m])
+        grad = whole(0, m)
+        grad_hidden = dyv[m] + ln_backward(normal, inv, gain_two, grad)
+        dyv[m] = grad_hidden
+        low = grad_hidden.astype(BF)
+        dob[m] = dot_nn(low, wall[3]).astype(BF)
+        tn2[owner(0, 0), pl.ds(m * LENGTH, LENGTH)] = low
+        nsum[pl.ds(2, 1)] += jnp.sum(grad * normal, axis=0, keepdims=True)
+        nsum[pl.ds(3, 1)] += jnp.sum(grad, axis=0, keepdims=True)
+
+    nsum[...] = jnp.zeros(nsum.shape, F32)
+    load_probs(0, 0).start()
+    second_backward(0)
+
+    def backward_at(it):
+        m = jnp.where(it < 6, it // 3, it % 2)
+        g = jnp.where(it < 6, it % 3, it // 2)
+        return m, g
+
+    def group_grads(g):
+        lanes = pl.ds(pl.multiple_of(g * LANES, LANES), LANES)
+        for p in range(3):
+            grad = dot_tn(qkv[0, p, :, lanes], n1[0]) + dot_tn(qkv[1, p, :, lanes], n1[1])
+            wgrad[p, lanes] = grad.astype(BF)
+
+    def backward_group(it, _):
+        m, g = backward_at(it)
+
+        @pl.when(it == 3)
+        def _():
+            second_backward(1)
+            rows = [tn2[owner(0, 0), pl.ds(i * LENGTH, LENGTH)] for i in range(MB)]
+            wgrad[3] = (dot_tn(rows[0], obuf[0]) + dot_tn(rows[1], obuf[1])).astype(BF)
+
+        at_step(it, 5, lambda: f_two(2))
+        at_step(it, 6, lambda: f_two(1))
+        at_step(it, 6, lambda: a_start(0))
+        at_step(it, 7, lambda: a_start(1))
+        at_step(it, 8, lambda: a_two(0))
+        at_step(it, 9, lambda: a_two(1))
+        at_step(it, 9, lambda: a_start(2))
+        at_step(it, 9, f_three)
+        slot = it % 2
+
+        @pl.when(it + 1 < MB * GROUPS)
+        def _():
+            m_next, g_next = backward_at(it + 1)
+            load_probs(it + 1, m_next * GROUPS + g_next).start()
+
+        load_probs(it, m * GROUPS + g).wait()
+        lanes = pl.ds(pl.multiple_of(g * LANES, LANES), LANES)
+        q = qkv[m, 0, :, lanes]
+        kk = qkv[m, 1, :, lanes]
+        v = qkv[m, 2, :, lanes]
+        do = dob[m, :, lanes]
+        q_turned = q.T
+        do_turned = do.T
+        grad_q = None
+        grad_k = []
+        grad_v = []
+        for h in range(HEADS_TILE):
+            probs = abuf[slot, h]
+            wide = probs.astype(F32)
+            grad_probs = dot_nt(do * head_mask[h], v)
+            product = grad_probs * wide
+            row = jnp.sum(product, axis=-1, keepdims=True)
+            grad_scores = (product - wide * row).astype(BF)
+            part = dot_nn(grad_scores, kk * head_mask[h])
+            grad_q = part if grad_q is None else grad_q + part
+            grad_v.append(dot_nn(do_turned[h * HD : (h + 1) * HD], probs))
+            grad_k.append(dot_nn(q_turned[h * HD : (h + 1) * HD], grad_scores))
+        qkv[m, 0, :, lanes] = (grad_q * scale).astype(BF)
+        qkv[m, 1, :, lanes] = (jnp.concatenate(grad_k, axis=0).T * scale).astype(BF)
+        qkv[m, 2, :, lanes] = jnp.concatenate(grad_v, axis=0).T.astype(BF)
+
+        @pl.when(m == 1)
+        def _():
+            group_grads(g)
+
+        at_step(it, 4, lambda: cross(0).start())
+        at_step(it, 5, lambda: cross(1).start())
+        at_step(it, 7, lambda: cross(2).start())
+        at_step(it, 9, lambda: cross(3).start())
+        return 0
+
+    lax.fori_loop(0, MB * GROUPS, backward_group, 0)
+
+    def first_backward(m):
+        grad = dot_nn(qkv[m, 0], wall[0]) + dot_nn(qkv[m, 1], wall[1]) + dot_nn(qkv[m, 2], wall[2])
+        normal, inv = ln_stats(ig[m])
+        ig[m] = dyv[m] + ln_backward(normal, inv, gain_one, grad)
+        nsum[pl.ds(0, 1)] += jnp.sum(grad * normal, axis=0, keepdims=True)
+        nsum[pl.ds(1, 1)] += jnp.sum(grad, axis=0, keepdims=True)
+
+    a_three(0)
+    a_start(3)
+    first_backward(0)
+    a_two(2)
+    first_backward(1)
+
+    sums = nsum[...]
+    lane_own = lax.broadcasted_iota(jnp.int32, (8, LANES), 1) < WIDTH
+    for cc in range(COLS):
+        shard = pltpu.roll(sums, D - cc * WIDTH, 1) if cc else sums
+        shard = jnp.where(lane_own, shard[:, 0:LANES], 0.0)
+        for rr in range(ROWS):
+            ngrad[rr, cc] = shard[rr : rr + 1]
+
+    def grad_rows(i):
+        rr = (rx, ry, rd)[i]
+        return remote(ngrad.at[rr], nr1.at[i], nb_s.at[i], nb_r.at[i], (dev_x, dev_y, dev_d)[i])
+
+    def grad_cols(j):
+        col = zat(j // 2) * 2 + (k + j % 2) % 2
+        return remote(ngrad.at[r, col], nr2.at[j - 1], nb_s.at[2 + j], nb_r.at[2 + j], dev_row(j))
+
+    for i in range(3):
+        grad_rows(i).start()
+    a_three(1)
+    a_two(3)
+    a_three(2)
+    for i in range(3):
+        grad_rows(i).wait_recv()
+    ngrad[r] = ngrad[r] + nr1[0] + nr1[1] + nr1[2]
+    for j in range(1, COLS):
+        grad_cols(j).start()
+
+    part_sib(1, 0).wait_recv()
+    for m in range(MB):
+        part_far(1, m).wait_recv()
+        yout[m] = yout[m] + whole(1, m)
+
+    a_three(3)
+    for p in range(2):
+        for u in range(2):
+            total = f_sum(u, p)
+            if u == 0:
+                f_far(p).wait_recv()
+            fgrad[p, :, unit_lanes(u)] = total + fr3[p, :, unit_lanes(u)].astype(F32)
+    total = ngrad[r, c]
+    for j in range(1, COLS):
+        grad_cols(j).wait_recv()
+        total = total + nr2[j - 1]
+    nout[...] = total
+    for j in (1, 2, 3):
+        a_far(z, j).wait_recv()
+    agrad[...] = agrad[...] + ar3[0].astype(F32) + ar3[1].astype(F32) + ar3[2].astype(F32)
+
+    for j in (1, 2, 3):
+        az(j).wait_send()
+        a_far(z, j).wait_send()
+    for j in range(Z_SIZE):
+        for op in (ax, ay, ad0, ad1, sib, cross):
+            op(j).wait_send()
+        a_drain(j)
+    for u in range(3):
+        f_drain(u)
+    for p in range(2):
+        f_far(p).wait_send()
+    for m in range(MB):
+        tok_sib(0, m).wait_send()
+        tok_far(0, m).wait_send()
+        for q in range(2):
+            tok_fwd(q, m).wait_send()
+            part_far(q, m).wait_send()
+            part_sib(q, m).wait_send()
+    for j in range(1, COLS):
+        norm_one(j).wait_send()
+        grad_cols(j).wait_send()
+    for i in range(3):
+        norm_two(i).wait_send()
+        grad_rows(i).wait_send()
+
+
+def run_step(x, dy, ids, attn_w, norm_w, ffn_w):
+    vm = pltpu.VMEM
+    dma = pltpu.SemaphoreType.DMA
+    any_spec = pl.BlockSpec(memory_space=pl.ANY)
+    vspec = pl.BlockSpec(memory_space=pltpu.VMEM)
+    tokens = MB * LENGTH
+    return pl.pallas_call(
+        step_kernel,
+        out_shape=(
+            jax.ShapeDtypeStruct((MB, LENGTH, D), F32),
+            jax.ShapeDtypeStruct((MB, LENGTH, D), F32),
+            jax.ShapeDtypeStruct((2, FEATURES, D), F32),
+            jax.ShapeDtypeStruct((WIDTH, D), F32),
+            jax.ShapeDtypeStruct((1, LANES), F32),
+            jax.ShapeDtypeStruct((MB * GROUPS, HEADS_TILE, LENGTH, LENGTH), BF),
+        ),
+        in_specs=[any_spec, any_spec, any_spec, vspec, vspec, vspec],
+        out_specs=(vspec, vspec, vspec, vspec, vspec, any_spec),
+        scratch_shapes=[
+            vm((ROWS, D, D), BF),
+            vm((ROWS, D, D), BF),
+            vm((2, ROWS, FEATURES, 2 * D), BF),
+            vm((MB, LENGTH, D), BF),
+            vm((MB, 3, LENGTH, D), BF),
+            vm((2, HEADS_TILE, LENGTH, LENGTH), BF),
+            vm((MB, LENGTH, D), BF),
+            vm((4, tokens, D), BF),
+            vm((4, tokens, D), BF),
+            vm((4, tokens, CHUNKS[1][1]), BF),
+            vm((4, tokens, CHUNKS[1][1]), BF),
+            vm((2, 4, tokens, D), F32),
+            vm((2, 2, tokens, D), F32),
+            vm((2, MB, LENGTH, D), BF),
+            vm((2, MB, LENGTH, D), BF),
+            vm((MB, LENGTH, D), F32),
+            vm((2, 2, FEATURES, 2 * D), BF),
+            vm((2, FEATURES, 2 * D), BF),
+            vm((2, FEATURES, D), BF),
+            vm((Z_SIZE, ROWS, WIDTH, D), BF),
+            vm((Z_SIZE, 2, WIDTH, D), BF),
+            vm((Z_SIZE, WIDTH, D), BF),
+            vm((Z_SIZE - 1, WIDTH, D), BF),
+            vm((MB, LENGTH, LENGTH), F32),
+            vm((MB, LENGTH, D), BF),
+            vm((ROWS, COLS, 1, LANES), F32),
+            vm((ROWS, COLS, 1, LANES), F32),
+            vm((8, D), F32),
+            vm((3, COLS, 1, LANES), F32),
+            vm((COLS - 1, 1, LANES), F32),
+            dma((4,)), dma((4,)),
+            dma((5, Z_SIZE)), dma((5, Z_SIZE)),
+            dma((5, 2)), dma((5, 2)),
+            dma((Z_SIZE,)), dma((Z_SIZE,)),
+            dma((2, 3, MB)), dma((2, 3, MB)),
+            dma((2, 4)), dma((2, 4)),
+            dma((8, 3)), dma((8, 3)),
+            dma((7, Z_SIZE)), dma((7, Z_SIZE)),
+            dma((Z_SIZE,)), dma((Z_SIZE,)),
+            dma((COLS + 3,)), dma((COLS + 3,)),
+            dma((COLS + 2,)), dma((COLS + 2,)),
+        ],
+        compiler_params=pltpu.CompilerParams(
+            collective_id=0, has_side_effects=True, vmem_limit_bytes=64 * 1024 * 1024 - 4096
+        ),
+        name="encoder_step",
+    )(x, dy, ffn_w, ids, attn_w, norm_w)
+
+
+def local_slice(
+    block_input, output_grad, sequence_ids,
+    attn_weights, attn_momentum, attn_average,
+    norm_params, norm_momentum, norm_average,
+    ffn_weights, ffn_momentum, ffn_average,
+):
+    outputs, grads, ffn_grad, shard, norm_shard, _probs = run_step(
+        block_input, output_grad, sequence_ids, attn_weights, norm_params[None], ffn_weights
+    )
+    attn_grad = shard.T
+    norm_grad = norm_shard[0, :WIDTH]
+    total_tokens = MB * block_input.shape[1] * lax.axis_size("row") * lax.axis_size("col")
+    step_rate = RATE_SCALE * total_tokens ** (-0.5)
+    attn = sgd_update(attn_weights, attn_momentum, attn_average, attn_grad, step_rate)
+    norm = sgd_update(norm_params, norm_momentum, norm_average, norm_grad, step_rate)
+    ffn = sgd_update(ffn_weights, ffn_momentum, ffn_average, ffn_grad, step_rate)
+    return (outputs, grads, attn_grad, *attn, norm_grad, *norm, ffn_grad, *ffn)
+
+
+def local(*args):
+    on_slice = (
+        lax.axis_size("row") == ROWS
+        and lax.axis_size("col") == COLS
+        and args[0].shape[1] == LENGTH
+        and args[3].shape == (D, WIDTH)
+        and args[9].shape == (2, FEATURES, D)
+    )
+    return (local_slice if on_slice else local_general)(*args)
+
+
 def solution(mesh):
     return jax.shard_map(
         local,

time: 642 us -> 156 us (0.24); the launches traced: 634 us -> 156 us
  waiting for transfers between devices: 305 us -> 0 us
  Pallas kernels: 0 us -> 138 us
  matrix products: 128 us -> 0 us
  blocking collectives: 81 us -> 0 us
  local copies, waits for them, and re-layouts: 62.4 us -> 7.2 us
  other arithmetic: 39.2 us -> 9.6 us
  between operations: 15.2 us -> 0.71 us
    pallas_call x0 -> x1, Pallas kernels: none -> 138 us  [run_step(): pl.pallas_call(step_kernel, out_shape=(jax.ShapeDtypeStruct((MB, LENGTH,...]
    dot_general x94 -> x0, matrix products: 128 us -> none  [the longest x8 61.2 us: matmul(): return jnp.dot(left_side, right_side, preferred_element_type=jnp.float32)]
    reduce_scatter x5 -> x0, waiting for transfers between devices: 110 us -> none  [the longest x2 74.5 us: local(): lax.psum_scatter(contract_cols(activ_low, ffn_rows[1]).astype(jnp.bfloat1...]
    all_gather x6 -> x0, waiting for transfers between devices: 105 us -> none  [the longest x2 54.2 us: local(): normed_all = lax.all_gather(normed_two_low, 'col', axis=0, tiled=True)]
    unnamed x13 -> x0, waiting for transfers between devices: 89.1 us -> none
    unnamed x2 -> x0, blocking collectives: 81 us -> none
    unnamed x123 -> x23, local copies, waits for them, and re-layouts: 25.9 us -> 7.2 us
    dynamic_slice x50 -> x0, local copies, waits for them, and re-layouts: 18.6 us -> none  [the longest x10 9.29 us: head_slices(): lax.dynamic_slice_in_dim(qkv_low, 2 * D + first_col, group_width, 1)]
  transfers between devices with their start and end apart: 12 -> 0, of which waited for: 9 -> 0; matrix products, arithmetic and copies ran while one was open for 34% -> 0% of each run, Pallas kernels for 0% -> 0%
where the time goes in v2:
time: 156 us
  Pallas kernels  138 us (88%)
  other arithmetic  9.6 us (6%)
  local copies, waits for them, and re-layouts  7.2 us (5%)
    pallas_call x1, Pallas kernels, run_step(): pl.pallas_call(step_kernel, out_shape=(jax.ShapeDtypeStruct((MB, LENGTH,...  138 us
    unnamed x23, local copies, waits for them, and re-layouts  7.2 us
    convert_element_type x3, other arithmetic, sgd_update(): weights_new.astype(jnp.bfloat16)  5.7 us
    add x3, other arithmetic, sgd_update(): average_new = AVERAGE_DECAY * average + (1.0 - AVERAGE_DECAY) * weights_new  3.91 us

profile of v2, /device:TPU:0, one launch (start us, length us, event | category | flops | bytes accessed | tf_op | source)
XLA Modules:
  0.0 155.7 jit_solution(9980557644260118405)
XLA Ops:
  0.7 1.8 %copy.29.attn_w = f32[640,80]{1,0:T(8,128)} copy(f32[640,80]{0,1:T(8,128)} %param.15) | data formatting | bytes 409600 | tf_op args[3]
  2.5 138.2 %encoder_step.1 = (f32[2,256,640]{2,1,0:T(8,128)}, f32[2,256,640]{2,1,0:T(8,128)}, f32[2,160,640]{2,1,0:T(8,128)}, f32[80,640]{1,0:T(8,128)}, f32[1,128]{1,0:T(1,128)}, /*index=5*/bf16[10,4,256,256]{3,2,1,0:T(8,128)(2,1)}) custom-call(f32[2,256,640]{2,1,0:T(8,128)} %x_hbm.1, f32[2,256,640]{2,1,0:T(8,128)} %dy_hbm.1, f32[2,160,640]{2,1,0:T(8,128)} %ffn_hbm.1, ...), custom_call_target="tpu_custom_call" | custom-call | tf_op jit(solution)/shard_map/encoder_step/pallas_call | solution.py:1000
  140.6 0.0 copy-start
  140.7 0.0 copy-start.2
  140.7 1.3 fusion.1
  142.0 1.2 multiply_add_fusion.4
  143.2 1.9 %fusion.2 = (bf16[640,80]{0,1:T(8,128)(2,1)}, f32[640,80]{0,1:T(8,128)S(1)}, f32[640,80]{0,1:T(8,128)}) fusion(f32[640,80]{0,1:T(8,128)} %param.15, f32[640,80]{0,1:T(8,128)} %param.16, f32[80,640]{1,0:T(8,128)} %get-tuple-element.24), kind=kLoop, calls=%fused_computation.12 | loop fusion | flops 358400 | bytes 1126400 | tf_op jit(solution)/shard_map/convert_element_type | solution.py:159
  145.1 1.7 %multiply_add_fusion.2 = f32[640,80]{0,1:T(8,128)} fusion(f32[640,80]{0,1:T(8,128)S(1)} %get-tuple-element.58, f32[640,80]{0,1:T(8,128)} %param.17), kind=kLoop, calls=%fused_computation.3 | loop fusion | flops 153600 | bytes 614400 | tf_op jit(solution)/shard_map/add | solution.py:158
  146.8 0.0 copy-done
  146.8 0.0 copy-done.2
  146.8 2.5 %fusion = (bf16[2,160,640]{2,1,0:T(8,128)(2,1)}, f32[2,160,640]{2,1,0:T(8,128)S(1)}, f32[2,160,640]{2,1,0:T(8,128)}) fusion(f32[2,160,640]{2,1,0:T(8,128)S(1)} %copy-done, f32[2,160,640]{2,1,0:T(8,128)S(1)} %copy-done.2, f32[2,160,640]{2,1,0:T(8,128)} %param.22), kind=kLoop, calls=%fused_computation.10 | loop fusion | flops 1433600 | bytes 4505600 | tf_op jit(solution)/shard_map/convert_element_type | solution.py:159
  149.3 0.0 copy-done.8
  149.3 0.0 copy-done.6
  149.3 0.0 copy-start.4
  149.3 0.0 copy-done.5
  149.3 1.0 multiply_add_fusion
  150.3 0.9 copy-done.4
  151.2 1.1 copy.34
  152.2 0.0 copy-done.1
  152.2 0.7 copy-done.3
  153.0 1.1 copy.35
  154.0 0.1 copy-done.7
  154.1 0.7 copy.36
  154.8 0.9 copy.37
  (6 shorter events, 0.0 us)
Async XLA Ops:
  140.6 6.1 %copy-start = (f32[2,160,640]{2,1,0:T(8,128)S(1)}, f32[2,160,640]{2,1,0:T(8,128)}, u32[]{:S(2)}) copy-start(f32[2,160,640]{2,1,0:T(8,128)} %ffn_hbm.1) | copy-start | bytes 2457604
  140.7 6.1 %copy-start.2 = (f32[2,160,640]{2,1,0:T(8,128)S(1)}, f32[2,160,640]{2,1,0:T(8,128)}, u32[]{:S(2)}) copy-start(f32[2,160,640]{2,1,0:T(8,128)} %get-tuple-element.66) | copy-start | bytes 2457604
  142.0 7.3 %copy-start.8 = (f32[80]{0:T(128)}, f32[80]{0:T(128)S(1)}, u32[]{:S(2)}) copy-start(f32[80]{0:T(128)S(1)} %get-tuple-element.63) | copy-start | bytes 964
  145.1 4.2 %copy-start.6 = (f32[640,80]{0,1:T(8,128)}, f32[640,80]{0,1:T(8,128)S(1)}, u32[]{:S(2)}) copy-start(f32[640,80]{0,1:T(8,128)S(1)} %get-tuple-element.58) | copy-start | bytes 614404
  146.8 2.5 %copy-start.5 = (f32[2,160,640]{2,1,0:T(8,128)S(1)}, f32[2,160,640]{2,1,0:T(8,128)}, u32[]{:S(2)}) copy-start(f32[2,160,640]{2,1,0:T(8,128)} %param.23) | copy-start | bytes 2457604
  149.3 3.0 %copy-start.1 = (f32[2,160,640]{2,1,0:T(8,128)}, f32[2,160,640]{2,1,0:T(8,128)S(1)}, u32[]{:S(2)}) copy-start(f32[2,160,640]{2,1,0:T(8,128)S(1)} %get-tuple-element.68) | copy-start | bytes 2457604
  149.3 1.9 %copy-start.4 = (f32[2,256,640]{2,1,0:T(8,128)S(1)}, f32[2,256,640]{2,1,0:T(8,128)}, u32[]{:S(2)}) copy-start(f32[2,256,640]{2,1,0:T(8,128)} %get-tuple-element.54) | copy-start | bytes 3932164
  151.2 1.8 %copy-start.3 = (f32[2,256,640]{2,1,0:T(8,128)S(1)}, f32[2,256,640]{2,1,0:T(8,128)}, u32[]{:S(2)}) copy-start(f32[2,256,640]{2,1,0:T(8,128)} %get-tuple-element.55) | copy-start | bytes 3932164
  153.0 1.1 copy-start.7

commit v3 on v2

--- a/solution.py
+++ b/solution.py
@@ -297,7 +297,8 @@
 LENGTH = 256
 FEATURES = D // ROWS
 PART_ROWS = (48, 32)
-UNITS = ((0, 512), (512, 128), (640, 640))
+UNITS = ((0, 512), (512, 128), (640, 256), (896, 256), (1152, 128))
+FAR_UNITS = (2, 3, 4)
 CHUNKS = ((0, 512), (512, 768))
 
 
@@ -341,11 +342,10 @@
 
 def step_kernel(
     x_hbm, dy_hbm, ffn_hbm, ids, attn_w, norm_w,
-    yout, ig, fgrad, agrad, nout, probs_hbm,
+    yout_hbm, ig_hbm, fgrad_hbm, agrad_hbm, nout, probs_hbm,
     wall, wgrad, fw, n1, qkv, abuf, obuf, tn2, tdy, gb, dub, acc, near, stage, far, dyv,
-    fr1, fr2, fr3, rc, ar1, ar2, ar3, bias, dob, nbuf, ngrad, nsum, nr1, nr2,
-    ld_sem, pb_sem, ag_s, ag_r, fg_s, fg_r, sib_s, sib_r, tok_s, tok_r, part_s, part_r,
-    frs_s, frs_r, ars_s, ars_r, rc_s, rc_r, na_s, na_r, nb_s, nb_r,
+    fr1, fr2, fr3, rc, ar1, ar2, ar3, bias, dob, nbuf, ngrad, nsum, nr1, nr2, yout, ig, fgrad, agrad, held,
+    ld_sem, pb_sem, out_sem, send, fg_s, ag_r, fg_r, sib_r, tok_r, part_r, frs_r, ars_r, rc_r, norm_r,
 ):
     r = lax.axis_index("row")
     c = lax.axis_index("col")
@@ -374,6 +374,17 @@
     def rows16(start, size):
         return pl.ds(pl.multiple_of(start, 16), size)
 
+    (
+        S_GATHER, S_SIB, S_TOK, S_OWN, S_PART, S_FAR, S_F_ONE, S_F_TWO, S_F_FAR,
+        S_A_ONE, S_A_TWO, S_A_NEAR, S_A_FAR, S_CROSS, S_N_ONE, S_N_TWO, S_G_ONE, S_G_TWO,
+    ) = range(18)
+
+    def sent(i, all_bytes):
+        remote(all_bytes, all_bytes, send.at[i], send.at[i], dev_sib).wait_send()
+
+    def received(sem, all_bytes):
+        remote(all_bytes, all_bytes, sem, sem, dev_sib).wait_recv()
+
     def remote(src, dst, ss, rs, dev):
         return pltpu.make_async_remote_copy(
             src_ref=src, dst_ref=dst, send_sem=ss, recv_sem=rs, device_id=dev, device_id_type=MESH_ID
@@ -391,16 +402,16 @@
     ld_y.start()
     ld_x.start()
 
-    wall[r, rows16(c * WIDTH, WIDTH)] = attn_w[...].T.astype(BF)
+    wall[r, rows16(c * WIDTH, WIDTH)] = attn_w[...].astype(BF)
     nbuf[r, c] = jnp.zeros((1, LANES), F32)
     nbuf[r, c, :, 0:WIDTH] = norm_w[...].astype(BF).astype(F32)
     pl.semaphore_wait(barrier, COLS + 2)
 
     def norm_one(j):
-        return remote(nbuf.at[r, c], nbuf.at[r, c], na_s.at[j], na_r.at[j], dev_row(j))
+        return remote(nbuf.at[r, c], nbuf.at[r, c], send.at[S_N_ONE], norm_r.at[0], dev_row(j))
 
     def norm_two(i):
-        return remote(nbuf.at[r], nbuf.at[r], na_s.at[COLS + i], na_r.at[COLS + i], (dev_x, dev_y, dev_d)[i])
+        return remote(nbuf.at[r], nbuf.at[r], send.at[S_N_TWO], norm_r.at[1], (dev_x, dev_y, dev_d)[i])
 
     def a_rows(j, p):
         start = (zat(j) * 2 + k) * WIDTH
@@ -410,19 +421,19 @@
 
     def gather_ops(piece, part, far_piece, far_dev, ss, rs):
         def cz(j):
-            return remote(piece(r, 0), far_piece(j), ss.at[0, j], rs.at[0, j], far_dev(j))
+            return remote(piece(r, 0), far_piece(j), ss(0, j), rs.at[0, j], far_dev(j))
 
         def cx(j):
-            return remote(piece(r, j), piece(r, j), ss.at[1, j], rs.at[1, j], dev_x)
+            return remote(piece(r, j), piece(r, j), ss(1, j), rs.at[1, j], dev_x)
 
         def cy(j):
-            return remote(piece(r, j), piece(r, j), ss.at[2, j], rs.at[2, j], dev_y)
+            return remote(piece(r, j), piece(r, j), ss(2, j), rs.at[2, j], dev_y)
 
         def cd0(j):
-            return remote(part(rx, j, 0), part(rx, j, 0), ss.at[3, j], rs.at[3, j], dev_y)
+            return remote(part(rx, j, 0), part(rx, j, 0), ss(3, j), rs.at[3, j], dev_y)
 
         def cd1(j):
-            return remote(part(ry, j, 1), part(ry, j, 1), ss.at[4, j], rs.at[4, j], dev_x)
+            return remote(part(ry, j, 1), part(ry, j, 1), ss(4, j), rs.at[4, j], dev_x)
 
         return cz, cx, cy, cd0, cd1
 
@@ -430,25 +441,26 @@
         lambda rr, j: wall.at[rr, a_rows(j, None)],
         lambda rr, j, p: wall.at[rr, a_rows(j, p)],
         lambda j: wall.at[r, a_rows(0, None)],
-        dev_z, ag_s, ag_r,
+        dev_z, lambda i, j: send.at[S_GATHER], ag_r,
     )
     fz, fx, fy, fd0, fd1 = gather_ops(
         lambda rr, i: fw.at[:, rr, :, pl.ds(i * D, D)],
         lambda rr, i, p: fw.at[p, rr, :, pl.ds(i * D, D)],
         lambda i: fw.at[:, r, :, pl.ds(D, D)],
-        lambda i: dev_z(2), fg_s, fg_r,
+        lambda i: dev_z(2), lambda i, j: fg_s.at[i, j], fg_r,
     )
 
     def sib(j):
         ref = wall.at[:, a_rows(j, None)]
-        return remote(ref, ref, sib_s.at[j], sib_r.at[j], dev_sib)
-
-    for j in (1, 2, 3):
-        az(j).start()
+        return remote(ref, ref, send.at[S_SIB], sib_r.at[j], dev_sib)
+
+    for j in range(1, COLS):
+        norm_one(j).start()
+    az(1).start()
     ax(0).start()
     ay(0).start()
-    for j in range(1, COLS):
-        norm_one(j).start()
+    az(2).start()
+    az(3).start()
 
     for s in range(2):
         ld_f[s].wait()
@@ -465,7 +477,8 @@
 
     def tok_copy(q, n, m, dev, whose):
         ref = (tdy, tn2)[q].at[whose, pl.ds(m * LENGTH, LENGTH)]
-        return remote(ref, ref, tok_s.at[q, n, m], tok_r.at[q, n, m], dev)
+        shared = S_OWN if q == 1 and n < 2 else S_TOK
+        return remote(ref, ref, send.at[shared], tok_r.at[q, n, m], dev)
 
     def tok_sib(q, m):
         return tok_copy(q, 0, m, dev_sib, owner(0, 0))
@@ -479,15 +492,17 @@
     for m in range(MB):
         tok_sib(0, m).start()
 
-    for j in range(1, COLS):
-        norm_one(j).wait_recv()
-    for i in range(3):
-        norm_two(i).start()
     ax(0).wait_recv()
     ad0(0).start()
     ay(0).wait_recv()
     ad1(0).start()
-    for j in (1, 2, 3):
+    az(1).wait_recv()
+    ax(1).start()
+    ay(1).start()
+    received(norm_r.at[0], nr2)
+    for i in range(3):
+        norm_two(i).start()
+    for j in (2, 3):
         az(j).wait_recv()
         ax(j).start()
         ay(j).start()
@@ -501,8 +516,7 @@
         ad1(j).start()
     fx(0).start()
     fy(0).start()
-    for i in range(3):
-        norm_two(i).wait_recv()
+    received(norm_r.at[1], nr1)
 
     vectors = None
     for cc in range(COLS):
@@ -572,7 +586,7 @@
     def forward_group(it, _):
         m, g = it // GROUPS, it % GROUPS
         at_step(it, 5, lambda: gather_diag(0))
-        at_step(it, 9, lambda: gather_xy(1))
+        at_step(it, 7, lambda: gather_xy(1))
         slot = it % 2
 
         @pl.when(it >= 2)
@@ -610,26 +624,25 @@
         tok_far(0, m).wait_recv()
         tok_fwd(0, m).start()
 
-    def scatter_ops(block, r1, r2, ss, rs):
+    def scatter_ops(block, r1, r1_both, r2, s_one, s_two, rs):
         def one(u, p, b):
             dev = dev_y if p == 0 else dev_x
             rr = rd if b == 1 else (ry if p == 0 else rx)
-            return remote(block(rr, u, p), r1(u, p, b), ss.at[2 * p + b, u], rs.at[2 * p + b, u], dev)
+            return remote(block(rr, u, p), r1(u, p, b), send.at[s_one], rs.at[p, u], dev)
 
         def two(u, p):
             dev = dev_x if p == 0 else dev_y
             rr = rx if p == 0 else ry
-            return remote(block(rr, u, p), r2(u, p), ss.at[4 + p, u], rs.at[4 + p, u], dev)
-
-        def start_one(u):
-            for p in range(2):
+            return remote(block(rr, u, p), r2(u, p), send.at[s_two], rs.at[2 + p, u], dev)
+
+        def start_one(u, parts=(0, 1)):
+            for p in parts:
                 for b in (1, 0):
                     one(u, p, b).start()
 
         def start_two(u):
             for p in range(2):
-                one(u, p, 0).wait_recv()
-                one(u, p, 1).wait_recv()
+                received(rs.at[p, u], r1_both(u, p))
                 mine = block(rx if p == 0 else ry, u, p)
                 mine[...] = (mine[...].astype(F32) + r1(u, p, 1)[...].astype(F32)).astype(BF)
                 two(u, p).start()
@@ -642,31 +655,27 @@
                 + r2(u, p)[...].astype(F32)
             )
 
-        def drain(u):
-            for p in range(2):
-                one(u, p, 0).wait_send()
-                one(u, p, 1).wait_send()
-                two(u, p).wait_send()
-
-        return start_one, start_two, own_sum, drain
+        return start_one, start_two, own_sum
 
     def unit_lanes(u):
         return pl.ds(UNITS[u][0], UNITS[u][1])
 
-    f_one, f_two, f_sum, f_drain = scatter_ops(
+    f_one, f_two, f_sum = scatter_ops(
         lambda rr, u, p: fw.at[p, rr, :, unit_lanes(u)],
         lambda u, p, b: fr1.at[p, b, :, unit_lanes(u)],
+        lambda u, p: fr1.at[p, :, :, unit_lanes(u)],
         lambda u, p: fr2.at[p, :, unit_lanes(u)],
-        frs_s, frs_r,
-    )
-
-    def f_far(p):
-        return remote(fw.at[p, r, :, unit_lanes(2)], fr3.at[p], frs_s.at[6 + p, 2], frs_r.at[6 + p, 2], dev_z(2))
-
-    def f_three():
+        S_F_ONE, S_F_TWO, frs_r,
+    )
+
+    def f_far(u, p):
+        lanes = pl.ds(UNITS[u][0] - D, UNITS[u][1])
+        return remote(fw.at[p, r, :, unit_lanes(u)], fr3.at[p, :, lanes], send.at[S_F_FAR], frs_r.at[4 + p, u], dev_z(2))
+
+    def f_three(u):
         for p in range(2):
-            fw[p, r, :, unit_lanes(2)] = f_sum(2, p).astype(BF)
-            f_far(p).start()
+            fw[p, r, :, unit_lanes(u)] = f_sum(u, p).astype(BF)
+            f_far(u, p).start()
 
     def g_rows(zz, p, parity):
         start = (zz * 2 + parity) * WIDTH
@@ -677,32 +686,50 @@
     def part_rows(p):
         return pl.ds(PART_ROWS[0] * p, PART_ROWS[p])
 
-    a_one, a_two, a_sum, a_drain = scatter_ops(
+    a_one, a_two, a_sum = scatter_ops(
         lambda rr, zz, p: wgrad.at[rr, g_rows(zz, p, k)],
         lambda zz, p, b: ar1.at[zz, b, part_rows(p)],
+        lambda zz, p: ar1.at[zz, :, part_rows(p)],
         lambda zz, p: ar2.at[zz, part_rows(p)],
-        ars_s, ars_r,
-    )
-
-    def a_far(zz, j):
-        return remote(wgrad.at[r, g_rows(zz, None, k)], ar3.at[j - 1], ars_s.at[6, j], ars_r.at[6, j], (r, zz * 2 + k))
+        S_A_ONE, S_A_TWO, ars_r,
+    )
+
+    def a_near(zz):
+        return remote(wgrad.at[r, g_rows(zz, None, k)], ar3.at[zz // 2], send.at[S_A_NEAR], ars_r.at[4, zz // 2], dev_z(1))
+
+    def a_far(zz):
+        return remote(wgrad.at[r, g_rows(zz, None, k)], ar3.at[2], send.at[S_A_FAR], ars_r.at[4, 2], dev_z(2))
 
     def a_three(zz):
         total = [a_sum(zz, p) for p in range(2)]
 
-        @pl.when(z == zz)
+        @pl.when(z % 2 == zz % 2)
         def _():
             for p in range(2):
-                agrad[part_rows(p)] = total[p]
-
-        @pl.when(z != zz)
+                held[zz // 2, part_rows(p)] = total[p]
+
+        @pl.when(z % 2 != zz % 2)
         def _():
             for p in range(2):
                 wgrad[r, g_rows(zz, p, k)] = total[p].astype(BF)
-            a_far(zz, exclusive(z, zz)).start()
+            a_near(zz).start()
+
+    def a_four(half):
+        zz = half * 2 + z % 2
+        a_near(2 * half).wait_recv()
+        total = held[half] + ar3[half].astype(F32)
+
+        @pl.when(z == zz)
+        def _():
+            agrad[...] = total
+
+        @pl.when(z != zz)
+        def _():
+            wgrad[r, g_rows(zz, None, k)] = total.astype(BF)
+            a_far(zz).start()
 
     def cross(zz):
-        return remote(wgrad.at[:, g_rows(zz, None, 1 - k)], rc.at[zz], rc_s.at[zz], rc_r.at[zz], dev_sib)
+        return remote(wgrad.at[:, g_rows(zz, None, 1 - k)], rc.at[zz], send.at[S_CROSS], rc_r.at[zz], dev_sib)
 
     def a_start(zz):
         cross(zz).wait_recv()
@@ -711,71 +738,79 @@
             mine[...] = (mine[...].astype(F32) + rc[zz, rr].astype(F32)).astype(BF)
         a_one(zz)
 
-    def ffn_tile(i, t):
+    def ffn_tile(i, t, rows=slice(None)):
         first, width = CHUNKS[i]
         up = fw[0, :, :, first : first + width].reshape(D, width)
         down = fw[1, :, :, first : first + width].reshape(D, width)
-        act, slope = gelu_pair(dot_nn(tn2[t], up))
-        grad_act = dot_nn(tdy[t], down)
+        act, slope = gelu_pair(dot_nn(tn2[t, rows], up))
+        grad_act = dot_nn(tdy[t, rows], down)
         act = act.astype(BF)
         grad_up = (grad_act * slope).astype(BF)
-        gb[t, :, 0:width] = act
-        dub[t, :, 0:width] = grad_up
+        gb[t, rows, 0:width] = act
+        dub[t, rows, 0:width] = grad_up
         dn_part = dot_nt(grad_up, up)
         y_part = dot_nt(act, down)
         if i == 0:
-            acc[0, t] = dn_part
-            acc[1, t] = y_part
+            acc[0, t, rows] = dn_part
+            acc[1, t, rows] = y_part
         else:
-            acc[0, t] += dn_part
-            acc[1, t] += y_part
-
-    def weight_grads(i):
+            acc[0, t, rows] += dn_part
+            acc[1, t, rows] += y_part
+
+    def weight_grads(i, units):
         first, width = CHUNKS[i]
         for p, (left, right) in enumerate(((tn2, dub), (tdy, gb))):
             grad = dot_tn(left[...].reshape(4 * MB * LENGTH, D), right[:, :, 0:width].reshape(4 * MB * LENGTH, width))
             fw[p, :, :, first : first + width] = grad.astype(BF).reshape(ROWS, FEATURES, width)
+            for u in units:
+                f_one(u, (p,))
 
     fd0(0).wait_recv()
     fd1(0).wait_recv()
 
-    def first_block(s, _):
+    def near_tiles(s, _):
         def sib_tiles():
             for q in range(2):
                 for m in range(MB):
                     tok_sib(q, m).wait_recv()
 
-        def far_tiles():
-            for m in range(MB):
-                tok_far(1, m).wait_recv()
-                tok_fwd(1, m).start()
-
-        def fwd_tiles():
-            for q in range(2):
-                for m in range(MB):
-                    tok_fwd(q, m).wait_recv()
-
         at_step(s, 1, sib_tiles)
-        at_step(s, 2, far_tiles)
-        at_step(s, 3, fwd_tiles)
-        at_step(s, 3, lambda: gather_diag(1))
-        ffn_tile(0, owner(s // 2, s % 2))
+        ffn_tile(0, owner(0, s))
         return 0
 
-    lax.fori_loop(0, 4, first_block, 0)
+    lax.fori_loop(0, 2, near_tiles, 0)
+
+    def far_tiles(s, _):
+        m = s // 2
+        for m_ in range(MB):
+
+            def arrived(m_=m_):
+                tok_far(1, m_).wait_recv()
+                tok_fwd(1, m_).start()
+
+            def forwarded(m_=m_):
+                for q in range(2):
+                    tok_fwd(q, m_).wait_recv()
+
+            at_step(s, 2 * m_, arrived)
+            at_step(s, 2 * m_ + 1, forwarded)
+        at_step(s, 2, lambda: gather_diag(1))
+        ffn_tile(0, owner(1, s % 2), pl.ds(pl.multiple_of(m * LENGTH, LENGTH), LENGTH))
+        return 0
+
+    lax.fori_loop(0, 2 * MB, far_tiles, 0)
     fz(1).wait_send()
     for op in (fx, fy, fd0, fd1):
         op(0).wait_send()
-    weight_grads(0)
-    f_one(0)
+    weight_grads(0, (0,))
     fd0(1).wait_recv()
     fd1(1).wait_recv()
 
     def part_sib(q, n):
-        return remote(acc.at[q, owner(n, 1)], near.at[q, n], part_s.at[q, n], part_r.at[q, n], dev_sib)
+        return remote(acc.at[q, owner(n, 1)], near.at[q, n], send.at[S_PART], part_r.at[q, n], dev_sib)
 
     def part_far(q, m):
-        return remote(stage.at[q, m], far.at[q, m], part_s.at[q, 2 + m], part_r.at[q, 2 + m], dev_z(1))
+        return remote(stage.at[q, m], far.at[q, m], send.at[S_FAR], part_r.at[q, 2 + m], dev_z(1))
 
     def to_far(q):
         part_sib(q, 1).wait_recv()
@@ -801,14 +836,10 @@
     lax.fori_loop(0, 4, second_block, 0)
     for op in (fx, fy, fd0, fd1):
         op(1).wait_send()
-    weight_grads(1)
-    f_one(2)
-    f_one(1)
+    weight_grads(1, (2, 3))
 
     zero = jnp.zeros((1, D), F32)
-    for m in range(MB):
-        tok_far(1, m).wait_send()
-        tok_sib(1, m).wait_send()
+    sent(S_OWN, tn2.at[pl.ds(0, 2)])
     part_sib(0, 0).wait_recv()
 
     def whole(q, m):
@@ -831,6 +862,13 @@
     load_probs(0, 0).start()
     second_backward(0)
 
+    def first_backward(m):
+        grad = dot_nn(qkv[m, 0], wall[0]) + dot_nn(qkv[m, 1], wall[1]) + dot_nn(qkv[m, 2], wall[2])
+        normal, inv = ln_stats(ig[m])
+        ig[m] = dyv[m] + ln_backward(normal, inv, gain_one, grad)
+        nsum[pl.ds(0, 1)] += jnp.sum(grad * normal, axis=0, keepdims=True)
+        nsum[pl.ds(1, 1)] += jnp.sum(grad, axis=0, keepdims=True)
+
     def backward_at(it):
         m = jnp.where(it < 6, it // 3, it % 2)
         g = jnp.where(it < 6, it % 3, it // 2)
@@ -845,20 +883,27 @@
     def backward_group(it, _):
         m, g = backward_at(it)
 
+        at_step(it, 3, lambda: f_two(2))
+        at_step(it, 3, lambda: f_one(4))
+        at_step(it, 3, lambda: f_one(1))
+
         @pl.when(it == 3)
         def _():
             second_backward(1)
             rows = [tn2[owner(0, 0), pl.ds(i * LENGTH, LENGTH)] for i in range(MB)]
             wgrad[3] = (dot_tn(rows[0], obuf[0]) + dot_tn(rows[1], obuf[1])).astype(BF)
 
-        at_step(it, 5, lambda: f_two(2))
-        at_step(it, 6, lambda: f_two(1))
+        at_step(it, 5, lambda: f_three(2))
+        at_step(it, 5, lambda: f_two(3))
         at_step(it, 6, lambda: a_start(0))
+        at_step(it, 7, lambda: f_two(4))
         at_step(it, 7, lambda: a_start(1))
-        at_step(it, 8, lambda: a_two(0))
-        at_step(it, 9, lambda: a_two(1))
+        at_step(it, 8, lambda: f_three(3))
+        at_step(it, 8, lambda: f_two(1))
+        at_step(it, 9, lambda: first_backward(0))
+        at_step(it, 9, lambda: f_three(4))
+        at_step(it, 9, lambda: a_two(0))
         at_step(it, 9, lambda: a_start(2))
-        at_step(it, 9, f_three)
         slot = it % 2
 
         @pl.when(it + 1 < MB * GROUPS)
@@ -904,18 +949,12 @@
 
     lax.fori_loop(0, MB * GROUPS, backward_group, 0)
 
-    def first_backward(m):
-        grad = dot_nn(qkv[m, 0], wall[0]) + dot_nn(qkv[m, 1], wall[1]) + dot_nn(qkv[m, 2], wall[2])
-        normal, inv = ln_stats(ig[m])
-        ig[m] = dyv[m] + ln_backward(normal, inv, gain_one, grad)
-        nsum[pl.ds(0, 1)] += jnp.sum(grad * normal, axis=0, keepdims=True)
-        nsum[pl.ds(1, 1)] += jnp.sum(grad, axis=0, keepdims=True)
-
-    a_three(0)
-    a_start(3)
-    first_backward(0)
-    a_two(2)
+    def put(i, src, dst):
+        return pltpu.make_async_copy(src, dst, out_sem.at[i])
+
     first_backward(1)
+    for m in range(MB):
+        put(m, ig.at[m], ig_hbm.at[m]).start()
 
     sums = nsum[...]
     lane_own = lax.broadcasted_iota(jnp.int32, (8, LANES), 1) < WIDTH
@@ -927,68 +966,77 @@
 
     def grad_rows(i):
         rr = (rx, ry, rd)[i]
-        return remote(ngrad.at[rr], nr1.at[i], nb_s.at[i], nb_r.at[i], (dev_x, dev_y, dev_d)[i])
+        return remote(ngrad.at[rr], nr1.at[i], send.at[S_G_ONE], norm_r.at[2], (dev_x, dev_y, dev_d)[i])
 
     def grad_cols(j):
         col = zat(j // 2) * 2 + (k + j % 2) % 2
-        return remote(ngrad.at[r, col], nr2.at[j - 1], nb_s.at[2 + j], nb_r.at[2 + j], dev_row(j))
+        return remote(ngrad.at[r, col], nr2.at[j - 1], send.at[S_G_TWO], norm_r.at[3], dev_row(j))
 
     for i in range(3):
         grad_rows(i).start()
-    a_three(1)
-    a_two(3)
-    a_three(2)
-    for i in range(3):
-        grad_rows(i).wait_recv()
+    a_start(3)
+    a_two(1)
+    a_two(2)
+    a_three(0)
+    received(norm_r.at[2], nr1)
     ngrad[r] = ngrad[r] + nr1[0] + nr1[1] + nr1[2]
     for j in range(1, COLS):
         grad_cols(j).start()
+    a_two(3)
+    a_three(1)
+    a_three(2)
+    a_four(0)
 
     part_sib(1, 0).wait_recv()
     for m in range(MB):
         part_far(1, m).wait_recv()
         yout[m] = yout[m] + whole(1, m)
+        put(2 + m, yout.at[m], yout_hbm.at[m]).start()
 
     a_three(3)
-    for p in range(2):
-        for u in range(2):
-            total = f_sum(u, p)
-            if u == 0:
-                f_far(p).wait_recv()
-            fgrad[p, :, unit_lanes(u)] = total + fr3[p, :, unit_lanes(u)].astype(F32)
+    for u in range(2):
+        for p in range(2):
+            fgrad[p, :, unit_lanes(u)] = f_sum(u, p)
+    a_four(1)
+
+    sent(S_GATHER, wall.at[pl.ds(0, 3), pl.ds(0, 5 * WIDTH)])
+    sent(S_SIB, wall.at[pl.ds(0, 2)])
+    sent(S_TOK, tdy)
+    sent(S_PART, acc.at[0])
+    sent(S_FAR, stage)
+    sent(S_F_ONE, fw.at[0])
+    sent(S_F_TWO, fr2)
+    sent(S_A_ONE, wgrad.at[0])
+    sent(S_A_TWO, ar2)
+    sent(S_CROSS, rc)
+    sent(S_N_ONE, nr2)
+    sent(S_N_TWO, nr1)
+    sent(S_G_ONE, nr1)
+
+    for u in FAR_UNITS:
+        lanes = pl.ds(UNITS[u][0] - D, UNITS[u][1])
+        for p in range(2):
+            f_far(u, p).wait_recv()
+            fgrad[p, :, lanes] += fr3[p, :, lanes].astype(F32)
+    put(4, fgrad, fgrad_hbm).start()
+    received(norm_r.at[3], nr2)
     total = ngrad[r, c]
-    for j in range(1, COLS):
-        grad_cols(j).wait_recv()
-        total = total + nr2[j - 1]
+    for j in range(COLS - 1):
+        total = total + nr2[j]
     nout[...] = total
-    for j in (1, 2, 3):
-        a_far(z, j).wait_recv()
-    agrad[...] = agrad[...] + ar3[0].astype(F32) + ar3[1].astype(F32) + ar3[2].astype(F32)
-
-    for j in (1, 2, 3):
-        az(j).wait_send()
-        a_far(z, j).wait_send()
-    for j in range(Z_SIZE):
-        for op in (ax, ay, ad0, ad1, sib, cross):
-            op(j).wait_send()
-        a_drain(j)
-    for u in range(3):
-        f_drain(u)
-    for p in range(2):
-        f_far(p).wait_send()
+    a_far(z).wait_recv()
+    agrad[...] = agrad[...] + ar3[2].astype(F32)
+    put(5, agrad, agrad_hbm).start()
+
+    sent(S_G_TWO, nr2)
+    sent(S_F_FAR, fr3)
+    sent(S_A_NEAR, ar3.at[pl.ds(0, 2)])
+    sent(S_A_FAR, ar3.at[2])
     for m in range(MB):
-        tok_sib(0, m).wait_send()
-        tok_far(0, m).wait_send()
-        for q in range(2):
-            tok_fwd(q, m).wait_send()
-            part_far(q, m).wait_send()
-            part_sib(q, m).wait_send()
-    for j in range(1, COLS):
-        norm_one(j).wait_send()
-        grad_cols(j).wait_send()
-    for i in range(3):
-        norm_two(i).wait_send()
-        grad_rows(i).wait_send()
+        put(m, ig.at[m], ig_hbm.at[m]).wait()
+        put(2 + m, yout.at[m], yout_hbm.at[m]).wait()
+    put(4, fgrad, fgrad_hbm).wait()
+    put(5, agrad, agrad_hbm).wait()
 
 
 def run_step(x, dy, ids, attn_w, norm_w, ffn_w):
@@ -1008,7 +1056,7 @@
             jax.ShapeDtypeStruct((MB * GROUPS, HEADS_TILE, LENGTH, LENGTH), BF),
         ),
         in_specs=[any_spec, any_spec, any_spec, vspec, vspec, vspec],
-        out_specs=(vspec, vspec, vspec, vspec, vspec, any_spec),
+        out_specs=(any_spec, any_spec, any_spec, any_spec, vspec, any_spec),
         scratch_shapes=[
             vm((ROWS, D, D), BF),
             vm((ROWS, D, D), BF),
@@ -1040,23 +1088,113 @@
             vm((8, D), F32),
             vm((3, COLS, 1, LANES), F32),
             vm((COLS - 1, 1, LANES), F32),
-            dma((4,)), dma((4,)),
-            dma((5, Z_SIZE)), dma((5, Z_SIZE)),
-            dma((5, 2)), dma((5, 2)),
-            dma((Z_SIZE,)), dma((Z_SIZE,)),
-            dma((2, 3, MB)), dma((2, 3, MB)),
-            dma((2, 4)), dma((2, 4)),
-            dma((8, 3)), dma((8, 3)),
-            dma((7, Z_SIZE)), dma((7, Z_SIZE)),
-            dma((Z_SIZE,)), dma((Z_SIZE,)),
-            dma((COLS + 3,)), dma((COLS + 3,)),
-            dma((COLS + 2,)), dma((COLS + 2,)),
+            vm((MB, LENGTH, D), F32),
+            vm((MB, LENGTH, D), F32),
+            vm((2, FEATURES, D), F32),
+            vm((WIDTH, D), F32),
+            vm((2, WIDTH, D), F32),
+            dma((4,)), dma((4,)), dma((6,)),
+            dma((18,)),
+            dma((5, 2)),
+            dma((5, Z_SIZE)),
+            dma((5, 2)),
+            dma((Z_SIZE,)),
+            dma((2, 3, MB)),
+            dma((2, 4)),
+            dma((6, len(UNITS))),
+            dma((5, Z_SIZE)),
+            dma((Z_SIZE,)),
+            dma((4,)),
         ],
         compiler_params=pltpu.CompilerParams(
             collective_id=0, has_side_effects=True, vmem_limit_bytes=64 * 1024 * 1024 - 4096
         ),
         name="encoder_step",
     )(x, dy, ffn_w, ids, attn_w, norm_w)
+
+
+def update_kernel(rate, *refs):
+    y_in, g_in, a_in, n_in, f_in = refs[0], refs[1], refs[2:6], refs[6:10], refs[10:14]
+    y_out, g_out, a_out, n_out, f_out = refs[14], refs[15], refs[16:21], refs[21:26], refs[26:31]
+    yb, gbuf, a_held, f_held, a_low, f_low, in_sem, out_sem = refs[31:]
+
+    def load(i, src, dst):
+        return pltpu.make_async_copy(src, dst, in_sem.at[i])
+
+    def save(i, src, dst):
+        return pltpu.make_async_copy(src, dst, out_sem.at[i])
+
+    pieces = []
+    for s in range(2):
+        pieces.append(([v.at[s] for v in f_in], [v.at[s] for v in f_out], f_held.at[s], f_low.at[s]))
+    pieces.append((list(a_in), list(a_out), a_held, a_low))
+    loads = [
+        [load(4 * n + i, src[i], held.at[i]) for i in range(4)]
+        for n, (src, dst, held, low) in enumerate(pieces)
+    ]
+    through = [(load(12, y_in, yb), save(15, yb, y_out)), (load(13, g_in, gbuf), save(16, gbuf, g_out))]
+    for copies in loads:
+        for copy in copies:
+            copy.start()
+    for first, _second in through:
+        first.start()
+
+    def update(weights, moment, average, grad):
+        moment_new = MOMENT_DECAY * moment + grad
+        weights_new = weights - rate * (grad + MOMENT_DECAY * moment_new)
+        average_new = AVERAGE_DECAY * average + (1.0 - AVERAGE_DECAY) * weights_new
+        return moment_new, weights_new, average_new
+
+    grad = n_in[3][:, 0:WIDTH]
+    moment, weights, average = update(n_in[0][...], n_in[1][...], n_in[2][...], grad)
+    for ref, value in zip(n_out, (grad, moment, weights, average, weights.astype(BF))):
+        ref[...] = value
+
+    saves = []
+    for n, (src, dst, held, low) in enumerate(pieces):
+        for copy in loads[n]:
+            copy.wait()
+        moment, weights, average = update(held[0], held[1], held[2], held[3])
+        held[0] = weights
+        held[1] = moment
+        held[2] = average
+        low[...] = weights.astype(BF)
+        for i, value in enumerate((held.at[3], held.at[1], held.at[0], held.at[2], low)):
+            saves.append(save(5 * n + i, value, dst[i]))
+            saves[-1].start()
+    for i, (first, second) in enumerate(through):
+        first.wait()
+        second.start()
+    for copy in saves:
+        copy.wait()
+    for _first, second in through:
+        second.wait()
+
+
+def run_update(rate, carried, attn, norm, ffn):
+    vm = pltpu.VMEM
+    any_spec = pl.BlockSpec(memory_space=pltpu.HBM)
+    vspec = pl.BlockSpec(memory_space=pltpu.VMEM)
+    five = lambda like: [jax.ShapeDtypeStruct(like.shape, F32)] * 4 + [jax.ShapeDtypeStruct(like.shape, BF)]
+    out = pl.pallas_call(
+        functools.partial(update_kernel, rate),
+        out_shape=[jax.ShapeDtypeStruct(v.shape, F32) for v in carried] + five(attn[0]) + five(norm[0]) + five(ffn[0]),
+        in_specs=[any_spec] * 6 + [vspec] * 4 + [any_spec] * 4,
+        out_specs=[any_spec] * 7 + [vspec] * 5 + [any_spec] * 5,
+        scratch_shapes=[
+            vm(carried[0].shape, F32),
+            vm(carried[1].shape, F32),
+            vm((4, *attn[0].shape), F32),
+            vm((2, 4, *ffn[0].shape[1:]), F32),
+            vm(attn[0].shape, BF),
+            vm(ffn[0].shape, BF),
+            pltpu.SemaphoreType.DMA((14,)),
+            pltpu.SemaphoreType.DMA((17,)),
+        ],
+        compiler_params=pltpu.CompilerParams(vmem_limit_bytes=64 * 1024 * 1024 - 4096),
+        name="update",
+    )(*carried, *attn, *norm, *ffn)
+    return out[0], out[1], out[2:7], out[7:12], out[12:17]
 
 
 def local_slice(
@@ -1066,16 +1204,18 @@
     ffn_weights, ffn_momentum, ffn_average,
 ):
     outputs, grads, ffn_grad, shard, norm_shard, _probs = run_step(
-        block_input, output_grad, sequence_ids, attn_weights, norm_params[None], ffn_weights
-    )
-    attn_grad = shard.T
-    norm_grad = norm_shard[0, :WIDTH]
+        block_input, output_grad, sequence_ids, attn_weights.T, norm_params[None], ffn_weights
+    )
     total_tokens = MB * block_input.shape[1] * lax.axis_size("row") * lax.axis_size("col")
     step_rate = RATE_SCALE * total_tokens ** (-0.5)
-    attn = sgd_update(attn_weights, attn_momentum, attn_average, attn_grad, step_rate)
-    norm = sgd_update(norm_params, norm_momentum, norm_average, norm_grad, step_rate)
-    ffn = sgd_update(ffn_weights, ffn_momentum, ffn_average, ffn_grad, step_rate)
-    return (outputs, grads, attn_grad, *attn, norm_grad, *norm, ffn_grad, *ffn)
+    outputs, grads, attn, norm, ffn = run_update(
+        step_rate,
+        (outputs, grads),
+        (attn_weights.T, attn_momentum.T, attn_average.T, shard),
+        (norm_params[None], norm_momentum[None], norm_average[None], norm_shard),
+        (ffn_weights, ffn_momentum, ffn_average, ffn_grad),
+    )
+    return (outputs, grads, *[v.T for v in attn], *[v[0] for v in norm], *ffn)
 
 
 def local(*args):

time: 156 us -> 132 us (0.85)
  other arithmetic: 9.6 us -> 0 us
  Pallas kernels: 138 us -> 130 us
  local copies, waits for them, and re-layouts: 7.2 us -> 0 us
    pallas_call x1, Pallas kernels: 138 us -> 123 us  [run_step(): pl.pallas_call(step_kernel, out_shape=(jax.ShapeDtypeStruct((MB, LENGTH,...]
    unnamed x23 -> x0, local copies, waits for them, and re-layouts: 7.2 us -> none
    pallas_call x0 -> x1, Pallas kernels: none -> 6.68 us  [run_update(): pl.pallas_call(functools.partial(update_kernel, rate), out_shape=[jax.Sha...]
    convert_element_type x3 -> x0, other arithmetic: 5.7 us -> none  [sgd_update(): weights_new.astype(jnp.bfloat16)]
    add x3 -> x0, other arithmetic: 3.91 us -> none  [sgd_update(): average_new = AVERAGE_DECAY * average + (1.0 - AVERAGE_DECAY) * weights_new]
where the time goes in v3:
time: 132 us; the launch traced here: 131 us
  Pallas kernels  130 us (98%)
    pallas_call x1, Pallas kernels, run_step(): pl.pallas_call(step_kernel, out_shape=(jax.ShapeDtypeStruct((MB, LENGTH,...  123 us
    pallas_call x1, Pallas kernels, run_update(): pl.pallas_call(functools.partial(update_kernel, rate), out_shape=[jax.Sha...  6.68 us

profile of v3, /device:TPU:0, one launch (start us, length us, event | category | flops | bytes accessed | tf_op | source)
XLA Modules:
  0.0 130.7 jit_solution(4170701270933541100)
XLA Ops:
  0.7 123.2 %encoder_step.1 = (f32[2,256,640]{2,1,0:T(8,128)}, f32[2,256,640]{2,1,0:T(8,128)}, f32[2,160,640]{2,1,0:T(8,128)}, f32[80,640]{1,0:T(8,128)}, f32[1,128]{1,0:T(1,128)}, /*index=5*/bf16[10,4,256,256]{3,2,1,0:T(8,128)(2,1)}) custom-call(f32[2,256,640]{2,1,0:T(8,128)} %x_hbm.1, f32[2,256,640]{2,1,0:T(8,128)} %dy_hbm.1, f32[2,160,640]{2,1,0:T(8,128)} %refs_10_.1, ...), custom_call_target="tpu_custom_call" | custom-call | tf_op jit(solution)/shard_map/encoder_step/pallas_call | solution.py:1048
  123.8 6.7 %update.1 = (f32[2,256,640]{2,1,0:T(8,128)}, f32[2,256,640]{2,1,0:T(8,128)}, f32[80,640]{1,0:T(8,128)}, f32[80,640]{1,0:T(8,128)}, f32[80,640]{1,0:T(8,128)}, /*...) custom-call(f32[2,256,640]{2,1,0:T(8,128)} %get-tuple-element.39.ref, ...), custom_call_target="tpu_custom_call" | custom-call | tf_op jit(solution)/shard_map/update/pallas_call | solution.py:1179

commit v4 on v3

--- a/solution.py
+++ b/solution.py
@@ -341,10 +341,10 @@
 
 
 def step_kernel(
-    x_hbm, dy_hbm, ffn_hbm, ids, attn_w, norm_w,
+    x_hbm, dy_hbm, ffn_hbm, ids, attn_hbm, norm_w,
     yout_hbm, ig_hbm, fgrad_hbm, agrad_hbm, nout, probs_hbm,
-    wall, wgrad, fw, n1, qkv, abuf, obuf, tn2, tdy, gb, dub, acc, near, stage, far, dyv,
-    fr1, fr2, fr3, rc, ar1, ar2, ar3, bias, dob, nbuf, ngrad, nsum, nr1, nr2, yout, ig, fgrad, agrad, held,
+    wall, wgrad, fw, n1, qkv, obuf, tn2, tdy, gb, dub, acc, near, stage, far, dyv,
+    fr1, fr2, fr3, rc, ar1, ar2, ar3, nbuf, ngrad, nsum, nr1, nr2, yout, ig,
     ld_sem, pb_sem, out_sem, send, fg_s, ag_r, fg_r, sib_r, tok_r, part_r, frs_r, ars_r, rc_r, norm_r,
 ):
     r = lax.axis_index("row")
@@ -376,8 +376,8 @@
 
     (
         S_GATHER, S_SIB, S_TOK, S_OWN, S_PART, S_FAR, S_F_ONE, S_F_TWO, S_F_FAR,
-        S_A_ONE, S_A_TWO, S_A_NEAR, S_A_FAR, S_CROSS, S_N_ONE, S_N_TWO, S_G_ONE, S_G_TWO,
-    ) = range(18)
+        S_A_ONE, S_A_TWO, S_A_NEAR, S_A_FAR, S_CROSS, S_N_ONE, S_N_TWO, S_G_ONE, S_G_TWO, S_FAR_DN,
+    ) = range(19)
 
     def sent(i, all_bytes):
         remote(all_bytes, all_bytes, send.at[i], send.at[i], dev_sib).wait_send()
@@ -399,10 +399,13 @@
     ld_y = pltpu.make_async_copy(dy_hbm, dyv, ld_sem.at[1])
     for s in range(2):
         ld_f[s].start()
+    ld_w = pltpu.make_async_copy(attn_hbm, acc.at[1, 2, pl.ds(0, WIDTH)], ld_sem.at[4])
+    ld_w.start()
     ld_y.start()
     ld_x.start()
 
-    wall[r, rows16(c * WIDTH, WIDTH)] = attn_w[...].astype(BF)
+    ld_w.wait()
+    wall[r, rows16(c * WIDTH, WIDTH)] = acc[1, 2, 0:WIDTH].astype(BF)
     nbuf[r, c] = jnp.zeros((1, LANES), F32)
     nbuf[r, c, :, 0:WIDTH] = norm_w[...].astype(BF).astype(F32)
     pl.semaphore_wait(barrier, COLS + 2)
@@ -443,12 +446,50 @@
         lambda j: wall.at[r, a_rows(0, None)],
         dev_z, lambda i, j: send.at[S_GATHER], ag_r,
     )
-    fz, fx, fy, fd0, fd1 = gather_ops(
-        lambda rr, i: fw.at[:, rr, :, pl.ds(i * D, D)],
-        lambda rr, i, p: fw.at[p, rr, :, pl.ds(i * D, D)],
-        lambda i: fw.at[:, r, :, pl.ds(D, D)],
-        lambda i: dev_z(2), lambda i, j: fg_s.at[i, j], fg_r,
-    )
+    def f_copy(src, dst, kind, j, dev):
+        return remote(src, dst, fg_s.at[kind, j], fg_r.at[kind, j], dev)
+
+    def f_part(rr, i, p):
+        return fw.at[p, rr, :, pl.ds(i * D, D)]
+
+    def fz():
+        return f_copy(fw.at[:, r, :, pl.ds(0, D)], fw.at[:, r, :, pl.ds(D, D)], 0, 0, dev_z(2))
+
+    def fx(j, p):
+        return f_copy(f_part(r, j, p), f_part(r, j, p), 1 + p, j, dev_x)
+
+    def fy(j, p):
+        return f_copy(f_part(r, j, p), f_part(r, j, p), 3 + p, j, dev_y)
+
+    def fd(j, p):
+        whose, dev = ((rx, dev_y), (ry, dev_x))[p]
+        return f_copy(f_part(whose, j, p), f_part(whose, j, p), 5 + p, j, dev)
+
+    def gather_first(j):
+        fx(j, 0).start()
+        fy(j, 1).start()
+
+    def gather_second(j):
+        fx(j, 1).start()
+        fy(j, 0).start()
+
+    def gather_diag(j):
+        fx(j, 0).wait_recv()
+        fd(j, 0).start()
+        fy(j, 1).wait_recv()
+        fd(j, 1).start()
+
+    def gathered(j):
+        fx(j, 1).wait_recv()
+        fy(j, 0).wait_recv()
+        fd(j, 0).wait_recv()
+        fd(j, 1).wait_recv()
+
+    def gather_sent(j):
+        for p in range(2):
+            fx(j, p).wait_send()
+            fy(j, p).wait_send()
+            fd(j, p).wait_send()
 
     def sib(j):
         ref = wall.at[:, a_rows(j, None)]
@@ -469,7 +510,7 @@
 
     def make_bias(m, _):
         across = jnp.broadcast_to(ids[pl.ds(m, 1)].astype(F32), (LENGTH, LENGTH))
-        bias[m] = jnp.where(across == across.T, 0.0, MASKED)
+        acc[1, m, 0:LENGTH, 0:LENGTH] = jnp.where(across == across.T, 0.0, MASKED)
         tdy[owner(0, 0), pl.ds(m * LENGTH, LENGTH)] = dyv[m].astype(BF)
         return 0
 
@@ -499,6 +540,8 @@
     az(1).wait_recv()
     ax(1).start()
     ay(1).start()
+    for m in range(MB):
+        tok_far(0, m).start()
     received(norm_r.at[0], nr2)
     for i in range(3):
         norm_two(i).start()
@@ -506,16 +549,13 @@
         az(j).wait_recv()
         ax(j).start()
         ay(j).start()
-    fz(1).start()
-    for m in range(MB):
-        tok_far(0, m).start()
+    fz().start()
     for j in (1, 2, 3):
         ax(j).wait_recv()
         ad0(j).start()
         ay(j).wait_recv()
         ad1(j).start()
-    fx(0).start()
-    fy(0).start()
+    gather_first(0)
     received(norm_r.at[1], nr1)
 
     vectors = None
@@ -541,6 +581,8 @@
     for j in range(Z_SIZE):
         sib(j).wait_recv()
 
+    gather_second(0)
+
     def project(i, _):
         m, p = i // 3, i % 3
         qkv[m, p] = dot_nt(n1[m], wall[p]).astype(BF)
@@ -558,22 +600,17 @@
         def _():
             fn()
 
-    def gather_xy(j):
-        fz(j).wait_recv()
-        fx(j).start()
-        fy(j).start()
-
-    def gather_diag(j):
-        fx(j).wait_recv()
-        fd0(j).start()
-        fy(j).wait_recv()
-        fd1(j).start()
+    def slot_lanes(it, first, size):
+        return pl.ds(pl.multiple_of((it % 2) * LENGTH + first, LANES), size)
+
+    def slot_of(it):
+        return gb.at[:, pl.ds(LENGTH, LENGTH), slot_lanes(it, 0, LENGTH)]
 
     def save_probs(it):
-        return pltpu.make_async_copy(abuf.at[it % 2], probs_hbm.at[it], pb_sem.at[it % 2])
+        return pltpu.make_async_copy(slot_of(it), probs_hbm.at[it], pb_sem.at[it % 2])
 
     def load_probs(it, where):
-        return pltpu.make_async_copy(probs_hbm.at[where], abuf.at[it % 2], pb_sem.at[2 + it % 2])
+        return pltpu.make_async_copy(probs_hbm.at[where], slot_of(it), pb_sem.at[2 + it % 2])
 
     def second_norm(m):
         hidden = ig[m] + dot_nt(obuf[m], wall[3])
@@ -585,9 +622,14 @@
 
     def forward_group(it, _):
         m, g = it // GROUPS, it % GROUPS
-        at_step(it, 5, lambda: gather_diag(0))
-        at_step(it, 7, lambda: gather_xy(1))
-        slot = it % 2
+        at_step(it, 1, lambda: gather_diag(0))
+
+        @pl.when(it == 8)
+        def _():
+            fz().wait_recv()
+            gather_first(1)
+            gather_second(1)
+
 
         @pl.when(it >= 2)
         def _():
@@ -597,18 +639,17 @@
         q = qkv[m, 0, :, lanes]
         kk = qkv[m, 1, :, lanes]
         v = qkv[m, 2, :, lanes]
-        mask_bias = bias[m]
-        mixed = None
+        v_turned = v.T
         for h in range(HEADS_TILE):
-            scores = dot_nt(q * head_mask[h], kk) * log2_scale + mask_bias
-            row_max = jnp.max(scores, axis=-1, keepdims=True)
-            expo = jnp.exp2(scores - row_max)
-            total = jnp.sum(expo, axis=-1, keepdims=True)
-            probs = (expo * (1.0 / total)).astype(BF)
-            abuf[slot, h] = probs
-            part = dot_nn(probs, v * head_mask[h])
-            mixed = part if mixed is None else mixed + part
-        obuf[m, :, lanes] = mixed.astype(BF)
+            scores = dot_nt(kk, q * head_mask[h])
+            for part in range(LENGTH // LANES):
+                cols = slice(part * LANES, (part + 1) * LANES)
+                shifted = scores[:, cols] * log2_scale + acc[1, m, 0:LENGTH, cols]
+                expo = jnp.exp2(shifted - jnp.max(shifted, axis=0, keepdims=True))
+                total = jnp.sum(expo, axis=0, keepdims=True)
+                gb[h, LENGTH : 2 * LENGTH, slot_lanes(it, part * LANES, LANES)] = (expo * (1.0 / total)).astype(BF)
+        mixed = [dot_nn(v_turned[h * HD : (h + 1) * HD], gb[h, LENGTH : 2 * LENGTH, slot_lanes(it, 0, LENGTH)]) for h in range(HEADS_TILE)]
+        obuf[m, :, lanes] = jnp.concatenate(mixed, axis=0).T.astype(BF)
         save_probs(it).start()
 
         @pl.when(g == GROUPS - 1)
@@ -700,13 +741,18 @@
     def a_far(zz):
         return remote(wgrad.at[r, g_rows(zz, None, k)], ar3.at[2], send.at[S_A_FAR], ars_r.at[4, 2], dev_z(2))
 
+    def held(i):
+        return acc.at[0, owner(1, 0), pl.ds(FEATURES + i * WIDTH, WIDTH)]
+
+    agrad = held(2)
+
     def a_three(zz):
         total = [a_sum(zz, p) for p in range(2)]
 
         @pl.when(z % 2 == zz % 2)
         def _():
             for p in range(2):
-                held[zz // 2, part_rows(p)] = total[p]
+                held(zz // 2)[part_rows(p)] = total[p]
 
         @pl.when(z % 2 != zz % 2)
         def _():
@@ -717,7 +763,7 @@
     def a_four(half):
         zz = half * 2 + z % 2
         a_near(2 * half).wait_recv()
-        total = held[half] + ar3[half].astype(F32)
+        total = held(half)[...] + ar3[half].astype(F32)
 
         @pl.when(z == zz)
         def _():
@@ -746,8 +792,8 @@
         grad_act = dot_nn(tdy[t, rows], down)
         act = act.astype(BF)
         grad_up = (grad_act * slope).astype(BF)
-        gb[t, rows, 0:width] = act
-        dub[t, rows, 0:width] = grad_up
+        gb[t, rows, first : first + width] = act
+        dub[t, rows, first : first + width] = grad_up
         dn_part = dot_nt(grad_up, up)
         y_part = dot_nt(act, down)
         if i == 0:
@@ -757,16 +803,32 @@
             acc[0, t, rows] += dn_part
             acc[1, t, rows] += y_part
 
+    def token_sums(i, left, right, first_owner, owners):
+        first, width = CHUNKS[i]
+        rows = owners * MB * LENGTH
+        span = pl.ds(first_owner, owners)
+        return dot_tn(left[span].reshape(rows, D), right[span, :, first : first + width].reshape(rows, width))
+
+    pairs = ((tn2, dub), (tdy, gb))
+
+    def weight_grads_near(i):
+        for p, (left, right) in enumerate(pairs):
+            wgrad[p, :, 0 : CHUNKS[0][1]] = token_sums(i, left, right, (z % 2) * 2, 2).astype(BF)
+
     def weight_grads(i, units):
         first, width = CHUNKS[i]
-        for p, (left, right) in enumerate(((tn2, dub), (tdy, gb))):
-            grad = dot_tn(left[...].reshape(4 * MB * LENGTH, D), right[:, :, 0:width].reshape(4 * MB * LENGTH, width))
+        for p, (left, right) in enumerate(pairs):
+            if i == 0:
+                grad = wgrad[p, :, 0:width].astype(F32) + token_sums(i, left, right, (1 - z % 2) * 2, 2)
+            else:
+                grad = token_sums(i, left, right, 0, 4)
             fw[p, :, :, first : first + width] = grad.astype(BF).reshape(ROWS, FEATURES, width)
             for u in units:
                 f_one(u, (p,))
-
-    fd0(0).wait_recv()
-    fd1(0).wait_recv()
+            if i == 1 and p == 0:
+                f_two(0)
+
+    gathered(0)
 
     def near_tiles(s, _):
         def sib_tiles():
@@ -792,31 +854,33 @@
                 for q in range(2):
                     tok_fwd(q, m_).wait_recv()
 
+            if m_ == 1:
+                at_step(s, 2, lambda: gather_diag(1))
+                at_step(s, 2, lambda: weight_grads_near(0))
             at_step(s, 2 * m_, arrived)
             at_step(s, 2 * m_ + 1, forwarded)
-        at_step(s, 2, lambda: gather_diag(1))
         ffn_tile(0, owner(1, s % 2), pl.ds(pl.multiple_of(m * LENGTH, LENGTH), LENGTH))
         return 0
 
     lax.fori_loop(0, 2 * MB, far_tiles, 0)
-    fz(1).wait_send()
-    for op in (fx, fy, fd0, fd1):
-        op(0).wait_send()
-    weight_grads(0, (0,))
-    fd0(1).wait_recv()
-    fd1(1).wait_recv()
+    fz().wait_send()
+    gather_sent(0)
+    gathered(1)
 
     def part_sib(q, n):
         return remote(acc.at[q, owner(n, 1)], near.at[q, n], send.at[S_PART], part_r.at[q, n], dev_sib)
 
+    def stage_of(q, m):
+        return stage.at[m] if q else wgrad.at[2, pl.ds(m * LENGTH, LENGTH)]
+
     def part_far(q, m):
-        return remote(stage.at[q, m], far.at[q, m], send.at[S_FAR], part_r.at[q, 2 + m], dev_z(1))
+        return remote(stage_of(q, m), far.at[q, m], send.at[(S_FAR_DN, S_FAR)[q]], part_r.at[q, 2 + m], dev_z(1))
 
     def to_far(q):
         part_sib(q, 1).wait_recv()
         for m in range(MB):
             rows = pl.ds(m * LENGTH, LENGTH)
-            stage[q, m] = (acc[q, owner(1, 0), rows] + near[q, 1, rows]).astype(BF)
+            stage_of(q, m)[...] = (acc[q, owner(1, 0), rows] + near[q, 1, rows]).astype(BF)
             part_far(q, m).start()
 
     def second_block(s, _):
@@ -829,14 +893,13 @@
 
             at_step(s, 2 * (1 - n), to_sib)
         at_step(s, 1, lambda: to_far(0))
-        at_step(s, 2, lambda: f_two(0))
+        at_step(s, 1, lambda: weight_grads(0, (0,)))
         at_step(s, 3, lambda: to_far(1))
         return 0
 
     lax.fori_loop(0, 4, second_block, 0)
-    for op in (fx, fy, fd0, fd1):
-        op(1).wait_send()
-    weight_grads(1, (2, 3))
+    gather_sent(1)
+    weight_grads(1, (2,))
 
     zero = jnp.zeros((1, D), F32)
     sent(S_OWN, tn2.at[pl.ds(0, 2)])
@@ -853,7 +916,7 @@
         grad_hidden = dyv[m] + ln_backward(normal, inv, gain_two, grad)
         dyv[m] = grad_hidden
         low = grad_hidden.astype(BF)
-        dob[m] = dot_nn(low, wall[3]).astype(BF)
+        dub[m, 0:LENGTH, 0:D] = dot_nn(low, wall[3]).astype(BF)
         tn2[owner(0, 0), pl.ds(m * LENGTH, LENGTH)] = low
         nsum[pl.ds(2, 1)] += jnp.sum(grad * normal, axis=0, keepdims=True)
         nsum[pl.ds(3, 1)] += jnp.sum(grad, axis=0, keepdims=True)
@@ -883,28 +946,27 @@
     def backward_group(it, _):
         m, g = backward_at(it)
 
+        at_step(it, 1, lambda: f_one(3))
         at_step(it, 3, lambda: f_two(2))
-        at_step(it, 3, lambda: f_one(4))
-        at_step(it, 3, lambda: f_one(1))
 
         @pl.when(it == 3)
         def _():
             second_backward(1)
+            sent(S_FAR_DN, wgrad.at[2, pl.ds(0, MB * LENGTH)])
             rows = [tn2[owner(0, 0), pl.ds(i * LENGTH, LENGTH)] for i in range(MB)]
             wgrad[3] = (dot_tn(rows[0], obuf[0]) + dot_tn(rows[1], obuf[1])).astype(BF)
 
-        at_step(it, 5, lambda: f_three(2))
+        at_step(it, 4, lambda: f_one(4))
+        at_step(it, 4, lambda: f_three(2))
         at_step(it, 5, lambda: f_two(3))
         at_step(it, 6, lambda: a_start(0))
         at_step(it, 7, lambda: f_two(4))
+        at_step(it, 7, lambda: f_three(3))
         at_step(it, 7, lambda: a_start(1))
-        at_step(it, 8, lambda: f_three(3))
-        at_step(it, 8, lambda: f_two(1))
-        at_step(it, 9, lambda: first_backward(0))
-        at_step(it, 9, lambda: f_three(4))
+        at_step(it, 8, lambda: f_one(1))
         at_step(it, 9, lambda: a_two(0))
         at_step(it, 9, lambda: a_start(2))
-        slot = it % 2
+        at_step(it, 9, lambda: f_three(4))
 
         @pl.when(it + 1 < MB * GROUPS)
         def _():
@@ -916,26 +978,26 @@
         q = qkv[m, 0, :, lanes]
         kk = qkv[m, 1, :, lanes]
         v = qkv[m, 2, :, lanes]
-        do = dob[m, :, lanes]
-        q_turned = q.T
-        do_turned = do.T
-        grad_q = None
-        grad_k = []
-        grad_v = []
+        do = dub[m, 0:LENGTH, lanes]
+        k_turned = kk.T
         for h in range(HEADS_TILE):
-            probs = abuf[slot, h]
-            wide = probs.astype(F32)
-            grad_probs = dot_nt(do * head_mask[h], v)
-            product = grad_probs * wide
-            row = jnp.sum(product, axis=-1, keepdims=True)
-            grad_scores = (product - wide * row).astype(BF)
-            part = dot_nn(grad_scores, kk * head_mask[h])
-            grad_q = part if grad_q is None else grad_q + part
-            grad_v.append(dot_nn(do_turned[h * HD : (h + 1) * HD], probs))
-            grad_k.append(dot_nn(q_turned[h * HD : (h + 1) * HD], grad_scores))
-        qkv[m, 0, :, lanes] = (grad_q * scale).astype(BF)
-        qkv[m, 1, :, lanes] = (jnp.concatenate(grad_k, axis=0).T * scale).astype(BF)
-        qkv[m, 2, :, lanes] = jnp.concatenate(grad_v, axis=0).T.astype(BF)
+            do_head = do * head_mask[h]
+            for part in range(LENGTH // LANES):
+                cols = slice(part * LANES, (part + 1) * LANES)
+                wide = gb[h, LENGTH : 2 * LENGTH, slot_lanes(it, part * LANES, LANES)].astype(F32)
+                product = dot_nt(v, do_head[cols]) * wide
+                total = jnp.sum(product, axis=0, keepdims=True)
+                gb[h, 0:LENGTH, cols] = (product - wide * total).astype(BF)
+        grad_q, grad_k, grad_v = [], None, None
+        for h in range(HEADS_TILE):
+            v_part = dot_nn(gb[h, LENGTH : 2 * LENGTH, slot_lanes(it, 0, LENGTH)], do * head_mask[h])
+            k_part = dot_nn(gb[h, 0:LENGTH, 0:LENGTH], q * head_mask[h])
+            grad_v = v_part if grad_v is None else grad_v + v_part
+            grad_k = k_part if grad_k is None else grad_k + k_part
+            grad_q.append(dot_nn(k_turned[h * HD : (h + 1) * HD], gb[h, 0:LENGTH, 0:LENGTH]))
+        qkv[m, 0, :, lanes] = (jnp.concatenate(grad_q, axis=0).T * scale).astype(BF)
+        qkv[m, 1, :, lanes] = (grad_k * scale).astype(BF)
+        qkv[m, 2, :, lanes] = grad_v.astype(BF)
 
         @pl.when(m == 1)
         def _():
@@ -952,6 +1014,13 @@
     def put(i, src, dst):
         return pltpu.make_async_copy(src, dst, out_sem.at[i])
 
+    def put_ffn(p):
+        return put(4 + p, acc.at[p, owner(1, 0), pl.ds(0, FEATURES)], fgrad_hbm.at[p])
+
+    first_backward(0)
+    a_start(3)
+    a_two(1)
+    a_two(2)
     first_backward(1)
     for m in range(MB):
         put(m, ig.at[m], ig_hbm.at[m]).start()
@@ -974,18 +1043,16 @@
 
     for i in range(3):
         grad_rows(i).start()
-    a_start(3)
-    a_two(1)
-    a_two(2)
     a_three(0)
+    a_two(3)
+    a_three(1)
     received(norm_r.at[2], nr1)
     ngrad[r] = ngrad[r] + nr1[0] + nr1[1] + nr1[2]
     for j in range(1, COLS):
         grad_cols(j).start()
-    a_two(3)
-    a_three(1)
     a_three(2)
     a_four(0)
+    f_two(1)
 
     part_sib(1, 0).wait_recv()
     for m in range(MB):
@@ -996,7 +1063,7 @@
     a_three(3)
     for u in range(2):
         for p in range(2):
-            fgrad[p, :, unit_lanes(u)] = f_sum(u, p)
+            acc[p, owner(1, 0), 0:FEATURES, unit_lanes(u)] = f_sum(u, p)
     a_four(1)
 
     sent(S_GATHER, wall.at[pl.ds(0, 3), pl.ds(0, 5 * WIDTH)])
@@ -1017,8 +1084,9 @@
         lanes = pl.ds(UNITS[u][0] - D, UNITS[u][1])
         for p in range(2):
             f_far(u, p).wait_recv()
-            fgrad[p, :, lanes] += fr3[p, :, lanes].astype(F32)
-    put(4, fgrad, fgrad_hbm).start()
+            acc[p, owner(1, 0), 0:FEATURES, lanes] += fr3[p, :, lanes].astype(F32)
+    for p in range(2):
+        put_ffn(p).start()
     received(norm_r.at[3], nr2)
     total = ngrad[r, c]
     for j in range(COLS - 1):
@@ -1026,7 +1094,7 @@
     nout[...] = total
     a_far(z).wait_recv()
     agrad[...] = agrad[...] + ar3[2].astype(F32)
-    put(5, agrad, agrad_hbm).start()
+    put(6, agrad, agrad_hbm).start()
 
     sent(S_G_TWO, nr2)
     sent(S_F_FAR, fr3)
@@ -1035,8 +1103,9 @@
     for m in range(MB):
         put(m, ig.at[m], ig_hbm.at[m]).wait()
         put(2 + m, yout.at[m], yout_hbm.at[m]).wait()
-    put(4, fgrad, fgrad_hbm).wait()
-    put(5, agrad, agrad_hbm).wait()
+    for p in range(2):
+        put_ffn(p).wait()
+    put(6, agrad, agrad_hbm).wait()
 
 
 def run_step(x, dy, ids, attn_w, norm_w, ffn_w):
@@ -1055,7 +1124,7 @@
             jax.ShapeDtypeStruct((1, LANES), F32),
             jax.ShapeDtypeStruct((MB * GROUPS, HEADS_TILE, LENGTH, LENGTH), BF),
         ),
-        in_specs=[any_spec, any_spec, any_spec, vspec, vspec, vspec],
+        in_specs=[any_spec, any_spec, any_spec, vspec, any_spec, vspec],
         out_specs=(any_spec, any_spec, any_spec, any_spec, vspec, any_spec),
         scratch_shapes=[
             vm((ROWS, D, D), BF),
@@ -1063,15 +1132,14 @@
             vm((2, ROWS, FEATURES, 2 * D), BF),
             vm((MB, LENGTH, D), BF),
             vm((MB, 3, LENGTH, D), BF),
-            vm((2, HEADS_TILE, LENGTH, LENGTH), BF),
             vm((MB, LENGTH, D), BF),
             vm((4, tokens, D), BF),
             vm((4, tokens, D), BF),
-            vm((4, tokens, CHUNKS[1][1]), BF),
-            vm((4, tokens, CHUNKS[1][1]), BF),
+            vm((4, tokens, 2 * D), BF),
+            vm((4, tokens, 2 * D), BF),
             vm((2, 4, tokens, D), F32),
             vm((2, 2, tokens, D), F32),
-            vm((2, MB, LENGTH, D), BF),
+            vm((MB, LENGTH, D), BF),
             vm((2, MB, LENGTH, D), BF),
             vm((MB, LENGTH, D), F32),
             vm((2, 2, FEATURES, 2 * D), BF),
@@ -1081,8 +1149,6 @@
             vm((Z_SIZE, 2, WIDTH, D), BF),
             vm((Z_SIZE, WIDTH, D), BF),
             vm((Z_SIZE - 1, WIDTH, D), BF),
-            vm((MB, LENGTH, LENGTH), F32),
-            vm((MB, LENGTH, D), BF),
             vm((ROWS, COLS, 1, LANES), F32),
             vm((ROWS, COLS, 1, LANES), F32),
             vm((8, D), F32),
@@ -1090,14 +1156,11 @@
             vm((COLS - 1, 1, LANES), F32),
             vm((MB, LENGTH, D), F32),
             vm((MB, LENGTH, D), F32),
-            vm((2, FEATURES, D), F32),
-            vm((WIDTH, D), F32),
-            vm((2, WIDTH, D), F32),
-            dma((4,)), dma((4,)), dma((6,)),
-            dma((18,)),
-            dma((5, 2)),
+            dma((5,)), dma((4,)), dma((7,)),
+            dma((19,)),
+            dma((7, 2)),
             dma((5, Z_SIZE)),
-            dma((5, 2)),
+            dma((7, 2)),
             dma((Z_SIZE,)),
             dma((2, 3, MB)),
             dma((2, 4)),

time: 132 us -> 128 us (0.970)
  Pallas kernels: 130 us -> 126 us
    pallas_call x1, Pallas kernels: 123 us -> 119 us  [run_step(): pl.pallas_call(step_kernel, out_shape=(jax.ShapeDtypeStruct((MB, LENGTH,...]
where the time goes in v4:
time: 128 us; the launch traced here: 127 us
  Pallas kernels  126 us (98%)
    pallas_call x1, Pallas kernels, run_step(): pl.pallas_call(step_kernel, out_shape=(jax.ShapeDtypeStruct((MB, LENGTH,...  119 us
    pallas_call x1, Pallas kernels, run_update(): pl.pallas_call(functools.partial(update_kernel, rate), out_shape=[jax.Sha...  6.68 us

profile of v4, /device:TPU:0, one launch (start us, length us, event | category | flops | bytes accessed | tf_op | source)
XLA Modules:
  0.0 126.6 jit_solution(1082623931821663188)
XLA Ops:
  0.7 119.1 %encoder_step.1 = (f32[2,256,640]{2,1,0:T(8,128)}, f32[2,256,640]{2,1,0:T(8,128)}, f32[2,160,640]{2,1,0:T(8,128)}, f32[80,640]{1,0:T(8,128)}, f32[1,128]{1,0:T(1,128)}, /*index=5*/bf16[10,4,256,256]{3,2,1,0:T(8,128)(2,1)}) custom-call(f32[2,256,640]{2,1,0:T(8,128)} %x_hbm.1, f32[2,256,640]{2,1,0:T(8,128)} %dy_hbm.1, f32[2,160,640]{2,1,0:T(8,128)} %refs_10_.1, ...), custom_call_target="tpu_custom_call" | custom-call | tf_op jit(solution)/shard_map/encoder_step/pallas_call | solution.py:1117
  119.7 6.7 %update.1 = (f32[2,256,640]{2,1,0:T(8,128)}, f32[2,256,640]{2,1,0:T(8,128)}, f32[80,640]{1,0:T(8,128)}, f32[80,640]{1,0:T(8,128)}, f32[80,640]{1,0:T(8,128)}, /*...) custom-call(f32[2,256,640]{2,1,0:T(8,128)} %get-tuple-element.39.ref, ...), custom_call_target="tpu_custom_call" | custom-call | tf_op jit(solution)/shard_map/update/pallas_call | solution.py:1242

commit v5 on v4

--- a/solution.py
+++ b/solution.py
@@ -584,11 +584,12 @@
     gather_second(0)
 
     def project(i, _):
-        m, p = i // 3, i % 3
-        qkv[m, p] = dot_nt(n1[m], wall[p]).astype(BF)
+        rows = dot_nt(n1[...].reshape(MB * LENGTH, D), wall[i]).astype(BF)
+        for m in range(MB):
+            qkv[m, i] = rows[m * LENGTH : (m + 1) * LENGTH]
         return 0
 
-    lax.fori_loop(0, 3 * MB, project, 0)
+    lax.fori_loop(0, 3, project, 0)
 
     lane_head = lax.broadcasted_iota(jnp.int32, (1, LANES), 1) // HD
     head_mask = [jnp.where(lane_head == h, 1.0, 0.0).astype(BF) for h in range(HEADS_TILE)]
@@ -803,30 +804,27 @@
             acc[0, t, rows] += dn_part
             acc[1, t, rows] += y_part
 
-    def token_sums(i, left, right, first_owner, owners):
-        first, width = CHUNKS[i]
+    def token_sums(lanes, left, right, first_owner, owners):
+        first, width = lanes
         rows = owners * MB * LENGTH
         span = pl.ds(first_owner, owners)
         return dot_tn(left[span].reshape(rows, D), right[span, :, first : first + width].reshape(rows, width))
 
     pairs = ((tn2, dub), (tdy, gb))
 
-    def weight_grads_near(i):
+    def near_grads(unit):
         for p, (left, right) in enumerate(pairs):
-            wgrad[p, :, 0 : CHUNKS[0][1]] = token_sums(i, left, right, (z % 2) * 2, 2).astype(BF)
-
-    def weight_grads(i, units):
-        first, width = CHUNKS[i]
+            grad = token_sums(UNITS[unit], left, right, (z % 2) * 2, 2)
+            wgrad[p, :, 0 : UNITS[unit][1]] = grad.astype(BF)
+
+    def unit_grads(unit, held_near=False):
+        first, width = UNITS[unit]
         for p, (left, right) in enumerate(pairs):
-            if i == 0:
-                grad = wgrad[p, :, 0:width].astype(F32) + token_sums(i, left, right, (1 - z % 2) * 2, 2)
+            if held_near:
+                grad = wgrad[p, :, 0:width].astype(F32) + token_sums(UNITS[unit], left, right, (1 - z % 2) * 2, 2)
             else:
-                grad = token_sums(i, left, right, 0, 4)
+                grad = token_sums(UNITS[unit], left, right, 0, 4)
             fw[p, :, :, first : first + width] = grad.astype(BF).reshape(ROWS, FEATURES, width)
-            for u in units:
-                f_one(u, (p,))
-            if i == 1 and p == 0:
-                f_two(0)
 
     gathered(0)
 
@@ -856,7 +854,7 @@
 
             if m_ == 1:
                 at_step(s, 2, lambda: gather_diag(1))
-                at_step(s, 2, lambda: weight_grads_near(0))
+                at_step(s, 2, lambda: near_grads(0))
             at_step(s, 2 * m_, arrived)
             at_step(s, 2 * m_ + 1, forwarded)
         ffn_tile(0, owner(1, s % 2), pl.ds(pl.multiple_of(m * LENGTH, LENGTH), LENGTH))
@@ -893,13 +891,23 @@
 
             at_step(s, 2 * (1 - n), to_sib)
         at_step(s, 1, lambda: to_far(0))
-        at_step(s, 1, lambda: weight_grads(0, (0,)))
+
+        @pl.when(s == 1)
+        def _():
+            unit_grads(0, held_near=True)
+            f_one(0)
+
         at_step(s, 3, lambda: to_far(1))
         return 0
 
     lax.fori_loop(0, 4, second_block, 0)
     gather_sent(1)
-    weight_grads(1, (2,))
+    unit_grads(2)
+    f_one(2)
+    unit_grads(3)
+    f_one(3)
+    unit_grads(4)
+    unit_grads(1)
 
     zero = jnp.zeros((1, D), F32)
     sent(S_OWN, tn2.at[pl.ds(0, 2)])
@@ -946,8 +954,8 @@
     def backward_group(it, _):
         m, g = backward_at(it)
 
-        at_step(it, 1, lambda: f_one(3))
-        at_step(it, 3, lambda: f_two(2))
+        at_step(it, 1, lambda: f_two(2))
+        at_step(it, 2, lambda: f_one(4))
 
         @pl.when(it == 3)
         def _():
@@ -956,17 +964,15 @@
             rows = [tn2[owner(0, 0), pl.ds(i * LENGTH, LENGTH)] for i in range(MB)]
             wgrad[3] = (dot_tn(rows[0], obuf[0]) + dot_tn(rows[1], obuf[1])).astype(BF)
 
-        at_step(it, 4, lambda: f_one(4))
-        at_step(it, 4, lambda: f_three(2))
-        at_step(it, 5, lambda: f_two(3))
+        at_step(it, 3, lambda: f_three(2))
+        at_step(it, 3, lambda: f_two(3))
+        at_step(it, 5, lambda: f_two(4))
+        at_step(it, 5, lambda: f_three(3))
         at_step(it, 6, lambda: a_start(0))
-        at_step(it, 7, lambda: f_two(4))
-        at_step(it, 7, lambda: f_three(3))
+        at_step(it, 7, lambda: f_three(4))
         at_step(it, 7, lambda: a_start(1))
-        at_step(it, 8, lambda: f_one(1))
+        at_step(it, 9, lambda: a_start(2))
         at_step(it, 9, lambda: a_two(0))
-        at_step(it, 9, lambda: a_start(2))
-        at_step(it, 9, lambda: f_three(4))
 
         @pl.when(it + 1 < MB * GROUPS)
         def _():
@@ -1044,27 +1050,27 @@
     for i in range(3):
         grad_rows(i).start()
     a_three(0)
-    a_two(3)
-    a_three(1)
-    received(norm_r.at[2], nr1)
-    ngrad[r] = ngrad[r] + nr1[0] + nr1[1] + nr1[2]
-    for j in range(1, COLS):
-        grad_cols(j).start()
-    a_three(2)
-    a_four(0)
-    f_two(1)
-
     part_sib(1, 0).wait_recv()
     for m in range(MB):
         part_far(1, m).wait_recv()
         yout[m] = yout[m] + whole(1, m)
         put(2 + m, yout.at[m], yout_hbm.at[m]).start()
-
+    a_two(3)
+    f_one(1)
+    f_two(0)
+    a_three(1)
+    a_three(2)
     a_three(3)
+    received(norm_r.at[2], nr1)
+    ngrad[r] = ngrad[r] + nr1[0] + nr1[1] + nr1[2]
+    for j in range(1, COLS):
+        grad_cols(j).start()
+    a_four(0)
+    f_two(1)
+    a_four(1)
     for u in range(2):
         for p in range(2):
             acc[p, owner(1, 0), 0:FEATURES, unit_lanes(u)] = f_sum(u, p)
-    a_four(1)
 
     sent(S_GATHER, wall.at[pl.ds(0, 3), pl.ds(0, 5 * WIDTH)])
     sent(S_SIB, wall.at[pl.ds(0, 2)])

time: 128 us -> 122 us (0.953)
  Pallas kernels: 126 us -> 121 us
    pallas_call x1, Pallas kernels: 119 us -> 114 us  [run_step(): pl.pallas_call(step_kernel, out_shape=(jax.ShapeDtypeStruct((MB, LENGTH,...]
where the time goes in v5:
time: 122 us
  Pallas kernels  121 us (99%)
    pallas_call x1, Pallas kernels, run_step(): pl.pallas_call(step_kernel, out_shape=(jax.ShapeDtypeStruct((MB, LENGTH,...  114 us
    pallas_call x1, Pallas kernels, run_update(): pl.pallas_call(functools.partial(update_kernel, rate), out_shape=[jax.Sha...  6.68 us

profile of v5, /device:TPU:0, one launch (start us, length us, event | category | flops | bytes accessed | tf_op | source)
XLA Modules:
  0.0 121.5 jit_solution(6171398964978121165)
XLA Ops:
  0.7 114.0 %encoder_step.1 = (f32[2,256,640]{2,1,0:T(8,128)}, f32[2,256,640]{2,1,0:T(8,128)}, f32[2,160,640]{2,1,0:T(8,128)}, f32[80,640]{1,0:T(8,128)}, f32[1,128]{1,0:T(1,128)}, /*index=5*/bf16[10,4,256,256]{3,2,1,0:T(8,128)(2,1)}) custom-call(f32[2,256,640]{2,1,0:T(8,128)} %x_hbm.1, f32[2,256,640]{2,1,0:T(8,128)} %dy_hbm.1, f32[2,160,640]{2,1,0:T(8,128)} %refs_10_.1, ...), custom_call_target="tpu_custom_call" | custom-call | tf_op jit(solution)/shard_map/encoder_step/pallas_call | solution.py:1123
  114.7 6.7 %update.1 = (f32[2,256,640]{2,1,0:T(8,128)}, f32[2,256,640]{2,1,0:T(8,128)}, f32[80,640]{1,0:T(8,128)}, f32[80,640]{1,0:T(8,128)}, f32[80,640]{1,0:T(8,128)}, /*...) custom-call(f32[2,256,640]{2,1,0:T(8,128)} %get-tuple-element.39.ref, ...), custom_call_target="tpu_custom_call" | custom-call | tf_op jit(solution)/shard_map/update/pallas_call | solution.py:1248

commit v6 on v5

--- a/solution.py
+++ b/solution.py
@@ -341,10 +341,10 @@
 
 
 def step_kernel(
-    x_hbm, dy_hbm, ffn_hbm, ids, attn_hbm, norm_w,
-    yout_hbm, ig_hbm, fgrad_hbm, agrad_hbm, nout, probs_hbm,
+    x_hbm, dy_hbm, ffn_hbm, ids_hbm, attn_hbm, norm_hbm,
+    yout_hbm, ig_hbm, fgrad_hbm, agrad_hbm, nout_hbm, probs_hbm,
     wall, wgrad, fw, n1, qkv, obuf, tn2, tdy, gb, dub, acc, near, stage, far, dyv,
-    fr1, fr2, fr3, rc, ar1, ar2, ar3, nbuf, ngrad, nsum, nr1, nr2, yout, ig,
+    fr1, fr2, fr3, rc, ar1, ar2, ar3, nbuf, ngrad, nsum, nr1, nr2, yout, ig, ids, norm_w, nout,
     ld_sem, pb_sem, out_sem, send, fg_s, ag_r, fg_r, sib_r, tok_r, part_r, frs_r, ars_r, rc_r, norm_r,
 ):
     r = lax.axis_index("row")
@@ -400,13 +400,18 @@
     for s in range(2):
         ld_f[s].start()
     ld_w = pltpu.make_async_copy(attn_hbm, acc.at[1, 2, pl.ds(0, WIDTH)], ld_sem.at[4])
+    ld_n = pltpu.make_async_copy(norm_hbm, norm_w, ld_sem.at[5])
+    ld_i = pltpu.make_async_copy(ids_hbm, ids, ld_sem.at[6])
     ld_w.start()
+    ld_n.start()
+    ld_i.start()
     ld_y.start()
     ld_x.start()
 
     ld_w.wait()
     wall[r, rows16(c * WIDTH, WIDTH)] = acc[1, 2, 0:WIDTH].astype(BF)
     nbuf[r, c] = jnp.zeros((1, LANES), F32)
+    ld_n.wait()
     nbuf[r, c, :, 0:WIDTH] = norm_w[...].astype(BF).astype(F32)
     pl.semaphore_wait(barrier, COLS + 2)
 
@@ -506,6 +511,7 @@
     for s in range(2):
         ld_f[s].wait()
         fw[s, r, :, 0:D] = acc[0, s, 0:FEATURES].astype(BF)
+    ld_i.wait()
     ld_y.wait()
 
     def make_bias(m, _):
@@ -907,10 +913,8 @@
     unit_grads(3)
     f_one(3)
     unit_grads(4)
-    unit_grads(1)
 
     zero = jnp.zeros((1, D), F32)
-    sent(S_OWN, tn2.at[pl.ds(0, 2)])
     part_sib(0, 0).wait_recv()
 
     def whole(q, m):
@@ -924,8 +928,8 @@
         grad_hidden = dyv[m] + ln_backward(normal, inv, gain_two, grad)
         dyv[m] = grad_hidden
         low = grad_hidden.astype(BF)
-        dub[m, 0:LENGTH, 0:D] = dot_nn(low, wall[3]).astype(BF)
-        tn2[owner(0, 0), pl.ds(m * LENGTH, LENGTH)] = low
+        dub[m, 0:LENGTH, D : 2 * D] = dot_nn(low, wall[3]).astype(BF)
+        dub[2 + m, 0:LENGTH, D : 2 * D] = low
         nsum[pl.ds(2, 1)] += jnp.sum(grad * normal, axis=0, keepdims=True)
         nsum[pl.ds(3, 1)] += jnp.sum(grad, axis=0, keepdims=True)
 
@@ -954,18 +958,18 @@
     def backward_group(it, _):
         m, g = backward_at(it)
 
-        at_step(it, 1, lambda: f_two(2))
+        at_step(it, 2, lambda: f_two(2))
         at_step(it, 2, lambda: f_one(4))
 
         @pl.when(it == 3)
         def _():
             second_backward(1)
             sent(S_FAR_DN, wgrad.at[2, pl.ds(0, MB * LENGTH)])
-            rows = [tn2[owner(0, 0), pl.ds(i * LENGTH, LENGTH)] for i in range(MB)]
+            rows = [dub[2 + i, 0:LENGTH, D : 2 * D] for i in range(MB)]
             wgrad[3] = (dot_tn(rows[0], obuf[0]) + dot_tn(rows[1], obuf[1])).astype(BF)
 
-        at_step(it, 3, lambda: f_three(2))
         at_step(it, 3, lambda: f_two(3))
+        at_step(it, 4, lambda: f_three(2))
         at_step(it, 5, lambda: f_two(4))
         at_step(it, 5, lambda: f_three(3))
         at_step(it, 6, lambda: a_start(0))
@@ -984,7 +988,7 @@
         q = qkv[m, 0, :, lanes]
         kk = qkv[m, 1, :, lanes]
         v = qkv[m, 2, :, lanes]
-        do = dub[m, 0:LENGTH, lanes]
+        do = dub[m, 0:LENGTH, pl.ds(pl.multiple_of(D + g * LANES, LANES), LANES)]
         k_turned = kk.T
         for h in range(HEADS_TILE):
             do_head = do * head_mask[h]
@@ -1025,6 +1029,7 @@
 
     first_backward(0)
     a_start(3)
+    unit_grads(1)
     a_two(1)
     a_two(2)
     first_backward(1)
@@ -1075,6 +1080,7 @@
     sent(S_GATHER, wall.at[pl.ds(0, 3), pl.ds(0, 5 * WIDTH)])
     sent(S_SIB, wall.at[pl.ds(0, 2)])
     sent(S_TOK, tdy)
+    sent(S_OWN, tn2.at[pl.ds(0, 2)])
     sent(S_PART, acc.at[0])
     sent(S_FAR, stage)
     sent(S_F_ONE, fw.at[0])
@@ -1098,6 +1104,7 @@
     for j in range(COLS - 1):
         total = total + nr2[j]
     nout[...] = total
+    put(7, nout, nout_hbm).start()
     a_far(z).wait_recv()
     agrad[...] = agrad[...] + ar3[2].astype(F32)
     put(6, agrad, agrad_hbm).start()
@@ -1112,6 +1119,7 @@
     for p in range(2):
         put_ffn(p).wait()
     put(6, agrad, agrad_hbm).wait()
+    put(7, nout, nout_hbm).wait()
 
 
 def run_step(x, dy, ids, attn_w, norm_w, ffn_w):
@@ -1130,8 +1138,8 @@
             jax.ShapeDtypeStruct((1, LANES), F32),
             jax.ShapeDtypeStruct((MB * GROUPS, HEADS_TILE, LENGTH, LENGTH), BF),
         ),
-        in_specs=[any_spec, any_spec, any_spec, vspec, any_spec, vspec],
-        out_specs=(any_spec, any_spec, any_spec, any_spec, vspec, any_spec),
+        in_specs=[any_spec] * 6,
+        out_specs=(any_spec,) * 6,
         scratch_shapes=[
             vm((ROWS, D, D), BF),
             vm((ROWS, D, D), BF),
@@ -1162,7 +1170,10 @@
             vm((COLS - 1, 1, LANES), F32),
             vm((MB, LENGTH, D), F32),
             vm((MB, LENGTH, D), F32),
-            dma((5,)), dma((4,)), dma((7,)),
+            vm((MB, LENGTH), jnp.int32),
+            vm((1, WIDTH), F32),
+            vm((1, LANES), F32),
+            dma((7,)), dma((4,)), dma((8,)),
             dma((19,)),
             dma((7, 2)),
             dma((5, Z_SIZE)),

time: 122 us -> 120 us (0.984)
  Pallas kernels: 121 us -> 119 us
    pallas_call x1, Pallas kernels: 114 us -> 112 us  [run_step(): pl.pallas_call(step_kernel, out_shape=(jax.ShapeDtypeStruct((MB, LENGTH,...]
where the time goes in v6:
time: 120 us; the launch traced here: 119 us
  Pallas kernels  119 us (99%)
    pallas_call x1, Pallas kernels, run_step(): pl.pallas_call(step_kernel, out_shape=(jax.ShapeDtypeStruct((MB, LENGTH,...  112 us
    pallas_call x1, Pallas kernels, run_update(): pl.pallas_call(functools.partial(update_kernel, rate), out_shape=[jax.Sha...  6.68 us

profile of v6, /device:TPU:0, one launch (start us, length us, event | category | flops | bytes accessed | tf_op | source)
XLA Modules:
  0.0 119.4 jit_solution(11082157340693463600)
XLA Ops:
  0.7 111.8 %encoder_step.1 = (f32[2,256,640]{2,1,0:T(8,128)}, f32[2,256,640]{2,1,0:T(8,128)}, f32[2,160,640]{2,1,0:T(8,128)}, f32[80,640]{1,0:T(8,128)}, f32[1,128]{1,0:T(1,128)}, /*index=5*/bf16[10,4,256,256]{3,2,1,0:T(8,128)(2,1)}) custom-call(f32[2,256,640]{2,1,0:T(8,128)} %x_hbm.1, f32[2,256,640]{2,1,0:T(8,128)} %dy_hbm.1, f32[2,160,640]{2,1,0:T(8,128)} %refs_10_.1, ...), custom_call_target="tpu_custom_call" | custom-call | tf_op jit(solution)/shard_map/encoder_step/pallas_call | solution.py:1131
  112.5 6.7 %update.1 = (f32[2,256,640]{2,1,0:T(8,128)}, f32[2,256,640]{2,1,0:T(8,128)}, f32[80,640]{1,0:T(8,128)}, f32[80,640]{1,0:T(8,128)}, f32[80,640]{1,0:T(8,128)}, /*...) custom-call(f32[2,256,640]{2,1,0:T(8,128)} %get-tuple-element.39.ref, ...), custom_call_target="tpu_custom_call" | custom-call | tf_op jit(solution)/shard_map/update/pallas_call | solution.py:1259

commit v7 on v6

--- a/solution.py
+++ b/solution.py
@@ -452,7 +452,7 @@
         dev_z, lambda i, j: send.at[S_GATHER], ag_r,
     )
     def f_copy(src, dst, kind, j, dev):
-        return remote(src, dst, fg_s.at[kind, j], fg_r.at[kind, j], dev)
+        return remote(src, dst, fg_s.at[j if kind else 2], fg_r.at[kind, j], dev)
 
     def f_part(rr, i, p):
         return fw.at[p, rr, :, pl.ds(i * D, D)]
@@ -491,10 +491,8 @@
         fd(j, 1).wait_recv()
 
     def gather_sent(j):
-        for p in range(2):
-            fx(j, p).wait_send()
-            fy(j, p).wait_send()
-            fd(j, p).wait_send()
+        six = fw.at[:, pl.ds(0, 3), :, pl.ds(0, D)]
+        remote(six, six, fg_s.at[j], fg_s.at[j], dev_sib).wait_send()
 
     def sib(j):
         ref = wall.at[:, a_rows(j, None)]
@@ -1175,7 +1173,7 @@
             vm((1, LANES), F32),
             dma((7,)), dma((4,)), dma((8,)),
             dma((19,)),
-            dma((7, 2)),
+            dma((3,)),
             dma((5, Z_SIZE)),
             dma((7, 2)),
             dma((Z_SIZE,)),

time: 120 us -> 120 us (level)
  no operation moved by 1% of the time
where the time goes in v7:
time: 120 us; the launch traced here: 119 us
  Pallas kernels  118 us (98%)
    pallas_call x1, Pallas kernels, run_step(): pl.pallas_call(step_kernel, out_shape=(jax.ShapeDtypeStruct((MB, LENGTH,...  112 us
    pallas_call x1, Pallas kernels, run_update(): pl.pallas_call(functools.partial(update_kernel, rate), out_shape=[jax.Sha...  6.68 us

profile of v7, /device:TPU:0, one launch (start us, length us, event | category | flops | bytes accessed | tf_op | source)
XLA Modules:
  0.0 119.3 jit_solution(15505065445359633728)
XLA Ops:
  0.7 111.7 %encoder_step.1 = (f32[2,256,640]{2,1,0:T(8,128)}, f32[2,256,640]{2,1,0:T(8,128)}, f32[2,160,640]{2,1,0:T(8,128)}, f32[80,640]{1,0:T(8,128)}, f32[1,128]{1,0:T(1,128)}, /*index=5*/bf16[10,4,256,256]{3,2,1,0:T(8,128)(2,1)}) custom-call(f32[2,256,640]{2,1,0:T(8,128)} %x_hbm.1, f32[2,256,640]{2,1,0:T(8,128)} %dy_hbm.1, f32[2,160,640]{2,1,0:T(8,128)} %refs_10_.1, ...), custom_call_target="tpu_custom_call" | custom-call | tf_op jit(solution)/shard_map/encoder_step/pallas_call | solution.py:1129
  112.4 6.7 %update.1 = (f32[2,256,640]{2,1,0:T(8,128)}, f32[2,256,640]{2,1,0:T(8,128)}, f32[80,640]{1,0:T(8,128)}, f32[80,640]{1,0:T(8,128)}, f32[80,640]{1,0:T(8,128)}, /*...) custom-call(f32[2,256,640]{2,1,0:T(8,128)} %get-tuple-element.39.ref, ...), custom_call_target="tpu_custom_call" | custom-call | tf_op jit(solution)/shard_map/update/pallas_call | solution.py:1257
